TPU v7x, 32 devices: a whole 2x2x4 slice. The times are simulated.
32 devices in a mesh: dp: 8 (over z, x), tensor: 4 (over y, core).
Axes of the slice: x: 2, y: 2, z: 4, core: 2. Of those that a mesh axis runs over, the one named last changes fastest.
Arguments:
- inputs: bfloat16 [16384, 1280], P(('dp', 'tensor')), may hold values from -6 to 6
- cotangent: bfloat16 [16384, 1280], P(('dp', 'tensor')), may hold values from -6 to 6
- adapter_choice_per_tree: int32 [8], P('dp'), may hold values from 0 to 7
- segment_lengths: int32 [8, 13], P('dp'), may hold values from 1 to 768, 2048 in all within a row
- segment_parents: int32 [8, 13], P('dp'), may hold values from 0 to 4, as said below
- norm_gain_rows: float32 [2, 1280], replicated, may hold values from 0.25 to 1.75
- query_dimension_scale: float32 [80], replicated, may hold values from 0.5 to 2
- attention_weights: bfloat16 [3, 1280, 1280], P(None, 'dp', 'tensor'), may hold values from -0.15625 to 0.15625
- output_weight: bfloat16 [1280, 1280], P('dp', 'tensor'), may hold values from -4 to 4
- feedforward_weights: bfloat16 [2, 1280, 1280], P(None, 'dp', 'tensor'), may hold values from -0.15625 to 0.15625
- adapter_first_input: bfloat16 [4, 8, 1280, 16], replicated, may hold values from -0.15625 to 0.15625
- adapter_second_attention: bfloat16 [3, 8, 16, 1280], replicated, may hold values from -1.5 to 1.5
- adapter_second_up: bfloat16 [8, 16, 1280], replicated, may hold values from -1.5 to 1.5
- adapter_first_output: bfloat16 [8, 1280, 16], replicated, may hold values from -4 to 4
- adapter_first_down: bfloat16 [8, 1280, 16], replicated, may hold values from -0.15625 to 0.15625
- adapter_second_residual: bfloat16 [2, 8, 16, 1280], replicated, may hold values from -1.5 to 1.5
Outputs:
- output: bfloat16 [16384, 1280], P(('dp', 'tensor'))
- input_grad: float32 [16384, 1280], P(('dp', 'tensor'))
- grad_lora_a_in: float32 [4, 8, 1280, 16], replicated
- grad_lora_b_qkv: float32 [3, 8, 16, 1280], replicated
- grad_lora_b_up: float32 [8, 16, 1280], replicated
- grad_lora_a_out: float32 [8, 1280, 16], replicated
- grad_lora_a_down: float32 [8, 1280, 16], replicated
- grad_lora_b_res: float32 [2, 8, 16, 1280], replicated
Inputs may be any that keep to these rules, and one draw needn't show every extreme that they name: `segment_lengths`: each row lists a tree's 13 segment lengths in token order (trunk, four branches, eight leaves) and sums to 2048; the longest segment of each tree has exactly 768 tokens. `segment_parents`: segment 0 is the trunk and is its own parent; segments 1 to 4 are branches with parent 0; segments 5 to 12 are leaves, exactly two under each branch, in drawn order.
All inputs are finite; a program needn't handle non-finite values.
Results may differ from a plain program's by a relative error of at most 0.015.
Values may be sent and summed in bfloat16 or wider, within the bound.
A program may use at most 192 MiB of HBM per device.

v0:
```python
import math

import jax
import jax.numpy as jnp
from jax import lax
from jax.sharding import PartitionSpec as P

HEAD_DIM = 80


adapter_scale = 0.5
epsilon = 1e-06
highest_precision = lax.Precision.HIGHEST
masked_value = -1e30


def precise_product(first_term, second_term):
    return jnp.dot(
        first_term, second_term, precision=highest_precision, preferred_element_type=jnp.float32
    )


def rms_norm(token_rows, gain_row):
    return (
        token_rows
        * lax.rsqrt(jnp.mean(token_rows * token_rows, axis=-1, keepdims=True) + epsilon)
        * gain_row
    )


def silu_act(values_in):
    return values_in / (1.0 + jnp.exp(-values_in))


def ancestry(parents):
    seg_count = parents.shape[0]
    indices = jnp.arange(seg_count, dtype=jnp.int32)
    parent_hot = (parents[:, None] == indices[None, :]).astype(jnp.float32)
    grand_hot = precise_product(parent_hot, parent_hot)
    return jnp.maximum(jnp.maximum(parent_hot, grand_hot), jnp.eye(seg_count, dtype=jnp.float32))


def token_hot(lengths, tree_len):
    seg_ends = jnp.cumsum(lengths)
    positions = jnp.arange(tree_len, dtype=jnp.int32)
    seg_ids = jnp.sum((positions[:, None] >= seg_ends[None, :]).astype(jnp.int32), axis=1)
    indices = jnp.arange(lengths.shape[0], dtype=jnp.int32)
    return (seg_ids, (seg_ids[:, None] == indices[None, :]).astype(jnp.float32))


def allowed_block(seg_ids, seg_hot, reach_table, block_start, block_rows):
    query_hot = lax.dynamic_slice_in_dim(seg_hot, block_start, block_rows, 0)
    query_ids = lax.dynamic_slice_in_dim(seg_ids, block_start, block_rows, 0)
    linked = precise_product(precise_product(query_hot, reach_table), seg_hot.T) > 0.5
    query_pos = block_start + jnp.arange(block_rows, dtype=jnp.int32)
    key_pos = jnp.arange(seg_ids.shape[0], dtype=jnp.int32)
    causal = (query_ids[:, None] != seg_ids[None, :]) | (key_pos[None, :] <= query_pos[:, None])
    return linked & causal


def attend_forward(queries, key_heads, values, query_offset, seg_ids, seg_hot, reach_table):
    query_len = queries.shape[0]
    block_rows = min(512, query_len)

    def one_block(local_start):
        block_q = lax.dynamic_slice_in_dim(queries, local_start, block_rows, 0)
        scores = jnp.einsum("qhd,khd->hqk", block_q, key_heads, preferred_element_type=jnp.float32)
        allowed = allowed_block(
            seg_ids, seg_hot, reach_table, query_offset + local_start, block_rows
        )
        scores = jnp.where(allowed[None], scores, masked_value)
        row_max = jnp.max(scores, axis=-1, keepdims=True)
        weights = jnp.exp(scores - row_max)
        row_total = jnp.sum(weights, axis=-1, keepdims=True)
        row_probs = (weights / row_total).astype(jnp.bfloat16)
        mixed_output = jnp.einsum(
            "hqk,khd->qhd", row_probs, values, preferred_element_type=jnp.float32
        )
        return (mixed_output, (row_max + jnp.log(row_total))[..., 0])

    local_starts = jnp.arange(query_len // block_rows, dtype=jnp.int32) * block_rows
    mixed_output, log_totals = lax.map(one_block, local_starts)
    return (mixed_output.reshape(query_len, -1), log_totals)


def attend_backward(
    queries, key_heads, values, grad_mixed, log_totals, query_offset, seg_ids, seg_hot, reach_table
):
    query_len = queries.shape[0]
    block_rows = min(512, query_len)

    def one_block(carried, block_items):
        grad_keys, grad_values = carried
        local_start, block_lse = block_items
        block_q = lax.dynamic_slice_in_dim(queries, local_start, block_rows, 0)
        block_grad = lax.dynamic_slice_in_dim(grad_mixed, local_start, block_rows, 0)
        scores = jnp.einsum("qhd,khd->hqk", block_q, key_heads, preferred_element_type=jnp.float32)
        allowed = allowed_block(
            seg_ids, seg_hot, reach_table, query_offset + local_start, block_rows
        )
        scores = jnp.where(allowed[None], scores, masked_value)
        row_probs = jnp.exp(scores - block_lse[..., None])
        grad_probs = jnp.einsum(
            "qhd,khd->hqk", block_grad, values, preferred_element_type=jnp.float32
        )
        row_delta = jnp.sum(row_probs * grad_probs, axis=-1, keepdims=True)
        grad_scores = (row_probs * (grad_probs - row_delta)).astype(jnp.bfloat16)
        grad_block_q = jnp.einsum(
            "hqk,khd->qhd", grad_scores, key_heads, preferred_element_type=jnp.float32
        )
        grad_keys = grad_keys + jnp.einsum(
            "hqk,qhd->khd", grad_scores, block_q, preferred_element_type=jnp.float32
        )
        grad_values = grad_values + jnp.einsum(
            "hqk,qhd->khd",
            row_probs.astype(jnp.bfloat16),
            block_grad,
            preferred_element_type=jnp.float32,
        )
        return ((grad_keys, grad_values), grad_block_q)

    zero_heads = jnp.zeros(key_heads.shape, jnp.float32)
    local_starts = jnp.arange(query_len // block_rows, dtype=jnp.int32) * block_rows
    (grad_keys, grad_values), grad_blocks = lax.scan(
        one_block, (zero_heads, zero_heads), (local_starts, log_totals)
    )
    tree_len = key_heads.shape[0]
    return (
        grad_blocks.reshape(query_len, -1),
        grad_keys.reshape(tree_len, -1),
        grad_values.reshape(tree_len, -1),
    )


def local(
    inputs,
    cotangent,
    adapter_choice_per_tree,
    segment_lengths,
    segment_parents,
    norm_gain_rows,
    query_dimension_scale,
    attention_weights,
    output_weight,
    feedforward_weights,
    adapter_first_input,
    adapter_second_attention,
    adapter_second_up,
    adapter_first_output,
    adapter_first_down,
    adapter_second_residual,
):
    tensor_position = lax.axis_index("tensor")
    tensor_count = lax.axis_size("tensor")
    head_columns = output_weight.shape[1]
    hidden_columns = feedforward_weights.shape[2]
    local_heads = head_columns // HEAD_DIM
    selected_index = adapter_choice_per_tree[0]
    tok_rows = inputs.shape[0]
    tree_len = tok_rows * tensor_count

    def selected_adapter(table_input, gather_along_axis):
        return lax.dynamic_index_in_dim(
            table_input, selected_index, gather_along_axis, keepdims=False
        )

    adapter_input_delta = selected_adapter(adapter_first_input, 1)
    adapter_residual_delta = selected_adapter(adapter_second_residual, 1)
    fwd_qkv, fwd_out, fwd_ffn = (
        lax.all_gather(attention_weights, "dp", axis=1, tiled=True),
        lax.all_gather(output_weight, "dp", axis=0, tiled=True),
        lax.all_gather(feedforward_weights, "dp", axis=1, tiled=True),
    )
    seg_ids, seg_hot = token_hot(segment_lengths[0], tree_len)
    reach_table = ancestry(segment_parents[0])
    token_rows = inputs.astype(jnp.float32)
    picked_adapter = (
        jnp.arange(adapter_first_input.shape[1], dtype=jnp.int32) == selected_index
    ).astype(jnp.float32)

    def select_slot(term, gather_along_axis):
        hot_shape = [1] * (term.ndim + 1)
        hot_shape[gather_along_axis] = picked_adapter.shape[0]
        return jnp.expand_dims(term, gather_along_axis) * picked_adapter.reshape(tuple(hot_shape))

    adapter_attention_delta = lax.dynamic_slice_in_dim(
        selected_adapter(adapter_second_attention, 1),
        tensor_position * head_columns,
        head_columns,
        2,
    )
    adapter_up_delta = lax.dynamic_slice_in_dim(
        selected_adapter(adapter_second_up, 0), tensor_position * hidden_columns, hidden_columns, 1
    )
    adapter_output_delta = lax.dynamic_slice_in_dim(
        selected_adapter(adapter_first_output, 0), tensor_position * head_columns, head_columns, 0
    )
    adapter_down_delta = lax.dynamic_slice_in_dim(
        selected_adapter(adapter_first_down, 0), tensor_position * hidden_columns, hidden_columns, 0
    )
    scale_row = jnp.tile(query_dimension_scale, local_heads) / math.sqrt(HEAD_DIM)
    shape_heads = (tree_len, local_heads, HEAD_DIM)
    normed_input = lax.all_gather(
        rms_norm(token_rows, norm_gain_rows[0]).astype(jnp.bfloat16), "tensor", axis=0, tiled=True
    )
    lowrank_attention = jnp.einsum(
        "ny,qyf->qnf", normed_input, adapter_input_delta[:3], preferred_element_type=jnp.float32
    )
    unscaled_projection = jnp.einsum(
        "td,sdc->stc", normed_input, fwd_qkv, preferred_element_type=jnp.float32
    )
    unscaled_projection = unscaled_projection + adapter_scale * jnp.einsum(
        "jlh,jhx->jlx",
        lowrank_attention,
        adapter_attention_delta,
        precision=highest_precision,
        preferred_element_type=jnp.float32,
    )
    queries = (unscaled_projection[0] * scale_row).astype(jnp.bfloat16).reshape(shape_heads)
    key_heads = unscaled_projection[1].astype(jnp.bfloat16).reshape(shape_heads)
    values = unscaled_projection[2].astype(jnp.bfloat16).reshape(shape_heads)
    mixed_output, log_totals = attend_forward(
        queries, key_heads, values, 0, seg_ids, seg_hot, reach_table
    )
    mixed_output = mixed_output.astype(jnp.bfloat16)
    lowrank_output = jnp.dot(mixed_output, adapter_output_delta, preferred_element_type=jnp.float32)
    attention_piece = jnp.einsum(
        "tc,dc->td", mixed_output, fwd_out, preferred_element_type=jnp.float32
    )
    attention_piece = attention_piece + adapter_scale * precise_product(
        lowrank_output, adapter_residual_delta[0]
    )
    middle = token_rows + lax.psum_scatter(
        attention_piece, "tensor", scatter_dimension=0, tiled=True
    )
    hidden_input = lax.all_gather(
        rms_norm(middle, norm_gain_rows[1]).astype(jnp.bfloat16), "tensor", axis=0, tiled=True
    )
    lowrank_up = jnp.dot(hidden_input, adapter_input_delta[3], preferred_element_type=jnp.float32)
    up_projection = jnp.dot(
        hidden_input, fwd_ffn[0], preferred_element_type=jnp.float32
    ) + adapter_scale * precise_product(lowrank_up, adapter_up_delta)
    hidden_activation = silu_act(up_projection).astype(jnp.bfloat16)
    lowrank_down = jnp.dot(
        hidden_activation, adapter_down_delta, preferred_element_type=jnp.float32
    )
    down_piece = jnp.einsum(
        "tf,df->td", hidden_activation, fwd_ffn[1], preferred_element_type=jnp.float32
    )
    down_piece = down_piece + adapter_scale * precise_product(
        lowrank_down, adapter_residual_delta[1]
    )
    output = (
        middle
        + lax.psum_scatter(
            down_piece.astype(jnp.bfloat16), "tensor", scatter_dimension=0, tiled=True
        ).astype(jnp.float32)
    ).astype(jnp.bfloat16)
    back_qkv, back_out, back_ffn = (
        lax.all_gather(attention_weights, "dp", axis=1, tiled=True),
        lax.all_gather(output_weight, "dp", axis=0, tiled=True),
        lax.all_gather(feedforward_weights, "dp", axis=1, tiled=True),
    )
    down_gradient = lax.all_gather(cotangent, "tensor", axis=0, tiled=True)
    low_down_gradient = adapter_scale * jnp.dot(
        down_gradient, adapter_residual_delta[1].T, preferred_element_type=jnp.float32
    )
    second_down_term = adapter_scale * precise_product(lowrank_down.T, down_gradient)
    first_down_term = precise_product(hidden_activation.T, low_down_gradient)
    activation_gradient = jnp.einsum(
        "td,df->tf", down_gradient, back_ffn[1], preferred_element_type=jnp.float32
    )
    activation_gradient = activation_gradient + precise_product(
        low_down_gradient, adapter_down_delta.T
    )
    silu_value, silu_back = jax.vjp(silu_act, up_projection)
    up_gradient = silu_back(activation_gradient)[0].astype(jnp.bfloat16)
    low_up_gradient = adapter_scale * jnp.dot(
        up_gradient, adapter_up_delta.T, preferred_element_type=jnp.float32
    )
    second_up_term = adapter_scale * precise_product(lowrank_up.T, up_gradient)
    term_a_up = precise_product(hidden_input.T, low_up_gradient)
    hidden_gradient = jnp.einsum(
        "tf,df->td", up_gradient, back_ffn[0], preferred_element_type=jnp.float32
    )
    hidden_gradient = hidden_gradient + precise_product(low_up_gradient, adapter_input_delta[3].T)
    hidden_gradient = lax.psum_scatter(
        hidden_gradient.astype(jnp.bfloat16), "tensor", scatter_dimension=0, tiled=True
    ).astype(jnp.float32)
    norm_value, second_back = jax.vjp(
        lambda mid_rows: rms_norm(mid_rows, norm_gain_rows[1]), middle
    )
    grad_middle = cotangent.astype(jnp.float32) + second_back(hidden_gradient)[0]
    attention_gradient = lax.all_gather(
        grad_middle.astype(jnp.bfloat16), "tensor", axis=0, tiled=True
    )
    low_output_gradient = adapter_scale * jnp.dot(
        attention_gradient, adapter_residual_delta[0].T, preferred_element_type=jnp.float32
    )
    second_output_term = adapter_scale * precise_product(lowrank_output.T, attention_gradient)
    first_output_term = precise_product(mixed_output.T, low_output_gradient)
    grad_mixed = jnp.dot(
        attention_gradient, back_out, preferred_element_type=jnp.float32
    ) + precise_product(low_output_gradient, adapter_output_delta.T)
    grad_mixed = grad_mixed.astype(jnp.bfloat16).reshape(shape_heads)
    grad_query, grad_key, grad_value = attend_backward(
        queries, key_heads, values, grad_mixed, log_totals, 0, seg_ids, seg_hot, reach_table
    )
    projection_gradient = jnp.stack(
        [
            (grad_query * scale_row).astype(jnp.bfloat16),
            grad_key.astype(jnp.bfloat16),
            grad_value.astype(jnp.bfloat16),
        ]
    )
    low_gradients = adapter_scale * jnp.einsum(
        "nag,nqg->naq",
        projection_gradient,
        adapter_attention_delta,
        preferred_element_type=jnp.float32,
    )
    second_attention_term = adapter_scale * jnp.einsum(
        "str,stc->src",
        lowrank_attention,
        projection_gradient,
        precision=highest_precision,
        preferred_element_type=jnp.float32,
    )
    term_a_qkv = jnp.einsum(
        "td,str->sdr",
        normed_input,
        low_gradients,
        precision=highest_precision,
        preferred_element_type=jnp.float32,
    )
    grad_normed = jnp.einsum(
        "stc,sdc->td", projection_gradient, back_qkv, preferred_element_type=jnp.float32
    )
    grad_normed = grad_normed + jnp.einsum(
        "str,sdr->td",
        low_gradients,
        adapter_input_delta[:3],
        precision=highest_precision,
        preferred_element_type=jnp.float32,
    )
    grad_normed = lax.psum_scatter(
        grad_normed.astype(jnp.bfloat16), "tensor", scatter_dimension=0, tiled=True
    ).astype(jnp.float32)
    first_value, first_back = jax.vjp(
        lambda in_rows: rms_norm(in_rows, norm_gain_rows[0]), token_rows
    )
    input_grad = grad_middle + first_back(grad_normed)[0]

    def placement_columns(term, gather_along_axis, start, full_len):
        full_shape = list(term.shape)
        full_shape[gather_along_axis] = full_len
        return lax.dynamic_update_slice_in_dim(
            jnp.zeros(tuple(full_shape), jnp.float32), term, start, gather_along_axis
        )

    grad_a_in = select_slot(jnp.concatenate([term_a_qkv, term_a_up[None]], axis=0), 1)
    grad_b_qkv = select_slot(
        placement_columns(
            second_attention_term,
            2,
            tensor_position * head_columns,
            adapter_second_attention.shape[3],
        ),
        1,
    )
    grad_b_up = select_slot(
        placement_columns(
            second_up_term, 1, tensor_position * hidden_columns, adapter_second_up.shape[2]
        ),
        0,
    )
    grad_a_out = select_slot(
        placement_columns(
            first_output_term, 0, tensor_position * head_columns, adapter_first_output.shape[1]
        ),
        0,
    )
    grad_a_down = select_slot(
        placement_columns(
            first_down_term, 0, tensor_position * hidden_columns, adapter_first_down.shape[1]
        ),
        0,
    )
    grad_b_res = select_slot(jnp.stack([second_output_term, second_down_term]), 1)
    summed = lax.psum(
        (grad_a_in, grad_b_qkv, grad_b_up, grad_a_out, grad_a_down, grad_b_res), ("dp", "tensor")
    )
    return (output, input_grad, summed[0], summed[1], summed[2], summed[3], summed[4], summed[5])


def solution(mesh):
    in_specs = (
        P(("dp", "tensor"), None),
        P(("dp", "tensor"), None),
        P("dp"),
        P("dp", None),
        P("dp", None),
        P(),
        P(),
        P(None, "dp", "tensor"),
        P("dp", "tensor"),
        P(None, "dp", "tensor"),
        P(),
        P(),
        P(),
        P(),
        P(),
        P(),
    )
    out_specs = (P(("dp", "tensor"), None), P(("dp", "tensor"), None), P(), P(), P(), P(), P(), P())
    return jax.shard_map(local, mesh=mesh, in_specs=in_specs, out_specs=out_specs, check_vma=False)
```

profile of v0, /device:TPU:0, one launch (start us, length us, event | category | flops | bytes accessed | tf_op | source)
XLA Modules:
  0.0 1237.3 jit_solution(18061953032688539600)
XLA Ops:
  16.9 36.2 %all_gather.26 = bf16[1280,320]{1,0:T(8,128)(2,1)} all-gather(bf16[160,320]{1,0:T(8,128)(2,1)S(1)} %copy-done.53), channel_id=1, replica_groups=mesh['dp'=8,'tensor'=4] {'dp'}, dimensions={0}, use_global_device_ids=true | all-gather | bytes 921600 | tf_op jit(solution)/shard_map/all_gather | solution.py:171
  61.8 56.1 %all-gather.9.cloned.1.call-done = bf16[3,1280,320]{2,1,0:T(8,128)(2,1)} async-done(((bf16[3,160,320]{2,1,0:T(8,128)(2,1)}), bf16[3,1280,320]{2,1,0:T(8,128)(2,1)}) %all-gather.9.cloned.1.call-update) | async-done | bytes 2457616 | tf_op jit(solution)/shard_map/all_gather | solution.py:170
  117.9 8.4 fusion.47
  126.3 4.7 fusion.110
  134.0 97.5 %while.27 = (s32[]{:T(128)}, bf16[4,512,4,80]{1,3,2,0:T(8,128)(2,1)}, f32[4,4,512]{2,1,0:T(4,128)}, s32[4]{0:T(128)}, f32[2048,13]{0,1:T(8,128)}, /*index=5*/f32...) while((s32[]{:T(128)}, ...), condition=%wide.region_6.7_spmd, body=%wide.region_3.6_spmd.sunk | while | flops 1549783552 | bytes 74136512 | solution.py:82
  139.1 5.5 fusion.201
  152.6 4.7 fusion.203
  163.4 5.5 fusion.201
  176.9 4.7 fusion.203
  187.6 5.5 fusion.201
  201.1 4.7 fusion.203
  211.8 5.5 fusion.201
  225.3 4.7 fusion.203
  238.3 8.3 multiply_add_fusion
  247.9 82.0 %reduce-scatter.5.cloned.1.call-done = f32[512,1280]{1,0:T(8,128)} async-done(((f32[2048,1280]{1,0:T(8,128)}), f32[512,1280]{1,0:T(8,128)}) %reduce-scatter.5.cloned.1.call-update) | async-done | bytes 2621456 | tf_op jit(solution)/shard_map/reduce_scatter | solution.py:233
  334.9 36.8 %all-gather.15.cloned.1.call-done = bf16[2048,1280]{1,0:T(8,128)(2,1)} async-done(((bf16[512,1280]{1,0:T(8,128)(2,1)}), bf16[2048,1280]{1,0:T(8,128)(2,1)}) %all-gather.15.cloned.1.call-update) | async-done | bytes 5242896 | tf_op jit(solution)/shard_map/all_gather | solution.py:264
  375.7 45.9 %all-gather.13.cloned.1.call-done = bf16[2,1280,320]{2,1,0:T(8,128)(2,1)} async-done(((bf16[2,160,320]{2,1,0:T(8,128)(2,1)}), bf16[2,1280,320]{2,1,0:T(8,128)(2,1)}) %all-gather.13.cloned.1.call-update) | async-done | bytes 1638416 | tf_op jit(solution)/shard_map/all_gather | solution.py:172
  421.6 6.2 fusion.66
  427.8 34.9 %all-gather.11.cloned.1.call-done = bf16[2048,1280]{1,0:T(8,128)(2,1)} async-done(((bf16[512,1280]{1,0:T(8,128)(2,1)}), bf16[2048,1280]{1,0:T(8,128)(2,1)}) %all-gather.11.cloned.1.call-update) | async-done | bytes 5242896 | tf_op jit(solution)/shard_map/all_gather | solution.py:236
  462.7 4.8 fusion.65
  480.4 6.7 add_convert_fusion
  487.1 51.4 %reduce-scatter.9.cloned.1.call-done = bf16[512,1280]{1,0:T(8,128)(2,1)} async-done(((bf16[2048,1280]{1,0:T(8,128)(2,1)}), bf16[512,1280]{1,0:T(8,128)(2,1)}) %reduce-scatter.9.cloned.1.call-update) | async-done | bytes 1310736 | tf_op jit(solution)/shard_map/reduce_scatter | solution.py:287
  546.8 39.8 %all-gather.17.cloned.1.call-done = bf16[2048,1280]{1,0:T(8,128)(2,1)} async-done(((bf16[512,1280]{1,0:T(8,128)(2,1)}), bf16[2048,1280]{1,0:T(8,128)(2,1)}) %all-gather.17.cloned.1.call-update) | async-done | bytes 5242896 | tf_op jit(solution)/shard_map/all_gather | solution.py:294
  596.1 313.9 %while.28 = (s32[]{:T(128)}, f32[2048,4,80]{0,2,1:T(8,128)}, f32[2048,4,80]{0,2,1:T(8,128)}, f32[4,512,4,80]{1,0,3,2:T(4,128)}, s32[4]{0:T(128)}, /*index=5*/bf1...) while((s32[]{:T(128)}, f32[2048,4,80]{0,2,1:T(8,128)}, ...), condition=%wide.region_14.15_spmd.clone, body=%wide.region_12.14_spmd.clone.sunk | while | flops 3578253824 | bytes 220601280 | solution.py:124
  602.3 6.3 fusion.219
  612.1 5.8 copy-done.1
  617.9 7.5 fusion.221
  625.3 15.1 %multiply_reduce_fusion.4 = (f32[4,512]{1,0:T(4,128)S(1)}, f32[4,512,2048]{2,1,0:T(8,128)}) fusion(f32[4,512,2048]{2,1,0:T(8,128)} %copy-done.1, f32[4,512]{1,0:T(4,128)S(1)} %dynamic-slice_bitcast_fusion.14, pred[512,2048]{1,0:T(8,128)(4,1)} %fusion.219, bf16[2048,4,80]{0,2,1:T(8,128)(2,1)} %get-tuple-element.476, ...), kind=kOutput, calls=%fused_computation.20.clone.1 | convolution fusion | flops 687863808 | bytes 36257796 | tf_op jit(solution)/shard_map/while/body/eval_jaxpr/qhd,khd->hqk/dot_general | solution.py:103
  640.5 12.0 multiply_convert_fusion.5
  655.1 4.2 fusion.220
  660.0 13.6 %dynamic_update_slice.43 = f32[4,512,4,80]{1,0,3,2:T(4,128)} dynamic-update-slice(f32[4,512,4,80]{1,0,3,2:T(4,128)} %get-tuple-element.451, f32[1,512,4,80]{1,0,3,2:T(1,128)S(1)} %copy.43, s32[]{:T(128)S(6)} %copy.60, s32[]{:T(128)} %constant.170.clone.1..sunk.1, s32[]{:T(128)} %constant.170.clone.1..sunk.1, s32[]{:T(128)} %constant.170.clone.1..sunk.1) | dynamic-update-slice | bytes 1310724 | tf_op jit(solution)/shard_map/while/body/jit(dynamic_update_index_in_dim)/dynamic_update_slice | solution.py:82
  679.5 6.3 fusion.219
  689.2 5.8 copy-done.1
  695.0 8.3 fusion.221
  703.3 15.1 %multiply_reduce_fusion.4 = (f32[4,512]{1,0:T(4,128)S(1)}, f32[4,512,2048]{2,1,0:T(8,128)}) fusion(f32[4,512,2048]{2,1,0:T(8,128)} %copy-done.1, f32[4,512]{1,0:T(4,128)S(1)} %dynamic-slice_bitcast_fusion.14, pred[512,2048]{1,0:T(8,128)(4,1)} %fusion.219, bf16[2048,4,80]{0,2,1:T(8,128)(2,1)} %get-tuple-element.476, ...), kind=kOutput, calls=%fused_computation.20.clone.1 | convolution fusion | flops 687863808 | bytes 36257796 | tf_op jit(solution)/shard_map/while/body/eval_jaxpr/qhd,khd->hqk/dot_general | solution.py:103
  718.4 12.0 multiply_convert_fusion.5
  733.0 5.1 fusion.220
  738.8 13.6 %dynamic_update_slice.43 = f32[4,512,4,80]{1,0,3,2:T(4,128)} dynamic-update-slice(f32[4,512,4,80]{1,0,3,2:T(4,128)} %get-tuple-element.451, f32[1,512,4,80]{1,0,3,2:T(1,128)S(1)} %copy.43, s32[]{:T(128)S(6)} %copy.60, s32[]{:T(128)} %constant.170.clone.1..sunk.1, s32[]{:T(128)} %constant.170.clone.1..sunk.1, s32[]{:T(128)} %constant.170.clone.1..sunk.1) | dynamic-update-slice | bytes 1310724 | tf_op jit(solution)/shard_map/while/body/jit(dynamic_update_index_in_dim)/dynamic_update_slice | solution.py:82
  758.3 6.3 fusion.219
  768.1 5.8 copy-done.1
  773.8 8.3 fusion.221
  782.1 15.0 %multiply_reduce_fusion.4 = (f32[4,512]{1,0:T(4,128)S(1)}, f32[4,512,2048]{2,1,0:T(8,128)}) fusion(f32[4,512,2048]{2,1,0:T(8,128)} %copy-done.1, f32[4,512]{1,0:T(4,128)S(1)} %dynamic-slice_bitcast_fusion.14, pred[512,2048]{1,0:T(8,128)(4,1)} %fusion.219, bf16[2048,4,80]{0,2,1:T(8,128)(2,1)} %get-tuple-element.476, ...), kind=kOutput, calls=%fused_computation.20.clone.1 | convolution fusion | flops 687863808 | bytes 36257796 | tf_op jit(solution)/shard_map/while/body/eval_jaxpr/qhd,khd->hqk/dot_general | solution.py:103
  797.2 12.0 multiply_convert_fusion.5
  811.8 5.1 fusion.220
  817.6 13.6 %dynamic_update_slice.43 = f32[4,512,4,80]{1,0,3,2:T(4,128)} dynamic-update-slice(f32[4,512,4,80]{1,0,3,2:T(4,128)} %get-tuple-element.451, f32[1,512,4,80]{1,0,3,2:T(1,128)S(1)} %copy.43, s32[]{:T(128)S(6)} %copy.60, s32[]{:T(128)} %constant.170.clone.1..sunk.1, s32[]{:T(128)} %constant.170.clone.1..sunk.1, s32[]{:T(128)} %constant.170.clone.1..sunk.1) | dynamic-update-slice | bytes 1310724 | tf_op jit(solution)/shard_map/while/body/jit(dynamic_update_index_in_dim)/dynamic_update_slice | solution.py:82
  837.0 6.3 fusion.219
  846.8 5.8 copy-done.1
  852.5 8.3 fusion.221
  860.8 15.1 %multiply_reduce_fusion.4 = (f32[4,512]{1,0:T(4,128)S(1)}, f32[4,512,2048]{2,1,0:T(8,128)}) fusion(f32[4,512,2048]{2,1,0:T(8,128)} %copy-done.1, f32[4,512]{1,0:T(4,128)S(1)} %dynamic-slice_bitcast_fusion.14, pred[512,2048]{1,0:T(8,128)(4,1)} %fusion.219, bf16[2048,4,80]{0,2,1:T(8,128)(2,1)} %get-tuple-element.476, ...), kind=kOutput, calls=%fused_computation.20.clone.1 | convolution fusion | flops 687863808 | bytes 36257796 | tf_op jit(solution)/shard_map/while/body/eval_jaxpr/qhd,khd->hqk/dot_general | solution.py:103
  875.9 12.0 multiply_convert_fusion.5
  890.5 5.1 fusion.220
  896.3 13.6 %dynamic_update_slice.43 = f32[4,512,4,80]{1,0,3,2:T(4,128)} dynamic-update-slice(f32[4,512,4,80]{1,0,3,2:T(4,128)} %get-tuple-element.451, f32[1,512,4,80]{1,0,3,2:T(1,128)S(1)} %copy.43, s32[]{:T(128)S(6)} %copy.60, s32[]{:T(128)} %constant.170.clone.1..sunk.1, s32[]{:T(128)} %constant.170.clone.1..sunk.1, s32[]{:T(128)} %constant.170.clone.1..sunk.1) | dynamic-update-slice | bytes 1310724 | tf_op jit(solution)/shard_map/while/body/jit(dynamic_update_index_in_dim)/dynamic_update_slice | solution.py:82
  910.0 4.5 reshape.254
  921.8 7.3 fusion.108
  929.1 6.5 fusion.42
  937.9 4.1 fusion.67
  942.1 7.5 add_convert_fusion.1
  957.3 4.8 convolution_bitcast_fusion.2
  967.5 5.3 convolution_multiply_fusion.7
  973.5 4.7 fusion.61
  978.2 5.3 fusion.58
  992.6 48.2 %reduce-scatter.7.cloned.1.call-done = bf16[512,1280]{1,0:T(8,128)(2,1)} async-done(((bf16[2048,1280]{1,0:T(8,128)(2,1)}), bf16[512,1280]{1,0:T(8,128)(2,1)}) %reduce-scatter.7.cloned.1.call-update) | async-done | bytes 1310736 | tf_op jit(solution)/shard_map/reduce_scatter | solution.py:255
  1040.8 5.5 fusion.52
  1046.4 175.3 %all-reduce.3.cloned.1.call-done = (f32[4,8,1280,16]{2,3,1,0:T(8,128)}, f32[3,8,16,1280]{3,2,1,0:T(8,128)}, f32[8,16,1280]{2,1,0:T(8,128)}, f32[8,1280,16]{1,2,0...) async-done(((f32[4,8,1280,16]{2,3,1,0:T(8,128)}, f32[3,8,16,1280]{3,2,1,0:T(8,128)}, f32[8,16,1280]{2,1,0:T(8,128)}, f32[8,1280,16]{1,2,0:T(8,128)}, ...) | async-done | bytes 7864336 | tf_op jit(solution)/shard_map/psum | solution.py:390
  (328 shorter events, 199.1 us)
Async XLA Ops:
  7.2 50.5 %copy-start = (bf16[4,8,1280,16]{2,3,1,0:T(8,128)(2,1)S(1)}, bf16[4,8,1280,16]{2,3,1,0:T(8,128)(2,1)}, u32[]{:S(2)}) copy-start(bf16[4,8,1280,16]{2,3,1,0:T(8,128)(2,1)} %param.30) | copy-start | bytes 3932164
  7.2 8.7 copy-start.66
  7.2 9.5 copy-start.67
  7.2 9.5 copy-start.68
  7.2 9.7 copy-start.53
  7.2 50.4 %all-gather.7.cloned.1.call-start = ((), (), s32[]{:S(2)}) async-start(), calls=%async_computation.4 | async-start | bytes 6553600 | tf_op jit(solution)/shard_map/all_gather | solution.py:203
  14.4 103.5 %all-gather.9.cloned.1.call-start = ((), (), s32[]{:S(2)}) async-start(), calls=%async_computation.5 | async-start | bytes 3317760 | tf_op jit(solution)/shard_map/all_gather | solution.py:170
  15.1 314.7 %reduce-scatter.5.cloned.1.call-start = ((), (), s32[]{:S(2)}) async-start(), calls=%async_computation.6 | async-start | bytes 13107200 | tf_op jit(solution)/shard_map/reduce_scatter | solution.py:233
  16.7 115.9 %copy-start.63 = (f32[80]{0:T(128)}, f32[80]{0:T(128)S(1)}, u32[]{:S(2)}) copy-start(f32[80]{0:T(128)S(1)} %broadcast_multiply_fusion.6) | copy-start | bytes 964
  61.8 64.5 %copy-start.23 = (f32[3,16,2048]{2,1,0:T(8,128)}, f32[3,16,2048]{2,1,0:T(8,128)S(1)}, u32[]{:S(2)}) copy-start(f32[3,16,2048]{2,1,0:T(8,128)S(1)} %fusion.45) | copy-start | bytes 1179652
  148.6 4.0 copy-start.9
  148.7 4.0 copy-start.28
  172.9 4.0 copy-start.9
  172.9 4.0 copy-start.28
  197.1 4.0 copy-start.9
  197.1 4.0 copy-start.28
  221.3 4.0 copy-start.9
  221.3 4.0 copy-start.28
  246.7 85.9 %copy-start.49 = (f32[1280]{0:T(1024)S(1)}, f32[1280]{0:T(1024)}, u32[]{:S(2)}) copy-start(f32[1280]{0:T(1024)} %get-tuple-element.178) | copy-start | bytes 15364
  246.7 125.0 %all-gather.15.cloned.1.call-start = ((), (), s32[]{:S(2)}) async-start(), calls=%async_computation.10 | async-start | bytes 6553600 | tf_op jit(solution)/shard_map/all_gather | solution.py:264
  247.3 174.3 %all-gather.13.cloned.1.call-start = ((), (), s32[]{:S(2)}) async-start(), calls=%async_computation.8 | async-start | bytes 2211840 | tf_op jit(solution)/shard_map/all_gather | solution.py:172
  247.9 214.8 %all-gather.11.cloned.1.call-start = ((), (), s32[]{:S(2)}) async-start(), calls=%async_computation.7 | async-start | bytes 6553600 | tf_op jit(solution)/shard_map/all_gather | solution.py:236
  329.9 3.3 copy-start.7
  332.5 209.3 %copy-start.54 = (f32[512]{0:T(512)}, f32[512]{0:T(512)S(1)}, u32[]{:S(2)}) copy-start(f32[512]{0:T(512)S(1)} %fusion.106) | copy-start | bytes 6148
  334.7 203.9 %reduce-scatter.9.cloned.1.call-start = ((), (), s32[]{:S(2)}) async-start(), calls=%async_computation.11 | async-start | bytes 6553600 | tf_op jit(solution)/shard_map/reduce_scatter | solution.py:287
  375.7 97.1 %copy-start.42 = (f32[16,2048]{1,0:T(8,128)}, f32[16,2048]{1,0:T(8,128)S(1)}, u32[]{:S(2)}) copy-start(f32[16,2048]{1,0:T(8,128)S(1)} %convolution_multiply_fusion.6) | copy-start | bytes 393220
  462.7 4.9 copy-start.10
  469.0 3.8 copy-start.37
  469.0 3.8 copy-start.69
  472.8 4.6 copy-start.21
  487.1 99.5 %all-gather.17.cloned.1.call-start = ((), (), s32[]{:S(2)}) async-start(), calls=%async_computation.12 | async-start | bytes 6553600 | tf_op jit(solution)/shard_map/all_gather | solution.py:294
  538.5 3.7 copy-start.8
  538.6 4.1 copy-start.17
  542.6 3.3 copy-start.60
  542.6 3.4 copy-start.64
  546.0 443.6 %reduce-scatter.11.cloned.1.call-start = ((), (), s32[]{:S(2)}) async-start(), calls=%async_computation.13 | async-start | bytes 6553600 | tf_op jit(solution)/shard_map/reduce_scatter | solution.py:346
  586.5 4.1 copy-start.11
  586.5 4.3 copy-start.20
  612.1 5.8 copy-start.1
  625.3 15.1 %copy-start.2 = (pred[512,2048]{1,0:T(8,128)(4,1)S(1)}, pred[512,2048]{1,0:T(8,128)(4,1)}, u32[]{:S(2)}) copy-start(pred[512,2048]{1,0:T(8,128)(4,1)} %fusion.219) | copy-start | bytes 3145732 | tf_op jit(solution)/shard_map/while
  689.2 5.8 copy-start.1
  703.3 15.1 %copy-start.2 = (pred[512,2048]{1,0:T(8,128)(4,1)S(1)}, pred[512,2048]{1,0:T(8,128)(4,1)}, u32[]{:S(2)}) copy-start(pred[512,2048]{1,0:T(8,128)(4,1)} %fusion.219) | copy-start | bytes 3145732 | tf_op jit(solution)/shard_map/while
  768.0 5.8 copy-start.1
  782.1 15.0 %copy-start.2 = (pred[512,2048]{1,0:T(8,128)(4,1)S(1)}, pred[512,2048]{1,0:T(8,128)(4,1)}, u32[]{:S(2)}) copy-start(pred[512,2048]{1,0:T(8,128)(4,1)} %fusion.219) | copy-start | bytes 3145732 | tf_op jit(solution)/shard_map/while
  846.7 5.8 copy-start.1
  860.8 15.1 %copy-start.2 = (pred[512,2048]{1,0:T(8,128)(4,1)S(1)}, pred[512,2048]{1,0:T(8,128)(4,1)}, u32[]{:S(2)}) copy-start(pred[512,2048]{1,0:T(8,128)(4,1)} %fusion.219) | copy-start | bytes 3145732 | tf_op jit(solution)/shard_map/while
  916.6 4.3 copy-start.31
  935.6 105.3 %reduce-scatter.7.cloned.1.call-start = ((), (), s32[]{:S(2)}) async-start(), calls=%async_computation.9 | async-start | bytes 6553600 | tf_op jit(solution)/shard_map/reduce_scatter | solution.py:255
  949.6 4.0 copy-start.43
  949.6 7.7 copy-start.34
  949.6 272.1 %all-reduce.3.cloned.1.call-start = ((), (), s32[]{:S(2)}) async-start(), calls=%async_computation.14 | async-start | bytes 15728640 | tf_op jit(solution)/shard_map/psum | solution.py:390
  953.6 8.4 slice-start
  957.3 4.8 slice-start.1
  962.1 3.8 copy-start.13
  962.1 3.8 copy-start.26
  962.1 5.3 copy-start.24
  967.4 6.1 copy-start.36
  973.5 4.7 copy-start.48
  978.2 6.6 copy-start.47
  989.5 51.3 %copy-start.50 = (f32[1280]{0:T(1024)S(1)}, f32[1280]{0:T(1024)}, u32[]{:S(2)}) copy-start(f32[1280]{0:T(1024)} %get-tuple-element.178) | copy-start | bytes 15364
  989.5 51.3 %copy-start.55 = (f32[512]{0:T(512)S(1)}, f32[512]{0:T(512)}, u32[]{:S(2)}) copy-start(f32[512]{0:T(512)} %copy-done.54) | copy-start | bytes 6148
  989.5 51.3 %copy-start.59 = (f32[512]{0:T(512)S(1)}, f32[512]{0:T(512)}, u32[]{:S(2)}) copy-start(f32[512]{0:T(512)} %copy-done.58) | copy-start | bytes 6148
  989.5 51.3 %copy-start.61 = (f32[512]{0:T(512)S(1)}, f32[512]{0:T(512)}, u32[]{:S(2)}) copy-start(f32[512]{0:T(512)} %copy-done.60) | copy-start | bytes 6148
  1221.7 3.6 copy-start.22
  (34 other events, 63.7 us)
Sparse Core Ops, SparseCore 0:
  14.5 43.1 all-gather.6
  59.9 57.9 all-gather.8
  246.8 83.0 reduce-scatter.4
  331.3 40.4 all-gather.14
  373.8 47.8 all-gather.12
  423.6 39.0 all-gather.10
  487.2 51.3 reduce-scatter.8
  546.1 40.3 all-gather.16
  935.7 51.3 reduce-scatter.10
  989.4 51.3 reduce-scatter.6
  1047.8 173.8 all-reduce.2
where the time goes:
time: 1250 us; the launch traced here: 1240 us
  waiting for transfers between devices  576 us (46%)
  matrix products  357 us (29%)
  local copies, waits for them, and re-layouts  127 us (10%)
  other arithmetic  107 us (9%)
  blocking collectives  36.2 us (3%)
  loops' own time  17.7 us (1%)
  between operations  15.8 us (1%)
    psum x1, waiting for transfers between devices, local(): lax.psum((grad_a_in, grad_b_qkv, grad_b_up, grad_a_out, grad_a_down, grad...  175 us
    dot_general x29, matrix products, precise_product(): jnp.dot(first_term, second_term, precision=highest_precision, preferred_e...  106 us
    reduce_scatter x1, waiting for transfers between devices, local(): lax.psum_scatter(attention_piece, 'tensor', scatter_dimension=0, tiled=True)  82 us
    dot_general x4, matrix products, one_block(): jnp.einsum('qhd,khd->hqk', block_grad, values, preferred_element_type=jnp...  60.3 us
    dynamic_update_slice x8, local copies, waits for them, and re-layouts, attend_forward(): mixed_output, log_totals = lax.map(one_block, local_starts)  57 us
    all_gather x1, waiting for transfers between devices, local(): lax.all_gather(attention_weights, 'dp', axis=1, tiled=True)  56.1 us
    reduce_scatter x1, waiting for transfers between devices, local(): lax.psum_scatter(hidden_gradient.astype(jnp.bfloat16), 'tensor', scatter_...  51.4 us
    reduce_scatter x1, waiting for transfers between devices, local(): lax.psum_scatter(down_piece.astype(jnp.bfloat16), 'tensor', scatter_dimen...  48.2 us
  transfers between devices with their start and end apart: 11, of which 10 were waited for; matrix products, arithmetic and copies ran while one was open for 6% of the time, Pallas kernels for 0%

commit v1 on v0

v1 whole, which is shorter than its diff:
```python
import functools
import math

import jax
import jax.numpy as jnp
from jax import lax
from jax.experimental import pallas as pl
from jax.experimental.pallas import tpu as pltpu
from jax.sharding import PartitionSpec as P

F32, BF16 = jnp.float32, jnp.bfloat16
BIG = 1e30
BLK = 256
HD = 80

def dot(a, b):
    return lax.dot_general(a, b, (((1,), (0,)), ((), ())), preferred_element_type=F32)
def dot_nt(a, b):
    return lax.dot_general(a, b, (((1,), (1,)), ((), ())), preferred_element_type=F32)
def dot_tn(a, b):
    return lax.dot_general(a, b, (((0,), (0,)), ((), ())), preferred_element_type=F32)

def project(b, x_ref, wp_ref, a_ref, bp_ref, scale_ref, seg_ref, mq_ref, q_ref, qt_ref, k_ref, kt_ref, v_ref, vt_ref, rank_ref):
    rows = pl.ds(pl.multiple_of(b * BLK, BLK), BLK)
    xb = x_ref[rows, :]
    rank = dot_nt(xb, a_ref[...]).astype(BF16)
    rank_ref[rows, :] = rank
    lane = lax.broadcasted_iota(jnp.int32, (BLK, 128), 1)
    tok = (lax.broadcasted_iota(jnp.int32, (BLK, 128), 0) + b * BLK).astype(F32)
    hot = jnp.where((tok >= seg_ref[0:1, :]) & (tok < seg_ref[1:2, :]), 1.0, 0.0)
    qfeat = dot(hot.astype(BF16), mq_ref[...])
    kfeat = jnp.where((lane >= HD + 13) & (lane < HD + 16), 1.0, hot)
    vfeat = jnp.where(lane < HD + 2, 1.0, 0.0)
    heads = q_ref.shape[0]
    for s, (n_ref, t_ref, feat) in enumerate(((q_ref, qt_ref, qfeat), (k_ref, kt_ref, kfeat), (v_ref, vt_ref, vfeat))):
        y = dot(xb, wp_ref[s]) + dot(rank, bp_ref[s])
        if s == 0:
            y = y * scale_ref[...]
        for h in range(heads):
            yh = jnp.where(lane < HD, y[:, h * 128:(h + 1) * 128], feat)
            n_ref[h, rows, :] = yh.astype(BF16)
            yt = yh.T
            t_ref[h, :, rows] = yt[:t_ref.shape[1]].astype(BF16)

def attend_block(i, qt_ref, k_ref, vt_ref, m_ref, acc_ref, mixt_ref, mix_ref, count=None, jlist=None):
    heads = qt_ref.shape[0]
    cols = pl.ds(pl.multiple_of(i * BLK, BLK), BLK)
    m_ref[...] = jnp.full_like(m_ref, -3e38)
    acc_ref[...] = jnp.zeros_like(acc_ref)
    def step(j, diag):
        rows = pl.ds(pl.multiple_of(j * BLK, BLK), BLK)
        hs = range(heads)
        ss = [dot(k_ref[h, rows, :], qt_ref[h, :, cols]) for h in hs]
        if diag:
            low = lax.broadcasted_iota(jnp.int32, ss[0].shape, 0) <= lax.broadcasted_iota(jnp.int32, ss[0].shape, 1)
            ss = [jnp.where(low, s, -BIG) for s in ss]
        olds = [m_ref[h] for h in hs]
        news = [jnp.maximum(olds[h], jnp.max(ss[h], axis=0, keepdims=True)) for h in hs]
        ps = [jnp.exp(ss[h] - news[h]).astype(BF16) for h in hs]
        pv = [dot(vt_ref[h, :, rows], ps[h]) for h in hs]
        accs = [acc_ref[h] * jnp.exp(olds[h] - news[h]) + pv[h] for h in hs]
        for h in hs:
            acc_ref[h] = accs[h]
            m_ref[h] = news[h]
    if jlist is None:
        lax.fori_loop(0, i, lambda j, c: (step(j, False), c)[1], 0)
    else:
        lax.fori_loop(0, count, lambda n, c: (step(jlist(n), False), c)[1], 0)
    step(i, True)
    outs = []
    for h in range(heads):
        acc = acc_ref[h]
        l = acc[HD:HD + 1]
        o = acc[:HD] * (1.0 / l)
        lse = m_ref[h] + jnp.log(l)
        hi = (-lse).astype(BF16).astype(F32)
        mid = (-lse - hi).astype(BF16).astype(F32)
        lo = -lse - hi - mid
        r = lax.broadcasted_iota(jnp.int32, (16, BLK), 0)
        old = qt_ref[h, HD:HD + 16, cols].astype(F32)
        new = jnp.where(r == 13, hi, jnp.where(r == 14, mid, jnp.where(r == 15, lo, old)))
        qt_ref[h, HD:HD + 16, cols] = new.astype(BF16)
        outs.append(o)
    ot = jnp.concatenate(outs, axis=0)
    mixt_ref[:, cols] = ot.astype(BF16)
    mix_ref[cols, :] = ot.T.astype(BF16)

def seg_masks(len_ref, par_ref, segs, nblk):
    start, km, qm = 0, [0] * nblk, [0] * nblk
    for u in range(segs):
        end = start + len_ref[u]
        up = par_ref[u]
        anc = jnp.int32(1 << u) | (jnp.int32(1) << up) | (jnp.int32(1) << par_ref[up])
        for b in range(nblk):
            inside = (start < (b + 1) * BLK) & (end > b * BLK)
            km[b] = km[b] | jnp.where(inside, jnp.int32(1 << u), 0)
            qm[b] = qm[b] | jnp.where(inside, anc, 0)
        start = end
    return km, qm

def spread_heads(hcols, pad):
    c = lax.broadcasted_iota(jnp.int32, (hcols, pad), 0)
    l = lax.broadcasted_iota(jnp.int32, (hcols, pad), 1)
    return jnp.where(((l & 127) < HD) & ((l >> 7) * HD + (l & 127) == c), 1.0, 0.0).astype(BF16)


def fwd_kernel(x_ref, wq_ref, a_ref, b_ref, scale_ref, seg_ref, mq_ref,
               q_ref, qt_ref, k_ref, kt_ref, v_ref, rank_ref, mixt_ref, mix_ref, wp_ref, bp_ref,
               vt_ref, m_ref, acc_ref):
    sel = spread_heads(wq_ref.shape[2], wp_ref.shape[2])
    bp_ref[...] = jnp.zeros_like(bp_ref)
    for s in range(3):
        wp_ref[s] = dot(wq_ref[s], sel).astype(BF16)
        n = b_ref.shape[1]
        bp_ref[s, s * n:(s + 1) * n] = (0.5 * dot(b_ref[s], sel)).astype(BF16)
    nblk = x_ref.shape[0] // BLK
    lax.fori_loop(0, nblk, lambda b, c: (project(b, x_ref, wp_ref, a_ref, bp_ref, scale_ref, seg_ref, mq_ref, q_ref, qt_ref, k_ref, kt_ref, v_ref, vt_ref, rank_ref), c)[1], 0)
    lax.fori_loop(0, nblk, lambda i, c: (attend_block(i, qt_ref, k_ref, vt_ref, m_ref, acc_ref, mixt_ref, mix_ref), c)[1], 0)


def bwd_prep(b, dm_ref, mixt_ref, do_ref, dot_ref):
    rows = pl.ds(pl.multiple_of(b * BLK, BLK), BLK)
    heads = do_ref.shape[0]
    dt = dm_ref[rows, :].astype(F32).T
    prod = dt * mixt_ref[:, rows].astype(F32)
    r = lax.broadcasted_iota(jnp.int32, (16, BLK), 0)
    for h in range(heads):
        d = dt[h * HD:(h + 1) * HD]
        delta = -jnp.sum(prod[h * HD:(h + 1) * HD], axis=0, keepdims=True)
        hi = delta.astype(BF16).astype(F32)
        ext = jnp.where(r == 0, hi, jnp.where(r == 1, delta - hi, 0.0))
        full = jnp.concatenate([d, ext, jnp.zeros((32, BLK), F32)], axis=0)
        dot_ref[h, :, rows] = full.astype(BF16)
        do_ref[h, rows, :] = full.T.astype(BF16)

def bwd_pair(i, j, diag, q_ref, qt_ref, k_ref, kt_ref, v_ref, do_ref, dot_ref, dqt_ref, dk_ref, dv_ref):
    heads = q_ref.shape[0]
    cols = pl.ds(pl.multiple_of(i * BLK, BLK), BLK)
    rows = pl.ds(pl.multiple_of(j * BLK, BLK), BLK)
    hs = range(heads)
    ss = [dot(k_ref[h, rows, :], qt_ref[h, :, cols]) for h in hs]
    dps = [dot(v_ref[h, rows, :], dot_ref[h, :, cols]) for h in hs]
    if diag:
        low = lax.broadcasted_iota(jnp.int32, ss[0].shape, 0) <= lax.broadcasted_iota(jnp.int32, ss[0].shape, 1)
        ss = [jnp.where(low, s, -BIG) for s in ss]
    ps = [jnp.exp(s) for s in ss]
    dss = [(p * dp).astype(BF16) for p, dp in zip(ps, dps)]
    ps = [p.astype(BF16) for p in ps]
    dvs = [dot(ps[h], do_ref[h, cols, :]) for h in hs]
    dks = [dot(dss[h], q_ref[h, cols, :]) for h in hs]
    dqs = [dot(kt_ref[h, :, rows], dss[h]) for h in hs]
    for h in hs:
        dv_ref[h, rows, :] += dvs[h]
        dk_ref[h, rows, :] += dks[h]
        dqt_ref[h, :, cols] += dqs[h]

def bwd_kernel(len_ref, par_ref, dm_ref, mixt_ref, q_ref, qt_ref, k_ref, kt_ref, v_ref, scale_ref,
               dqo_ref, dko_ref, dvo_ref, do_ref, dot_ref, dqt_ref, dk_ref, dv_ref, list_ref):
    nblk = dm_ref.shape[0] // BLK
    heads = q_ref.shape[0]
    km, qm = seg_masks(len_ref, par_ref, len_ref.shape[0], nblk)
    n = jnp.int32(0)
    for j in range(nblk):
        for i in range(j + 1, nblk):
            list_ref[n] = jnp.int32(i * nblk + j)
            n = n + jnp.where((qm[i] & km[j]) != 0, 1, 0)
    dqt_ref[...] = jnp.zeros_like(dqt_ref)
    dk_ref[...] = jnp.zeros_like(dk_ref)
    dv_ref[...] = jnp.zeros_like(dv_ref)
    lax.fori_loop(0, nblk, lambda b, c: (bwd_prep(b, dm_ref, mixt_ref, do_ref, dot_ref), c)[1], 0)
    args = (q_ref, qt_ref, k_ref, kt_ref, v_ref, do_ref, dot_ref, dqt_ref, dk_ref, dv_ref)
    lax.fori_loop(0, nblk, lambda b, c: (bwd_pair(b, b, True, *args), c)[1], 0)
    def one(t, c):
        w = list_ref[t]
        bwd_pair(w // nblk, w % nblk, False, *args)
        return c
    lax.fori_loop(0, n, one, 0)
    lane = lax.broadcasted_iota(jnp.int32, (BLK, 128), 1)
    def finish(b, c):
        rows = pl.ds(pl.multiple_of(b * BLK, BLK), BLK)
        for h in range(heads):
            hl = slice(h * 128, (h + 1) * 128)
            dq = jnp.concatenate([dqt_ref[h, :, rows], jnp.zeros((48, BLK), F32)], axis=0).T
            dqo_ref[rows, hl] = (dq * scale_ref[:, hl]).astype(BF16)
            dko_ref[rows, hl] = jnp.where(lane < HD, dk_ref[h, rows, :], 0.0).astype(BF16)
            dvo_ref[rows, hl] = jnp.where(lane < HD, dv_ref[h, rows, :], 0.0).astype(BF16)
        return c
    lax.fori_loop(0, nblk, finish, 0)


MESH = pl.DeviceIdType.MESH


class Place:
    def __init__(self, ndp):
        self.d, self.t = lax.axis_index("dp"), lax.axis_index("tensor")
        self.line = ndp // 2
        self.p, self.par = self.d // 2, self.d % 2
        self.dx = self.d + 1 - 2 * self.par
        self.c, self.y = self.t % 2, self.t // 2
        self.t1 = self.t + 1 - 2 * self.c
        self.t2 = (self.t + 2) % 4
        self.t3 = (self.t1 + 2) % 4
        self.has_left, self.has_right = self.p > 0, self.p < self.line - 1


def signal(sem, d, t):
    pl.semaphore_signal(sem, inc=1, device_id=(d, t), device_id_type=MESH)


def remote(src, dst, send_sem, recv_sem, d, t):
    return pltpu.make_async_remote_copy(src_ref=src, dst_ref=dst, send_sem=send_sem, recv_sem=recv_sem, device_id=(d, t), device_id_type=MESH)


def greet(me, tensor=(), pair=False, line=False):
    bar = pltpu.get_barrier_semaphore()
    count = len(tensor) + (1 if pair else 0)
    for t in tensor:
        signal(bar, me.d, t)
    if pair:
        signal(bar, me.dx, me.t)
    if line:
        @pl.when(me.has_left)
        def _():
            signal(bar, me.d - 2, me.t)
        @pl.when(me.has_right)
        def _():
            signal(bar, me.d + 2, me.t)
        count = count + jnp.where(me.has_left, 1, 0) + jnp.where(me.has_right, 1, 0)
    pl.semaphore_wait(bar, count)


class PairLine:
    def __init__(self, me, own, buf, send, recv):
        self.me, self.own, self.buf, self.send, self.recv = me, own, buf, send, recv

    def copy(self, o, src, d, kind):
        return remote(src, self.buf.at[o], self.send.at[kind, o], self.recv.at[o], d, self.me.t)

    def start(self):
        me = self.me
        @pl.when(me.has_left)
        def _():
            self.copy(me.d, self.own, me.d - 2, 0).start()
        @pl.when(me.has_right)
        def _():
            self.copy(me.d, self.own, me.d + 2, 1).start()
        self.copy(me.d, self.own, me.dx, 2).start()

    def hop(self, k, then=None):
        me = self.me
        @pl.when(me.p - k >= 0)
        def _():
            o = me.d - 2 * k
            self.copy(o, self.buf.at[o], me.dx, 2).wait_recv()
            @pl.when(me.has_right)
            def _():
                self.copy(o, self.buf.at[o], me.d + 2, 1).start()
            self.copy(o, self.buf.at[o], me.dx, 2).start()
            if then is not None:
                then(o)
        @pl.when(me.p + k < me.line)
        def _():
            o = me.d + 2 * k
            self.copy(o, self.buf.at[o], me.dx, 2).wait_recv()
            @pl.when(me.has_left)
            def _():
                self.copy(o, self.buf.at[o], me.d - 2, 0).start()
            self.copy(o, self.buf.at[o], me.dx, 2).start()
            if then is not None:
                then(o)

    def pair_arrivals(self, then=None):
        def one(q, c):
            o = 2 * q + 1 - self.me.par
            self.copy(o, self.buf.at[o], self.me.dx, 2).wait_recv()
            if then is not None:
                then(o)
            return c
        lax.fori_loop(0, self.me.line, one, 0)

    def sent(self):
        me = self.me
        def one(q, c):
            o = 2 * q + me.par
            self.copy(o, self.buf.at[o], me.dx, 2).wait_send()
            @pl.when((q >= me.p) & me.has_left)
            def _():
                self.copy(o, self.buf.at[o], me.dx, 0).wait_send()
            @pl.when((q <= me.p) & me.has_right)
            def _():
                self.copy(o, self.buf.at[o], me.dx, 1).wait_send()
            return c
        lax.fori_loop(0, me.line, one, 0)


class FullGather:
    def __init__(self, me, own, buf, send, first, recv):
        self.me, self.own, self.buf, self.send, self.first, self.recv = me, own, buf, send, first, recv
        cut = own.shape[0] // 32 * 16
        self.parts = (pl.ds(0, cut), pl.ds(cut, own.shape[0] - cut))

    def copy(self, h, o, t, d2, t2, kind, own=False):
        rows = self.parts[h]
        src = self.own.at[rows] if own else self.buf.at[o, t, rows]
        sem = self.first.at[h] if kind == 4 else self.send.at[h, o, t, kind]
        return remote(src, self.buf.at[o, t, rows], sem, self.recv.at[h, o, t], d2, t2)

    def last(self, h):
        me = self.me
        return (me.d, me.t2) if h == 0 else (me.dx, me.t)

    def spread(self, h, o, t, left, right, own=False):
        me = self.me
        @pl.when(left)
        def _():
            self.copy(h, o, t, me.d - 2, me.t, 0, own).start()
        @pl.when(right)
        def _():
            self.copy(h, o, t, me.d + 2, me.t, 1, own).start()
        self.copy(h, o, t, *self.last(h), 2, own).start()
        self.copy(h, o, t, me.d, me.t1, 3, own).start()

    def start(self):
        me = self.me
        self.copy(0, me.d, me.t, me.dx, me.t, 4, True).start()
        self.copy(1, me.d, me.t, me.d, me.t2, 4, True).start()
        for h in range(2):
            self.spread(h, me.d, me.t, me.has_left, me.has_right, True)

    def arrived(self, h, o, t):
        self.copy(h, o, t, self.me.d, self.me.t1, 3).wait_recv()

    def firsts(self):
        me = self.me
        self.arrived(0, me.dx, me.t)
        self.spread(0, me.dx, me.t, me.has_left, me.has_right)
        self.arrived(1, me.d, me.t2)
        self.spread(1, me.d, me.t2, me.has_left, me.has_right)

    def streams(self, q):
        me = self.me
        return ((0, 2 * q + me.par, me.t), (0, 2 * q + 1 - me.par, me.t), (1, 2 * q + me.par, me.t), (1, 2 * q + me.par, me.t2))

    def hop(self, k):
        me = self.me
        @pl.when(me.p - k >= 0)
        def _():
            for h, o, t in self.streams(me.p - k):
                self.arrived(h, o, t)
                self.spread(h, o, t, False, me.has_right)
        @pl.when(me.p + k < me.line)
        def _():
            for h, o, t in self.streams(me.p + k):
                self.arrived(h, o, t)
                self.spread(h, o, t, me.has_left, False)

    def lasts(self):
        me = self.me
        def one(q, c):
            for h, o, t in ((0, 2 * q, me.t2), (0, 2 * q + 1, me.t2), (1, 2 * q + 1 - me.par, me.t), (1, 2 * q + 1 - me.par, me.t2)):
                self.arrived(h, o, t)
                self.copy(h, o, t, me.d, me.t1, 3).start()
            return c
        lax.fori_loop(0, me.line, one, 0)

    def finish(self):
        me = self.me
        def one(o, c):
            for h in range(2):
                self.arrived(h, o, me.t1)
                self.arrived(h, o, me.t3)
                for t in (me.t, me.t2):
                    self.copy(h, o, t, me.d, me.t1, 3).wait_send()
            return c
        lax.fori_loop(0, 2 * me.line, one, 0)
        def two(q, c):
            for h, o, t in self.streams(q):
                self.copy(h, o, t, me.d, me.t1, 2).wait_send()
                @pl.when((q >= me.p) & me.has_left)
                def _():
                    self.copy(h, o, t, me.d, me.t1, 0).wait_send()
                @pl.when((q <= me.p) & me.has_right)
                def _():
                    self.copy(h, o, t, me.d, me.t1, 1).wait_send()
            return c
        lax.fori_loop(0, me.line, two, 0)
        for h in range(2):
            self.copy(h, me.d, me.t, me.d, me.t1, 4).wait_send()


EPS = 1e-6


def gather_kernel(ndp, chunks, x_ref, gain_ref, choice_ref, a_ref, wo_ref, wf_ref, xo_ref, ao_ref, wout_ref, cho_ref,
                  xn_ref, aown_ref, wown_ref, ls, xs, xr, a_s, a_r, c_s, c_r, w_s, w_f, w_r):
    me = Place(ndp)
    rows_o = wo_ref.shape[0]
    loads = [pltpu.make_async_copy(a_ref, aown_ref, ls.at[0]), pltpu.make_async_copy(wo_ref, wown_ref.at[pl.ds(0, rows_o)], ls.at[1]),
             pltpu.make_async_copy(wf_ref, wown_ref.at[pl.ds(rows_o, wf_ref.shape[0])], ls.at[2])]
    for copy in loads:
        copy.start()
    x = x_ref[...].astype(F32)
    xn_ref[...] = (x * lax.rsqrt(jnp.mean(x * x, axis=-1, keepdims=True) + EPS) * gain_ref[0:1, :]).astype(BF16)
    greet(me, tensor=(me.t1, me.t2), pair=True, line=True)
    size = x_ref.shape[0] // chunks

    def xcopy(o, c, own, t, kind):
        rows = pl.ds(c * size, size)
        return remote(xn_ref.at[rows] if own else xo_ref.at[o, rows], xo_ref.at[o, rows], xs.at[kind, c], xr.at[o, c], me.d, t)

    for c in range(chunks):
        xcopy(me.t, c, True, me.t2, 0).start()
    for c in range(chunks):
        xcopy(me.t, c, True, me.t1, 1).start()
    for copy in loads:
        copy.wait()
    a = PairLine(me, aown_ref, ao_ref, a_s, a_r)
    ch = PairLine(me, choice_ref, cho_ref, c_s, c_r)
    w = FullGather(me, wown_ref, wout_ref, w_s, w_f, w_r)
    a.start()
    ch.start()
    w.start()
    mine = [pltpu.make_async_copy(xn_ref, xo_ref.at[me.t], ls.at[0]), pltpu.make_async_copy(aown_ref, ao_ref.at[me.d], ls.at[1]),
            pltpu.make_async_copy(wown_ref, wout_ref.at[me.d, me.t], ls.at[2]), pltpu.make_async_copy(choice_ref, cho_ref.at[me.d], ls.at[3])]
    for copy in mine:
        copy.start()
    w.firsts()

    def forward(c):
        xcopy(me.t2, c, False, me.t1, 2).wait_recv()
        xcopy(me.t2, c, False, me.t1, 2).start()

    forward(0)

    def hop(k, carry):
        a.hop(k)
        ch.hop(k)
        w.hop(k)
        return carry
    lax.fori_loop(1, me.line, hop, 0)
    for c in range(1, chunks):
        forward(c)
    w.lasts()
    a.pair_arrivals()
    ch.pair_arrivals()
    for c in range(chunks):
        xcopy(me.t1, c, False, me.t1, 2).wait_recv()
        xcopy(me.t3, c, False, me.t1, 2).wait_recv()
    w.finish()
    a.sent()
    ch.sent()
    for c in range(chunks):
        for kind in range(3):
            xcopy(me.t, c, True, me.t1, kind).wait_send()
    for copy in mine:
        copy.wait()


def swap_kernel(ndp, x_ref, o_ref, send, recv, ls):
    me = Place(ndp)
    greet(me, tensor=(me.t1, me.t2, me.t3))
    size = o_ref.shape[1]

    def copy(n, t):
        return remote(x_ref.at[pl.ds(pl.multiple_of(t * size, size), size)], o_ref.at[me.t], send.at[n], recv.at[me.t], me.d, t)

    own = pltpu.make_async_copy(x_ref.at[pl.ds(pl.multiple_of(me.t * size, size), size)], o_ref.at[me.t], ls.at[0])
    for n, t in enumerate((me.t3, me.t2, me.t1)):
        copy(n, t).start()
    own.start()
    for t in (me.t1, me.t2, me.t3):
        remote(o_ref.at[t], o_ref.at[t], send.at[0], recv.at[t], me.d, t).wait_recv()
    for n, t in enumerate((me.t3, me.t2, me.t1)):
        copy(n, t).wait_send()
    own.wait()


def sigmoid(v):
    return 1.0 / (1.0 + jnp.exp(-v))


def mid_kernel(x_ref, g_ref, mix4_ref, gain_ref, w_ref, at_ref, b_ref, out_ref, dmid_ref, dmix_ref, grads_ref,
               mix_ref, mid_ref, hid_ref, up_ref, act_ref, f_ref, low_ref):
    width = x_ref.shape[1]
    step = 256
    part = mix4_ref.shape[2]
    for t in range(mix4_ref.shape[0]):
        mix_ref[:, t * part:(t + 1) * part] = mix4_ref[t]

    def cols(n):
        return pl.ds(pl.multiple_of(n * step, step), step)

    def each(fn):
        lax.fori_loop(0, width // step, lambda n, c: (fn(cols(n)), c)[1], 0)

    gain = gain_ref[1:2, :]
    r_out = dot_nt(mix_ref[...], at_ref[0]).astype(BF16)

    def project_out(n):
        attn = dot_nt(mix_ref[...], w_ref[0, n, :]) + 0.5 * dot(r_out, b_ref[0, :, n])
        mid_ref[:, n] = x_ref[:, n].astype(F32) + attn
    each(project_out)
    middle = mid_ref[...]
    r = lax.rsqrt(jnp.mean(middle * middle, axis=-1, keepdims=True) + EPS)
    hid_ref[...] = (middle * r * gain).astype(BF16)
    r_up = dot_nt(hid_ref[...], at_ref[1]).astype(BF16)

    def up_step(n):
        up = dot(hid_ref[...], w_ref[1, :, n]) + 0.5 * dot(r_up, b_ref[1, :, n])
        up_ref[:, n] = up
        act_ref[:, n] = (up * sigmoid(up)).astype(BF16)
    each(up_step)
    r_down = dot_nt(act_ref[...], at_ref[2]).astype(BF16)

    def down_step(n):
        down = dot_nt(act_ref[...], w_ref[2, n, :]) + 0.5 * dot(r_down, b_ref[2, :, n])
        out_ref[:, n] = (mid_ref[:, n] + down).astype(BF16)
    each(down_step)
    grads_ref[5] = 0.5 * dot_tn(r_down, g_ref[...])
    dz_down = (0.5 * dot_nt(g_ref[...], b_ref[2])).astype(BF16)
    grads_ref[3] = dot_tn(dz_down, act_ref[...])

    def act_back(n):
        d_act = dot(g_ref[...], w_ref[2, :, n]) + dot(dz_down, at_ref[2, :, n])
        up = up_ref[:, n]
        sg = sigmoid(up)
        low_ref[:, n] = (d_act * sg * (1.0 + up * (1.0 - sg))).astype(BF16)
    each(act_back)
    dz_up = (0.5 * dot_nt(low_ref[...], b_ref[1])).astype(BF16)
    grads_ref[1] = 0.5 * dot_tn(r_up, low_ref[...])
    grads_ref[0] = dot_tn(dz_up, hid_ref[...])

    def hidden_back(n):
        f_ref[:, n] = (dot_nt(low_ref[...], w_ref[1, n, :]) + dot(dz_up, at_ref[1, :, n])) * gain_ref[1:2, n]
    each(hidden_back)
    gd = f_ref[...]
    middle = mid_ref[...]
    s = jnp.mean(middle * gd, axis=-1, keepdims=True)
    d_mid = g_ref[...].astype(F32) + r * gd - middle * (r * r * r * s)
    dmid_ref[...] = d_mid
    low_ref[...] = d_mid.astype(BF16)
    dz_out = (0.5 * dot_nt(low_ref[...], b_ref[0])).astype(BF16)
    grads_ref[4] = 0.5 * dot_tn(r_out, low_ref[...])
    grads_ref[2] = dot_tn(dz_out, mix_ref[...])

    def mixed_back(n):
        act_ref[:, n] = (dot(low_ref[...], w_ref[0, :, n]) + dot(dz_out, at_ref[0, :, n])).astype(BF16)
    each(mixed_back)
    for t in range(dmix_ref.shape[0]):
        dmix_ref[t] = act_ref[:, t * part:(t + 1) * part]


def finish_kernel(ndp, chunks, dq_ref, dk_ref, dv_ref, wp_ref, bp_ref, at_ref, xn_ref, rank_ref, x_ref, dmid_ref, gain_ref, gmid_ref,
                  ig_ref, gall_ref,
                  dn_ref, r1_ref, s2_ref, r2_ref, ga_ref, gb_ref, gp_ref, gr_ref, g2_ref, gown_ref,
                  s1s, s1r, s2s, s2r, g1s, g1r, gs, gr, fs, fr, ls):
    me = Place(ndp)
    tok = x_ref.shape[0]
    greet(me, tensor=(me.t1, me.t2), pair=True, line=True)
    ga_ref[...] = jnp.zeros_like(ga_ref)
    gb_ref[...] = jnp.zeros_like(gb_ref)

    def shard(t, slot):
        def half(b, c):
            rows = pl.ds(pl.multiple_of(t * tok + b * BLK, BLK), BLK)
            ds = [ref[rows, :] for ref in (dq_ref, dk_ref, dv_ref)]
            dz = sum(dot_nt(ds[s], bp_ref[s]) for s in range(3)).astype(BF16)
            dn = sum(dot_nt(ds[s], wp_ref[s]) for s in range(3)) + dot(dz, at_ref[...])
            dn_ref[slot, pl.ds(pl.multiple_of(b * BLK, BLK), BLK), :] = dn.astype(BF16)
            ga_ref[...] += dot_tn(dz, xn_ref[rows, :])
            for s in range(3):
                gb_ref[s] += dot_tn(rank_ref[rows, :], ds[s])
            return c
        lax.fori_loop(0, tok // BLK, half, 0)

    def one(slot):
        return remote(dn_ref.at[slot], r1_ref.at[slot], s1s.at[slot], s1r.at[slot], me.d, me.t1)

    shard(me.t3, 0)
    one(0).start()
    shard(me.t2, 2)
    one(0).wait_recv()
    s2_ref[...] = (dn_ref[2].astype(F32) + r1_ref[0].astype(F32)).astype(BF16)
    size = tok // chunks

    def two(c):
        rows = pl.ds(c * size, size)
        return remote(s2_ref.at[rows], r2_ref.at[rows], s2s.at[c], s2r.at[c], me.d, me.t2)

    two(0).start()
    shard(me.t1, 1)
    one(1).start()
    shard(me.t, 3)
    hd = gb_ref.shape[2]
    heads_cols = (hd // 128) * HD
    l = lax.broadcasted_iota(jnp.int32, (hd, at_ref.shape[1]), 0)
    col = lax.broadcasted_iota(jnp.int32, (hd, at_ref.shape[1]), 1)
    put = ((l & 127) < HD) & (me.t * heads_cols + (l >> 7) * HD + (l & 127) == col)
    put = jnp.where(put, 1.0, 0.0).astype(BF16)
    n16 = gb_ref.shape[1] // 3
    n48 = 3 * n16
    gp_ref[0, :n48] = ga_ref[...].astype(BF16)
    for s in range(3):
        gp_ref[0, n48 + s * n16:n48 + (s + 1) * n16] = dot((0.5 * gb_ref[s, s * n16:(s + 1) * n16]).astype(BF16), put).astype(BF16)
    gp_ref[1] = gmid_ref[...].astype(BF16)

    g1 = remote(gp_ref.at[1 - me.c], gr_ref.at[0], g1s.at[0], g1r.at[0], me.d, me.t1)
    g1.start()
    g1.wait_recv()
    g2_ref[...] = (gp_ref[me.c].astype(F32) + gr_ref[0].astype(F32)).astype(BF16)
    g2 = remote(g2_ref, gr_ref.at[1], g1s.at[1], g1r.at[1], me.d, me.t2)
    g2.start()
    for c in range(1, chunks):
        two(c).start()
    g2.wait_recv()
    gown_ref[...] = (g2_ref[...].astype(F32) + gr_ref[1].astype(F32)).astype(BF16)
    g = PairLine(me, gown_ref, gall_ref.at[me.c], gs, gr)
    g.start()

    def relay(o, own=False):
        return remote(gown_ref if own else gall_ref.at[me.c, o], gall_ref.at[me.c, o], fs.at[o], fr.at[o], me.d, me.t1)

    relay(me.d, True).start()
    keep = pltpu.make_async_copy(gown_ref, gall_ref.at[me.c, me.d], ls.at[0])
    keep.start()
    lax.fori_loop(1, me.line, lambda k, c: (g.hop(k, lambda o: relay(o).start()), c)[1], 0)
    g.pair_arrivals(lambda o: relay(o).start())
    one(1).wait_recv()
    for c in range(chunks):
        two(c).wait_recv()
        rows = pl.ds(c * size, size)
        dn = dn_ref[3, rows, :].astype(F32) + r1_ref[1, rows, :].astype(F32) + r2_ref[rows, :].astype(F32)
        x = x_ref[rows, :].astype(F32)
        r = lax.rsqrt(jnp.mean(x * x, axis=-1, keepdims=True) + EPS)
        gd = gain_ref[0:1, :] * dn
        ig_ref[rows, :] = dmid_ref[rows, :] + r * gd - x * (r * r * r * jnp.mean(x * gd, axis=-1, keepdims=True))
    def settle(o, c):
        remote(gown_ref, gall_ref.at[1 - me.c, o], fs.at[o], fr.at[o], me.d, me.t1).wait_recv()
        remote(gown_ref, gall_ref.at[1 - me.c, o], fs.at[o], fr.at[o], me.d, me.t1).wait_send()
        return c
    lax.fori_loop(0, ndp, settle, 0)
    g.sent()
    keep.wait()
    for slot in range(2):
        one(slot).wait_send()
    for c in range(chunks):
        two(c).wait_send()
    g1.wait_send()
    g2.wait_send()


def place_kernel(e_ref, g_ref, ain_ref, bqkv_ref, bup_ref, aout_ref, adown_ref, bres_ref):
    ndp = g_ref.shape[1]
    for ref in (ain_ref, bqkv_ref, bup_ref, aout_ref, adown_ref, bres_ref):
        ref[...] = jnp.zeros_like(ref)

    def add(d, c):
        e = e_ref[d]
        for n in range(3):
            ain_ref[n, e] += g_ref[0, d, n * 16:(n + 1) * 16, :].astype(F32)
            bqkv_ref[n, e] += g_ref[0, d, (3 + n) * 16:(4 + n) * 16, :].astype(F32)
        ain_ref[3, e] += g_ref[1, d, 0:16, :].astype(F32)
        bup_ref[e] += g_ref[1, d, 16:32, :].astype(F32)
        aout_ref[e] += g_ref[1, d, 32:48, :].astype(F32)
        adown_ref[e] += g_ref[1, d, 48:64, :].astype(F32)
        bres_ref[0, e] += g_ref[1, d, 64:80, :].astype(F32)
        bres_ref[1, e] += g_ref[1, d, 80:96, :].astype(F32)
        return c
    lax.fori_loop(0, ndp, add, 0)


VMEM = pltpu.VMEM
DMA = pltpu.SemaphoreType.DMA
IN_VMEM = pl.BlockSpec(memory_space=pltpu.VMEM)
IN_SMEM = pl.BlockSpec(memory_space=pltpu.SMEM)
IN_ANY = pl.BlockSpec(memory_space=pl.ANY)


def shape(*dims, dtype=BF16):
    return jax.ShapeDtypeStruct(dims, dtype)


def params(cid=None, limit=60 << 20):
    if cid is None:
        return pltpu.CompilerParams(vmem_limit_bytes=limit)
    return pltpu.CompilerParams(collective_id=cid, has_side_effects=True, vmem_limit_bytes=limit)


def local(
    inputs, cotangent, adapter_choice_per_tree, segment_lengths, segment_parents, norm_gain_rows, query_dimension_scale,
    attention_weights, output_weight, feedforward_weights, adapter_first_input, adapter_second_attention, adapter_second_up,
    adapter_first_output, adapter_first_down, adapter_second_residual,
):
    ndp, nt = lax.axis_size("dp"), lax.axis_size("tensor")
    tpos = lax.axis_index("tensor")
    tok, width = inputs.shape
    tree = tok * nt
    wrows, hcols = output_weight.shape
    heads = hcols // HD
    pad = heads * 128
    segs = segment_lengths.shape[1]
    rank = adapter_first_input.shape[3]
    nblk = tree // BLK
    e = adapter_choice_per_tree[0]
    lens, parents = segment_lengths[0], segment_parents[0]

    def pick(table, axis):
        return lax.dynamic_index_in_dim(table, e, axis, keepdims=False)

    a_in = pick(jnp.swapaxes(adapter_first_input, 2, 3), 1)
    b_attn = lax.dynamic_slice_in_dim(pick(adapter_second_attention, 1), tpos * hcols, hcols, 2)
    b_res = pick(adapter_second_residual, 1)
    at_qkv = a_in[:3].reshape(3 * rank, width)
    at_mid = jnp.stack([pick(jnp.swapaxes(adapter_first_output, 1, 2), 0), a_in[3], pick(jnp.swapaxes(adapter_first_down, 1, 2), 0)])
    b_mid = jnp.stack([b_res[0], pick(adapter_second_up, 0), b_res[1]])
    ends = jnp.cumsum(lens)
    lane = jnp.arange(128, dtype=jnp.int32) - HD
    spot = (lane[None, :] == jnp.arange(segs, dtype=jnp.int32)[:, None])
    seg = jnp.stack([jnp.sum(jnp.where(spot, (ends - lens)[:, None], 0), 0), jnp.sum(jnp.where(spot, ends[:, None], 0), 0)]
                    + [jnp.zeros((128,), jnp.int32)] * 6).astype(F32)
    idx = jnp.arange(segs, dtype=jnp.int32)
    grand = jnp.sum(jnp.where(parents[:, None] == idx[None, :], parents[None, :], 0), axis=1)
    reach = (idx[:, None] == idx[None, :]) | (parents[:, None] == idx[None, :]) | (grand[:, None] == idx[None, :])
    mq = jnp.pad(jnp.where(reach, 0.0, -BIG).astype(BF16), ((HD, 128 - HD - segs), (HD, 128 - HD - segs)))
    scale = jnp.pad(jnp.broadcast_to(query_dimension_scale[None, :] / math.sqrt(HD), (heads, HD)), ((0, 0), (0, 128 - HD))).reshape(1, pad)

    chunks = 4
    choice = jnp.full((8, 128), e, F32)
    wr = wrows * 3
    xn, wa, wall, choices = pl.pallas_call(
        functools.partial(gather_kernel, ndp, chunks),
        out_shape=[shape(nt, tok, width), shape(ndp, wr, hcols), shape(ndp, nt, wr, hcols), shape(ndp, 8, 128, dtype=F32)],
        in_specs=[IN_VMEM] * 3 + [IN_ANY] * 3, out_specs=[IN_ANY] * 4,
        scratch_shapes=[VMEM((tok, width), BF16), VMEM((wr, hcols), BF16), VMEM((wr, hcols), BF16), DMA((4,)),
                        DMA((3, chunks)), DMA((nt, chunks)), DMA((3, ndp)), DMA((ndp,)), DMA((3, ndp)), DMA((ndp,)),
                        DMA((2, ndp, nt, 4)), DMA((2,)), DMA((2, ndp, nt))],
        compiler_params=params(1), name="gather",
    )(inputs, norm_gain_rows, choice, attention_weights.reshape(wr, hcols), output_weight, feedforward_weights.reshape(2 * wrows, hcols))
    xn = xn.reshape(tree, width)
    wq = wa.reshape(ndp, 3, wrows, hcols).swapaxes(0, 1).reshape(3, width, hcols)
    wmid = wall.reshape(ndp, nt, 3, wrows, hcols).transpose(2, 0, 3, 1, 4).reshape(3, width, nt * hcols)

    q, qt, k, kt, v, ranks, mixt, mix, wp, bp = pl.pallas_call(
        fwd_kernel,
        out_shape=[shape(heads, tree, 128), shape(heads, 128, tree), shape(heads, tree, 128), shape(heads, HD, tree), shape(heads, tree, 128),
                   shape(tree, 3 * rank), shape(hcols, tree), shape(tree, hcols), shape(3, width, pad), shape(3, 3 * rank, pad)],
        in_specs=[IN_VMEM] * 7, out_specs=[IN_VMEM] * 10,
        scratch_shapes=[VMEM((heads, HD + 16, tree), BF16), VMEM((heads, 1, BLK), F32), VMEM((heads, HD + 16, BLK), F32)],
        compiler_params=params(), name="attend",
    )(xn, wq, at_qkv, b_attn, scale, seg, mq)

    def swap(x, cid):
        return pl.pallas_call(
            functools.partial(swap_kernel, ndp), out_shape=shape(nt, tok, hcols), in_specs=[IN_VMEM], out_specs=IN_ANY,
            scratch_shapes=[DMA((3,)), DMA((nt,)), DMA((1,))], compiler_params=params(cid), name="swap",
        )(x)

    mixed = swap(mix, 2)
    output, d_mid, d_mix, g_mid = pl.pallas_call(
        mid_kernel,
        out_shape=[shape(tok, width), shape(tok, width, dtype=F32), shape(nt, tok, hcols), shape(6, rank, width, dtype=F32)],
        in_specs=[IN_VMEM] * 7, out_specs=[IN_VMEM] * 4,
        scratch_shapes=[VMEM((tok, width), BF16), VMEM((tok, width), F32), VMEM((tok, width), BF16), VMEM((tok, width), F32),
                        VMEM((tok, width), BF16), VMEM((tok, width), F32), VMEM((tok, width), BF16)],
        compiler_params=params(), name="middle",
    )(inputs, cotangent, mixed, norm_gain_rows, wmid, at_mid, b_mid)
    d_mixed = swap(d_mix.reshape(nt * tok, hcols), 3).reshape(tree, hcols)

    dq, dk, dv = pl.pallas_call(
        bwd_kernel, out_shape=[shape(tree, pad)] * 3, in_specs=[IN_SMEM] * 2 + [IN_VMEM] * 8, out_specs=[IN_VMEM] * 3,
        scratch_shapes=[VMEM((heads, tree, 128), BF16), VMEM((heads, 128, tree), BF16), VMEM((heads, HD, tree), F32),
                        VMEM((heads, tree, 128), F32), VMEM((heads, tree, 128), F32), pltpu.SMEM((nblk * nblk,), jnp.int32)],
        compiler_params=params(limit=62 << 20), name="attend_back",
    )(lens, parents, d_mixed, mixt, q, qt, k, kt, v, scale)

    gr = 6 * rank
    input_grad, gathered = pl.pallas_call(
        functools.partial(finish_kernel, ndp, chunks),
        out_shape=[shape(tok, width, dtype=F32), shape(2, ndp, gr, width)],
        in_specs=[IN_VMEM] * 12, out_specs=[IN_VMEM, IN_ANY],
        scratch_shapes=[VMEM((4, tok, width), BF16), VMEM((2, tok, width), BF16), VMEM((tok, width), BF16), VMEM((tok, width), BF16),
                        VMEM((3 * rank, width), F32), VMEM((3, 3 * rank, pad), F32), VMEM((2, gr, width), BF16), VMEM((2, gr, width), BF16),
                        VMEM((gr, width), BF16), VMEM((gr, width), BF16),
                        DMA((2,)), DMA((2,)), DMA((chunks,)), DMA((chunks,)), DMA((2,)), DMA((2,)), DMA((3, ndp)), DMA((ndp,)),
                        DMA((ndp,)), DMA((ndp,)), DMA((1,))],
        compiler_params=params(4, 62 << 20), name="finish",
    )(dq, dk, dv, wp, bp, at_qkv, xn, ranks, inputs, d_mid, norm_gain_rows, g_mid.reshape(gr, width))

    count = adapter_first_input.shape[1]
    ga_in, gb_qkv, gb_up, ga_out, ga_down, gb_res = pl.pallas_call(
        place_kernel,
        out_shape=[shape(4, count, rank, width, dtype=F32), shape(3, count, rank, width, dtype=F32), shape(count, rank, width, dtype=F32),
                   shape(count, rank, width, dtype=F32), shape(count, rank, width, dtype=F32), shape(2, count, rank, width, dtype=F32)],
        in_specs=[IN_SMEM, IN_VMEM], out_specs=[IN_VMEM] * 6, compiler_params=params(), name="place",
    )(choices[:, 0, 0].astype(jnp.int32), gathered)
    return (output, input_grad, jnp.swapaxes(ga_in, 2, 3), gb_qkv, gb_up, jnp.swapaxes(ga_out, 1, 2), jnp.swapaxes(ga_down, 1, 2), gb_res)


def solution(mesh):
    tokens, weights = P(("dp", "tensor"), None), P(None, "dp", "tensor")
    in_specs = (tokens, tokens, P("dp"), P("dp", None), P("dp", None), P(), P(), weights, P("dp", "tensor"), weights) + (P(),) * 6
    out_specs = (tokens, tokens) + (P(),) * 6
    return jax.shard_map(local, mesh=mesh, in_specs=in_specs, out_specs=out_specs, check_vma=False)
```

time: 1250 us -> 387 us (0.31)
  waiting for transfers between devices: 576 us -> 0 us
  matrix products: 357 us -> 0 us
  Pallas kernels: 0 us -> 333 us
  other arithmetic: 107 us -> 7.42 us
  local copies, waits for them, and re-layouts: 127 us -> 44.1 us
  blocking collectives: 36.2 us -> 0 us
  loops' own time: 17.7 us -> 0 us
  between operations: 15.8 us -> 1.48 us
    dot_general x77 -> x0, matrix products: 357 us -> none  [the longest x29 106 us: precise_product(): jnp.dot(first_term, second_term, precision=highest_precision, preferred_e...]
    pallas_call x0 -> x8, Pallas kernels: none -> 333 us  [the longest x1 103 us: local(): pl.pallas_call(functools.partial(gather_kernel, ndp, chunks), out_shape=[...]
    all_gather x6 -> x0, waiting for transfers between devices: 217 us -> none  [the longest x1 56.1 us: local(): lax.all_gather(attention_weights, 'dp', axis=1, tiled=True)]
    reduce_scatter x4 -> x0, waiting for transfers between devices: 182 us -> none  [the longest x1 82 us: local(): lax.psum_scatter(attention_piece, 'tensor', scatter_dimension=0, tiled=True)]
    psum x1 -> x0, waiting for transfers between devices: 175 us -> none  [local(): lax.psum((grad_a_in, grad_b_qkv, grad_b_up, grad_a_out, grad_a_down, grad...]
    dynamic_update_slice x12 -> x0, local copies, waits for them, and re-layouts: 59.5 us -> none  [the longest x8 57 us: attend_forward(): mixed_output, log_totals = lax.map(one_block, local_starts)]
    convert_element_type x13 -> x3, other arithmetic: 59.9 us -> 2.93 us  [the longest x1 1.54 us: local(): choices[:, 0, 0].astype(jnp.int32)]
    all_gather x1 -> x0, blocking collectives: 36.2 us -> none  [local(): lax.all_gather(output_weight, 'dp', axis=0, tiled=True)]
  transfers between devices with their start and end apart: 11 -> 0, of which waited for: 10 -> 0; matrix products, arithmetic and copies ran while one was open for 6% -> 0% of each run, Pallas kernels for 0% -> 0%
where the time goes in v1:
time: 387 us; the launch traced here: 386 us
  Pallas kernels  333 us (86%)
  local copies, waits for them, and re-layouts  44.1 us (11%)
  other arithmetic  7.42 us (2%)
    pallas_call x1, Pallas kernels, local(): pl.pallas_call(functools.partial(gather_kernel, ndp, chunks), out_shape=[...  103 us
    pallas_call x1, Pallas kernels, local(): pl.pallas_call(functools.partial(finish_kernel, ndp, chunks), out_shape=[...  62.6 us
    pallas_call x1, Pallas kernels, local(): pl.pallas_call(fwd_kernel, out_shape=[shape(heads, tree, 128), shape(head...  47.2 us
    pallas_call x2, Pallas kernels, swap(): pl.pallas_call(functools.partial(swap_kernel, ndp), out_shape=shape(nt, t...  42.9 us
    pallas_call x1, Pallas kernels, local(): pl.pallas_call(bwd_kernel, out_shape=[shape(tree, pad)] * 3, in_specs=[IN...  38.9 us
    reshape x2, local copies, waits for them, and re-layouts, local(): wall.reshape(ndp, nt, 3, wrows, hcols).transpose(2, 0, 3, 1, 4)  31.4 us
    pallas_call x1, Pallas kernels, local(): pl.pallas_call(mid_kernel, out_shape=[shape(tok, width), shape(tok, width...  31.2 us

profile of v1, /device:TPU:0, one launch (start us, length us, event | category | flops | bytes accessed | tf_op | source)
XLA Modules:
  0.0 385.7 jit_solution(4665777439352275642)
XLA Ops:
  0.6 0.0 copy-start
  1.4 0.8 reduce-window.7
  2.3 0.7 bitcast_subtract_fusion
  2.9 0.9 select_reduce_fusion
  3.8 0.7 broadcast_multiply_fusion
  4.5 0.1 pad.22.clone
  4.6 0.1 pad.21.clone
  4.7 0.1 select_reduce_fusion.2
  4.7 0.6 pad.11
  5.3 0.7 add_convert_fusion.seg_ref
  6.0 0.7 select_convert_fusion
  6.7 0.6 broadcast_in_dim.55.choice_ref
  7.3 0.7 pad.12.mq_ref
  8.0 1.5 dynamic-slice_bitcast_fusion.5.b_ref
  9.5 0.8 constant_dynamic-slice_fusion
  10.3 0.8 dynamic-slice_bitcast_fusion.2
  11.1 0.7 pad_maximum_fusion.1.b_ref
  11.8 0.8 dynamic-slice_bitcast_fusion.3
  12.6 0.0 copy-done
  12.6 0.7 slice.33
  13.3 0.7 pad_maximum_fusion.at_ref
  13.9 103.3 %gather.1 = (bf16[4,512,1280]{2,1,0:T(8,128)(2,1)}, bf16[8,480,320]{2,1,0:T(8,128)(2,1)}, bf16[8,4,480,320]{3,2,1,0:T(8,128)(2,1)}, f32[8,8,128]{2,1,0:T(8,128)}) custom-call(bf16[512,1280]{1,0:T(8,128)(2,1)} %x_ref.5, f32[2,1280]{1,0:T(2,128)} %gain_ref.5, f32[8,128]{1,0:T(8,128)} %broadcast_in_dim.55.choice_ref, bf16[480,320]{1,0:T(8,128)(2,1)} %bitcast.57, ...), custom_call_target="tpu_custom_call" | custom-call | tf_op jit(solution)/shard_map/gather/pallas_call | solution.py:731
  117.3 3.9 %copy.28 = bf16[8,3,160,320]{3,2,0,1:T(8,128)(2,1)} copy(bf16[8,3,160,320]{3,2,1,0:T(8,128)(2,1)} %bitcast.52) | data formatting | bytes 4915200 | tf_op jit(solution)/shard_map/reshape | solution.py:741
  121.1 1.5 convert_reduce_fusion.e_ref
  122.7 12.4 %copy.31 = bf16[8,4,3,160,320]{4,1,3,0,2:T(4,128)(2,1)} copy(bf16[8,4,3,160,320]{4,3,2,1,0:T(8,128)(2,1)} %bitcast.49) | data formatting | bytes 19660800 | tf_op jit(solution)/shard_map/reshape | solution.py:742
  135.1 19.0 %reshape.105.w_ref = bf16[3,1280,1280]{2,1,0:T(8,128)(2,1)} reshape(bf16[3,8,160,4,320]{4,3,2,1,0:T(4,128)(2,1)} %bitcast.46) | data formatting | bytes 19660800 | tf_op jit(solution)/shard_map/reshape | solution.py:742
  154.1 47.2 %attend.1 = (bf16[4,2048,128]{2,1,0:T(8,128)(2,1)}, bf16[4,128,2048]{2,1,0:T(8,128)(2,1)}, bf16[4,2048,128]{2,1,0:T(8,128)(2,1)}, bf16[4,80,2048]{2,1,0:T(8,128)...) custom-call(bf16[2048,1280]{1,0:T(8,128)(2,1)} %bitcast.47, ...), custom_call_target="tpu_custom_call" | custom-call | tf_op jit(solution)/shard_map/attend/pallas_call | solution.py:744
  201.3 21.4 %swap.2.mix4_ref = bf16[4,512,320]{2,1,0:T(8,128)(2,1)} custom-call(bf16[2048,320]{1,0:T(8,128)(2,1)} %get-tuple-element.39.x_ref), custom_call_target="tpu_custom_call" | custom-call | tf_op jit(solution)/shard_map/swap/pallas_call | solution.py:754
  222.8 31.2 %middle.1 = (bf16[512,1280]{1,0:T(8,128)(2,1)}, f32[512,1280]{1,0:T(8,128)}, bf16[4,512,320]{2,1,0:T(8,128)(2,1)}, f32[6,16,1280]{2,1,0:T(8,128)}) custom-call(bf16[512,1280]{1,0:T(8,128)(2,1)} %x_ref.5, bf16[512,1280]{1,0:T(8,128)(2,1)} %g_ref.1, bf16[4,512,320]{2,1,0:T(8,128)(2,1)} %swap.2.mix4_ref, f32[2,1280]{1,0:T(2,128)} %gain_ref.5, ...), custom_call_target="tpu_custom_call" | custom-call | tf_op jit(solution)/shard_map/middle/pallas_call | solution.py:760
  253.9 21.4 %swap.3 = bf16[4,512,320]{2,1,0:T(8,128)(2,1)} custom-call(bf16[2048,320]{1,0:T(8,128)(2,1)} %bitcast.53), custom_call_target="tpu_custom_call" | custom-call | tf_op jit(solution)/shard_map/swap/pallas_call | solution.py:754
  275.4 38.9 %attend_back.1 = (bf16[2048,512]{1,0:T(8,128)(2,1)}, bf16[2048,512]{1,0:T(8,128)(2,1)}, bf16[2048,512]{1,0:T(8,128)(2,1)}) custom-call(s32[13]{0:T(128)} %bitcast.67, s32[13]{0:T(128)} %bitcast.63, bf16[2048,320]{1,0:T(8,128)(2,1)} %bitcast.51, bf16[320,2048]{1,0:T(8,128)(2,1)} %get-tuple-element.43.mixt_ref, bf16[4,2048,128]{2,1,0:T(8,128)(2,1)} %get-tuple-element.44.q_ref, ...), custom_call_target="tpu_custom_call" | custom-call | tf_op jit(solution)/shard_map/attend_back/pallas_call | solution.py:770
  314.3 62.6 %finish.1 = (f32[512,1280]{1,0:T(8,128)}, bf16[2,8,96,1280]{3,2,1,0:T(8,128)(2,1)}) custom-call(bf16[2048,512]{1,0:T(8,128)(2,1)} %get-tuple-element.49.dq_ref, bf16[2048,512]{1,0:T(8,128)(2,1)} %get-tuple-element.50.dk_ref, bf16[2048,512]{1,0:T(8,128)(2,1)} %get-tuple-element.51.dv_ref, bf16[3,1280,512]{2,1,0:T(8,128)(2,1)} %get-tuple-element.52.wp_ref, ...), custom_call_target="tpu_custom_call" | custom-call | tf_op jit(solution)/shard_map/finish/pallas_call | solution.py:778
  376.9 0.0 copy-start.2
  376.9 6.6 %place.1 = (f32[4,8,16,1280]{3,2,1,0:T(8,128)}, f32[3,8,16,1280]{3,2,1,0:T(8,128)}, f32[8,16,1280]{2,1,0:T(8,128)}, f32[8,16,1280]{2,1,0:T(8,128)}, f32[8,16,1280]{2,1,0:T(8,128)}, /*index=5*/f32[2,8,16,1280]{3,2,1,0:T(8,128)}) custom-call(s32[8]{0:T(128)} %convert_reduce_fusion.e_ref, bf16[2,8,96,1280]{3,2,1,0:T(8,128)(2,1)} %get-tuple-element.59.g_ref), custom_call_target="tpu_custom_call" | custom-call | tf_op jit(solution)/shard_map/place/pallas_call | solution.py:791
  383.5 0.0 copy-start.1
  383.5 0.0 copy-done.2
  383.5 1.5 copy.34
  385.0 0.7 copy-done.1
  (6 shorter events, 0.0 us)
Async XLA Ops:
  0.6 11.9 %copy-start = (bf16[4,8,1280,16]{2,3,1,0:T(8,128)(2,1)S(1)}, bf16[4,8,1280,16]{2,3,1,0:T(8,128)(2,1)}, u32[]{:S(2)}) copy-start(bf16[4,8,1280,16]{2,3,1,0:T(8,128)(2,1)} %param.26) | copy-start | bytes 3932164
  376.9 6.6 %copy-start.2 = (f32[512,1280]{1,0:T(8,128)S(1)}, f32[512,1280]{1,0:T(8,128)}, u32[]{:S(2)}) copy-start(f32[512,1280]{1,0:T(8,128)} %get-tuple-element.81) | copy-start | bytes 7864324
  383.5 2.2 copy-start.1

commit v2 on v1

--- a/solution.py
+++ b/solution.py
@@ -104,20 +104,6 @@
     return jnp.where(((l & 127) < HD) & ((l >> 7) * HD + (l & 127) == c), 1.0, 0.0).astype(BF16)
 
 
-def fwd_kernel(x_ref, wq_ref, a_ref, b_ref, scale_ref, seg_ref, mq_ref,
-               q_ref, qt_ref, k_ref, kt_ref, v_ref, rank_ref, mixt_ref, mix_ref, wp_ref, bp_ref,
-               vt_ref, m_ref, acc_ref):
-    sel = spread_heads(wq_ref.shape[2], wp_ref.shape[2])
-    bp_ref[...] = jnp.zeros_like(bp_ref)
-    for s in range(3):
-        wp_ref[s] = dot(wq_ref[s], sel).astype(BF16)
-        n = b_ref.shape[1]
-        bp_ref[s, s * n:(s + 1) * n] = (0.5 * dot(b_ref[s], sel)).astype(BF16)
-    nblk = x_ref.shape[0] // BLK
-    lax.fori_loop(0, nblk, lambda b, c: (project(b, x_ref, wp_ref, a_ref, bp_ref, scale_ref, seg_ref, mq_ref, q_ref, qt_ref, k_ref, kt_ref, v_ref, vt_ref, rank_ref), c)[1], 0)
-    lax.fori_loop(0, nblk, lambda i, c: (attend_block(i, qt_ref, k_ref, vt_ref, m_ref, acc_ref, mixt_ref, mix_ref), c)[1], 0)
-
-
 def bwd_prep(b, dm_ref, mixt_ref, do_ref, dot_ref):
     rows = pl.ds(pl.multiple_of(b * BLK, BLK), BLK)
     heads = do_ref.shape[0]
@@ -392,68 +378,140 @@
 EPS = 1e-6
 
 
-def gather_kernel(ndp, chunks, x_ref, gain_ref, choice_ref, a_ref, wo_ref, wf_ref, xo_ref, ao_ref, wout_ref, cho_ref,
-                  xn_ref, aown_ref, wown_ref, ls, xs, xr, a_s, a_r, c_s, c_r, w_s, w_f, w_r):
+def forward_kernel(ndp, chunks, x_ref, gain_ref, choice_ref, at_ref, b_ref, scale_ref, seg_ref, mq_ref, a_ref, wo_ref, wf_ref,
+                   wout_ref, cho_ref, mixed_ref, xno_ref, qo_ref, qto_ref, ko_ref, kto_ref, vo_ref, ranko_ref, mixto_ref, wpo_ref, bpo_ref,
+                   aown_ref, wown_ref, xn_ref, wa_ref, wp_ref, bp_ref, q_ref, qt_ref, k_ref, kt_ref, v_ref, vt_ref, rank_ref, mixt_ref,
+                   mix_ref, m_ref, acc_ref, ls, os, xs, xr, a_s, a_r, c_s, c_r, w_s, w_f, w_r, ms, mr):
     me = Place(ndp)
+    tok, width = x_ref.shape
     rows_o = wo_ref.shape[0]
     loads = [pltpu.make_async_copy(a_ref, aown_ref, ls.at[0]), pltpu.make_async_copy(wo_ref, wown_ref.at[pl.ds(0, rows_o)], ls.at[1]),
              pltpu.make_async_copy(wf_ref, wown_ref.at[pl.ds(rows_o, wf_ref.shape[0])], ls.at[2])]
     for copy in loads:
         copy.start()
     x = x_ref[...].astype(F32)
-    xn_ref[...] = (x * lax.rsqrt(jnp.mean(x * x, axis=-1, keepdims=True) + EPS) * gain_ref[0:1, :]).astype(BF16)
-    greet(me, tensor=(me.t1, me.t2), pair=True, line=True)
-    size = x_ref.shape[0] // chunks
-
-    def xcopy(o, c, own, t, kind):
-        rows = pl.ds(c * size, size)
-        return remote(xn_ref.at[rows] if own else xo_ref.at[o, rows], xo_ref.at[o, rows], xs.at[kind, c], xr.at[o, c], me.d, t)
+    mine = pl.ds(pl.multiple_of(me.t * tok, tok), tok)
+    xn_ref[mine, :] = (x * lax.rsqrt(jnp.mean(x * x, axis=-1, keepdims=True) + EPS) * gain_ref[0:1, :]).astype(BF16)
+    greet(me, tensor=(me.t1, me.t2, me.t3), pair=True, line=True)
+    size = tok // chunks
+
+    def xcopy(o, c, t, kind):
+        rows = pl.ds(pl.multiple_of(o * tok + c * size, size), size)
+        return remote(xn_ref.at[rows], xn_ref.at[rows], xs.at[kind, c], xr.at[o, c], me.d, t)
 
     for c in range(chunks):
-        xcopy(me.t, c, True, me.t2, 0).start()
+        xcopy(me.t, c, me.t2, 0).start()
     for c in range(chunks):
-        xcopy(me.t, c, True, me.t1, 1).start()
+        xcopy(me.t, c, me.t1, 1).start()
     for copy in loads:
         copy.wait()
-    a = PairLine(me, aown_ref, ao_ref, a_s, a_r)
+    a = PairLine(me, aown_ref, wa_ref, a_s, a_r)
     ch = PairLine(me, choice_ref, cho_ref, c_s, c_r)
     w = FullGather(me, wown_ref, wout_ref, w_s, w_f, w_r)
     a.start()
     ch.start()
-    w.start()
-    mine = [pltpu.make_async_copy(xn_ref, xo_ref.at[me.t], ls.at[0]), pltpu.make_async_copy(aown_ref, ao_ref.at[me.d], ls.at[1]),
-            pltpu.make_async_copy(wown_ref, wout_ref.at[me.d, me.t], ls.at[2]), pltpu.make_async_copy(choice_ref, cho_ref.at[me.d], ls.at[3])]
-    for copy in mine:
+    keep = [pltpu.make_async_copy(wown_ref, wout_ref.at[me.d, me.t], ls.at[0]), pltpu.make_async_copy(choice_ref, cho_ref.at[me.d], ls.at[1])]
+    for copy in keep:
         copy.start()
-    w.firsts()
-
-    def forward(c):
-        xcopy(me.t2, c, False, me.t1, 2).wait_recv()
-        xcopy(me.t2, c, False, me.t1, 2).start()
-
-    forward(0)
+    wa_ref[me.d] = aown_ref[...]
+    early = max(1, me.line - 2)
 
     def hop(k, carry):
         a.hop(k)
         ch.hop(k)
-        w.hop(k)
         return carry
-    lax.fori_loop(1, me.line, hop, 0)
-    for c in range(1, chunks):
+    lax.fori_loop(1, early + 1, hop, 0)
+    w.start()
+
+    def forward(c):
+        xcopy(me.t2, c, me.t1, 2).wait_recv()
+        xcopy(me.t2, c, me.t1, 2).start()
+
+    for c in range(chunks // 2):
         forward(c)
-    w.lasts()
+    lax.fori_loop(early + 1, me.line, hop, 0)
+    for c in range(chunks // 2, chunks):
+        forward(c)
     a.pair_arrivals()
     ch.pair_arrivals()
+
+    sel = spread_heads(wa_ref.shape[2], wp_ref.shape[2])
+    bp_ref[...] = jnp.zeros_like(bp_ref)
+    wrows = wa_ref.shape[1] // 3
+    group = 16 // math.gcd(wrows, 16)
+    for s in range(3):
+        n = b_ref.shape[1]
+        bp_ref[s, s * n:(s + 1) * n] = (0.5 * dot(b_ref[s], sel)).astype(BF16)
+        for o in range(0, ndp, group):
+            wp_ref[s, o * wrows:(o + group) * wrows] = jnp.concatenate(
+                [dot(wa_ref[o + j, s * wrows:(s + 1) * wrows], sel) for j in range(group)], axis=0).astype(BF16)
     for c in range(chunks):
-        xcopy(me.t1, c, False, me.t1, 2).wait_recv()
-        xcopy(me.t3, c, False, me.t1, 2).wait_recv()
+        xcopy(me.t1, c, me.t1, 2).wait_recv()
+        xcopy(me.t3, c, me.t1, 2).wait_recv()
+    w.firsts()
+    nblk = xn_ref.shape[0] // BLK
+    span = 2 * nblk - 3
+
+    def upto(step):
+        return 1 + jnp.minimum(step * (me.line - 1) // span, me.line - 1)
+
+    def relay(step):
+        lax.fori_loop(upto(step), upto(step + 1), lambda k, c: (w.hop(k), c)[1], 0)
+
+    def project_step(b, c):
+        project(b, xn_ref, wp_ref, at_ref, bp_ref, scale_ref, seg_ref, mq_ref, q_ref, qt_ref, k_ref, kt_ref, v_ref, vt_ref, rank_ref)
+        relay(b)
+        return c
+    lax.fori_loop(0, nblk, project_step, 0)
+    outs = [pltpu.make_async_copy(src, dst, os.at[n]) for n, (src, dst) in enumerate((
+        (xn_ref, xno_ref), (q_ref, qo_ref), (k_ref, ko_ref), (kt_ref, kto_ref), (v_ref, vo_ref), (rank_ref, ranko_ref),
+        (wp_ref, wpo_ref), (bp_ref, bpo_ref)))]
+    for copy in outs:
+        copy.start()
+    per = tok // BLK
+
+    def piece(i):
+        rows = pl.ds(pl.multiple_of(i * BLK, BLK), BLK)
+        return mix_ref.at[rows], mixed_ref.at[me.t, pl.ds(pl.multiple_of((i % per) * BLK, BLK), BLK)], i // per
+
+    def attend_step(i, c):
+        attend_block(i, qt_ref, k_ref, vt_ref, m_ref, acc_ref, mixt_ref, mix_ref)
+        src, dst, t = piece(i)
+        @pl.when(t == me.t)
+        def _():
+            pltpu.make_async_copy(src, dst, ms.at[i]).start()
+        @pl.when(t != me.t)
+        def _():
+            remote(src, dst, ms.at[i], mr.at[me.t, i % per], me.d, t).start()
+        relay(nblk + i)
+        return c
+    lax.fori_loop(0, nblk, attend_step, 0)
+    late = [pltpu.make_async_copy(qt_ref, qto_ref, os.at[len(outs)]), pltpu.make_async_copy(mixt_ref, mixto_ref, os.at[len(outs) + 1])]
+    for copy in late:
+        copy.start()
+    w.lasts()
+    for t in (me.t1, me.t2, me.t3):
+        for h in range(per):
+            dst = mixed_ref.at[t, pl.ds(h * BLK, BLK)]
+            remote(dst, dst, ms.at[0], mr.at[t, h], me.d, t).wait_recv()
     w.finish()
     a.sent()
     ch.sent()
     for c in range(chunks):
         for kind in range(3):
-            xcopy(me.t, c, True, me.t1, kind).wait_send()
-    for copy in mine:
+            xcopy(me.t, c, me.t1, kind).wait_send()
+
+    def settle(i, c):
+        src, dst, t = piece(i)
+        @pl.when(t == me.t)
+        def _():
+            pltpu.make_async_copy(src, dst, ms.at[i]).wait()
+        @pl.when(t != me.t)
+        def _():
+            remote(src, dst, ms.at[i], mr.at[me.t, i % per], me.d, t).wait_send()
+        return c
+    lax.fori_loop(0, nblk, settle, 0)
+    for copy in keep + outs + late:
         copy.wait()
 
 
@@ -480,11 +538,23 @@
     return 1.0 / (1.0 + jnp.exp(-v))
 
 
-def mid_kernel(x_ref, g_ref, mix4_ref, gain_ref, w_ref, at_ref, b_ref, out_ref, dmid_ref, dmix_ref, grads_ref,
-               mix_ref, mid_ref, hid_ref, up_ref, act_ref, f_ref, low_ref):
+def mid_kernel(x_ref, g_ref, mix4_ref, gain_ref, at_ref, b_ref, wall_ref, out_ref, dmid_ref, dmix_ref, grads_ref,
+               mix_ref, mid_ref, hid_ref, up_ref, act_ref, f_ref, low_ref, w_ref, wb0_ref, wb1_ref, wb2_ref, ls):
     width = x_ref.shape[1]
     step = 256
     part = mix4_ref.shape[2]
+    blocks = (wb0_ref, wb1_ref, wb2_ref)
+    ndp, nt, wrows = wb0_ref.shape[:3]
+    loads = [pltpu.make_async_copy(wall_ref.at[:, :, pl.ds(n * wrows, wrows)], blocks[n], ls.at[n]) for n in range(3)]
+    for copy in loads:
+        copy.start()
+
+    def assemble(n):
+        loads[n].wait()
+        for o in range(ndp):
+            for t in range(nt):
+                w_ref[n, o * wrows:(o + 1) * wrows, t * part:(t + 1) * part] = blocks[n][o, t]
+
     for t in range(mix4_ref.shape[0]):
         mix_ref[:, t * part:(t + 1) * part] = mix4_ref[t]
 
@@ -496,6 +566,7 @@
 
     gain = gain_ref[1:2, :]
     r_out = dot_nt(mix_ref[...], at_ref[0]).astype(BF16)
+    assemble(0)
 
     def project_out(n):
         attn = dot_nt(mix_ref[...], w_ref[0, n, :]) + 0.5 * dot(r_out, b_ref[0, :, n])
@@ -505,6 +576,7 @@
     r = lax.rsqrt(jnp.mean(middle * middle, axis=-1, keepdims=True) + EPS)
     hid_ref[...] = (middle * r * gain).astype(BF16)
     r_up = dot_nt(hid_ref[...], at_ref[1]).astype(BF16)
+    assemble(1)
 
     def up_step(n):
         up = dot(hid_ref[...], w_ref[1, :, n]) + 0.5 * dot(r_up, b_ref[1, :, n])
@@ -512,6 +584,7 @@
         act_ref[:, n] = (up * sigmoid(up)).astype(BF16)
     each(up_step)
     r_down = dot_nt(act_ref[...], at_ref[2]).astype(BF16)
+    assemble(2)
 
     def down_step(n):
         down = dot_nt(act_ref[...], w_ref[2, n, :]) + 0.5 * dot(r_down, b_ref[2, :, n])
@@ -728,27 +801,23 @@
     chunks = 4
     choice = jnp.full((8, 128), e, F32)
     wr = wrows * 3
-    xn, wa, wall, choices = pl.pallas_call(
-        functools.partial(gather_kernel, ndp, chunks),
-        out_shape=[shape(nt, tok, width), shape(ndp, wr, hcols), shape(ndp, nt, wr, hcols), shape(ndp, 8, 128, dtype=F32)],
-        in_specs=[IN_VMEM] * 3 + [IN_ANY] * 3, out_specs=[IN_ANY] * 4,
-        scratch_shapes=[VMEM((tok, width), BF16), VMEM((wr, hcols), BF16), VMEM((wr, hcols), BF16), DMA((4,)),
+    tall = (heads, tree, 128)
+    wall, choices, mixed, xn, q, qt, k, kt, v, ranks, mixt, wp, bp = pl.pallas_call(
+        functools.partial(forward_kernel, ndp, chunks),
+        out_shape=[shape(ndp, nt, wr, hcols), shape(ndp, 8, 128, dtype=F32), shape(nt, tok, hcols), shape(tree, width),
+                   shape(*tall), shape(heads, 128, tree), shape(*tall), shape(heads, HD, tree), shape(*tall),
+                   shape(tree, 3 * rank), shape(hcols, tree), shape(3, width, pad), shape(3, 3 * rank, pad)],
+        in_specs=[IN_VMEM] * 8 + [IN_ANY] * 3, out_specs=[IN_ANY] * 13,
+        scratch_shapes=[VMEM((wr, hcols), BF16), VMEM((wr, hcols), BF16), VMEM((tree, width), BF16), VMEM((ndp, wr, hcols), BF16),
+                        VMEM((3, width, pad), BF16), VMEM((3, 3 * rank, pad), BF16), VMEM(tall, BF16), VMEM((heads, 128, tree), BF16),
+                        VMEM(tall, BF16), VMEM((heads, HD, tree), BF16), VMEM(tall, BF16), VMEM((heads, HD + 16, tree), BF16),
+                        VMEM((tree, 3 * rank), BF16), VMEM((hcols, tree), BF16), VMEM((tree, hcols), BF16),
+                        VMEM((heads, 1, BLK), F32), VMEM((heads, HD + 16, BLK), F32), DMA((3,)), DMA((10,)),
                         DMA((3, chunks)), DMA((nt, chunks)), DMA((3, ndp)), DMA((ndp,)), DMA((3, ndp)), DMA((ndp,)),
-                        DMA((2, ndp, nt, 4)), DMA((2,)), DMA((2, ndp, nt))],
-        compiler_params=params(1), name="gather",
-    )(inputs, norm_gain_rows, choice, attention_weights.reshape(wr, hcols), output_weight, feedforward_weights.reshape(2 * wrows, hcols))
-    xn = xn.reshape(tree, width)
-    wq = wa.reshape(ndp, 3, wrows, hcols).swapaxes(0, 1).reshape(3, width, hcols)
-    wmid = wall.reshape(ndp, nt, 3, wrows, hcols).transpose(2, 0, 3, 1, 4).reshape(3, width, nt * hcols)
-
-    q, qt, k, kt, v, ranks, mixt, mix, wp, bp = pl.pallas_call(
-        fwd_kernel,
-        out_shape=[shape(heads, tree, 128), shape(heads, 128, tree), shape(heads, tree, 128), shape(heads, HD, tree), shape(heads, tree, 128),
-                   shape(tree, 3 * rank), shape(hcols, tree), shape(tree, hcols), shape(3, width, pad), shape(3, 3 * rank, pad)],
-        in_specs=[IN_VMEM] * 7, out_specs=[IN_VMEM] * 10,
-        scratch_shapes=[VMEM((heads, HD + 16, tree), BF16), VMEM((heads, 1, BLK), F32), VMEM((heads, HD + 16, BLK), F32)],
-        compiler_params=params(), name="attend",
-    )(xn, wq, at_qkv, b_attn, scale, seg, mq)
+                        DMA((2, ndp, nt, 4)), DMA((2,)), DMA((2, ndp, nt)), DMA((nblk,)), DMA((nt, tok // BLK))],
+        compiler_params=params(1), name="forward",
+    )(inputs, norm_gain_rows, choice, at_qkv, b_attn, scale, seg, mq, attention_weights.reshape(wr, hcols), output_weight,
+      feedforward_weights.reshape(2 * wrows, hcols))
 
     def swap(x, cid):
         return pl.pallas_call(
@@ -756,15 +825,15 @@
             scratch_shapes=[DMA((3,)), DMA((nt,)), DMA((1,))], compiler_params=params(cid), name="swap",
         )(x)
 
-    mixed = swap(mix, 2)
     output, d_mid, d_mix, g_mid = pl.pallas_call(
         mid_kernel,
         out_shape=[shape(tok, width), shape(tok, width, dtype=F32), shape(nt, tok, hcols), shape(6, rank, width, dtype=F32)],
-        in_specs=[IN_VMEM] * 7, out_specs=[IN_VMEM] * 4,
+        in_specs=[IN_VMEM] * 6 + [IN_ANY], out_specs=[IN_VMEM] * 4,
         scratch_shapes=[VMEM((tok, width), BF16), VMEM((tok, width), F32), VMEM((tok, width), BF16), VMEM((tok, width), F32),
-                        VMEM((tok, width), BF16), VMEM((tok, width), F32), VMEM((tok, width), BF16)],
+                        VMEM((tok, width), BF16), VMEM((tok, width), F32), VMEM((tok, width), BF16), VMEM((3, width, width), BF16)]
+        + [VMEM((ndp, nt, wrows, hcols), BF16)] * 3 + [DMA((3,))],
         compiler_params=params(), name="middle",
-    )(inputs, cotangent, mixed, norm_gain_rows, wmid, at_mid, b_mid)
+    )(inputs, cotangent, mixed, norm_gain_rows, at_mid, b_mid, wall)
     d_mixed = swap(d_mix.reshape(nt * tok, hcols), 3).reshape(tree, hcols)
 
     dq, dk, dv = pl.pallas_call(

time: 387 us -> 292 us (0.75)
  Pallas kernels: 333 us -> 273 us
  local copies, waits for them, and re-layouts: 44.1 us -> 8.86 us
    pallas_call x2 -> x1, Pallas kernels: 151 us -> 115 us  [local(): pl.pallas_call(functools.partial(forward_kernel, ndp, chunks), out_shape=...]
    reshape x3 -> x0, local copies, waits for them, and re-layouts: 35.3 us -> none  [the longest x2 31.4 us: local(): wall.reshape(ndp, nt, 3, wrows, hcols).transpose(2, 0, 3, 1, 4)]
    pallas_call x2 -> x1, Pallas kernels: 42.9 us -> 21.5 us  [swap(): pl.pallas_call(functools.partial(swap_kernel, ndp), out_shape=shape(nt, t...]
where the time goes in v2:
time: 292 us; the launch traced here: 291 us
  Pallas kernels  273 us (93%)
  local copies, waits for them, and re-layouts  8.86 us (3%)
  other arithmetic  7.54 us (3%)
    pallas_call x1, Pallas kernels, local(): pl.pallas_call(functools.partial(forward_kernel, ndp, chunks), out_shape=...  115 us
    pallas_call x1, Pallas kernels, local(): pl.pallas_call(functools.partial(finish_kernel, ndp, chunks), out_shape=[...  62 us
    pallas_call x1, Pallas kernels, local(): pl.pallas_call(bwd_kernel, out_shape=[shape(tree, pad)] * 3, in_specs=[IN...  36.6 us
    pallas_call x1, Pallas kernels, local(): pl.pallas_call(mid_kernel, out_shape=[shape(tok, width), shape(tok, width...  32.1 us
    pallas_call x1, Pallas kernels, swap(): pl.pallas_call(functools.partial(swap_kernel, ndp), out_shape=shape(nt, t...  21.5 us
    pallas_call x1, Pallas kernels, local(): pl.pallas_call(place_kernel, out_shape=[shape(4, count, rank, width, dtyp...  6.47 us

profile of v2, /device:TPU:0, one launch (start us, length us, event | category | flops | bytes accessed | tf_op | source)
XLA Modules:
  0.0 291.2 jit_solution(13559576620408851459)
XLA Ops:
  0.6 0.0 copy-start
  1.4 0.8 reduce-window.7
  2.3 0.7 bitcast_subtract_fusion
  2.9 0.9 select_reduce_fusion
  3.8 0.7 broadcast_multiply_fusion
  4.5 0.1 pad.22.clone
  4.6 0.1 pad.21.clone
  4.7 0.1 select_reduce_fusion.2
  4.7 0.6 pad.11
  5.3 0.7 add_convert_fusion.seg_ref
  6.0 0.7 select_convert_fusion
  6.7 0.6 broadcast_in_dim.55.choice_ref
  7.3 0.7 pad.12.mq_ref
  8.0 1.5 dynamic-slice_bitcast_fusion.5.b_ref
  9.5 0.8 constant_dynamic-slice_fusion
  10.3 0.8 dynamic-slice_bitcast_fusion.2
  11.1 0.7 pad_maximum_fusion.1.b_ref
  11.8 0.8 dynamic-slice_bitcast_fusion.3
  12.6 0.0 copy-done
  12.6 0.7 slice.33
  13.3 0.7 pad_maximum_fusion.at_ref
  13.9 114.7 %forward.1 = (bf16[8,4,480,320]{3,2,1,0:T(8,128)(2,1)}, f32[8,8,128]{2,1,0:T(8,128)}, bf16[4,512,320]{2,1,0:T(8,128)(2,1)}, bf16[2048,1280]{1,0:T(8,128)(2,1)}, ...) custom-call(bf16[512,1280]{1,0:T(8,128)(2,1)} %x_ref.5, ...), custom_call_target="tpu_custom_call" | custom-call | tf_op jit(solution)/shard_map/forward/pallas_call | solution.py:805
  128.6 32.1 %middle.1 = (bf16[512,1280]{1,0:T(8,128)(2,1)}, f32[512,1280]{1,0:T(8,128)}, bf16[4,512,320]{2,1,0:T(8,128)(2,1)}, f32[6,16,1280]{2,1,0:T(8,128)}) custom-call(bf16[512,1280]{1,0:T(8,128)(2,1)} %x_ref.5, bf16[512,1280]{1,0:T(8,128)(2,1)} %g_ref.1, bf16[4,512,320]{2,1,0:T(8,128)(2,1)} %get-tuple-element.36.mix4_ref, f32[2,1280]{1,0:T(2,128)} %gain_ref.5, ...), custom_call_target="tpu_custom_call" | custom-call | tf_op jit(solution)/shard_map/middle/pallas_call | solution.py:828
  160.8 21.5 %swap.1 = bf16[4,512,320]{2,1,0:T(8,128)(2,1)} custom-call(bf16[2048,320]{1,0:T(8,128)(2,1)} %bitcast.38), custom_call_target="tpu_custom_call" | custom-call | tf_op jit(solution)/shard_map/swap/pallas_call | solution.py:823
  182.2 36.6 %attend_back.1 = (bf16[2048,512]{1,0:T(8,128)(2,1)}, bf16[2048,512]{1,0:T(8,128)(2,1)}, bf16[2048,512]{1,0:T(8,128)(2,1)}) custom-call(s32[13]{0:T(128)} %bitcast.52, s32[13]{0:T(128)} %bitcast.48, bf16[2048,320]{1,0:T(8,128)(2,1)} %bitcast.37, bf16[320,2048]{1,0:T(8,128)(2,1)} %get-tuple-element.40.mixt_ref, bf16[4,2048,128]{2,1,0:T(8,128)(2,1)} %get-tuple-element.41.q_ref, ...), custom_call_target="tpu_custom_call" | custom-call | tf_op jit(solution)/shard_map/attend_back/pallas_call | solution.py:839
  218.8 62.0 %finish.1 = (f32[512,1280]{1,0:T(8,128)}, bf16[2,8,96,1280]{3,2,1,0:T(8,128)(2,1)}) custom-call(bf16[2048,512]{1,0:T(8,128)(2,1)} %get-tuple-element.46.dq_ref, bf16[2048,512]{1,0:T(8,128)(2,1)} %get-tuple-element.47.dk_ref, bf16[2048,512]{1,0:T(8,128)(2,1)} %get-tuple-element.48.dv_ref, bf16[3,1280,512]{2,1,0:T(8,128)(2,1)} %get-tuple-element.49.wp_ref, ...), custom_call_target="tpu_custom_call" | custom-call | tf_op jit(solution)/shard_map/finish/pallas_call | solution.py:847
  280.8 0.0 copy-start.2
  280.8 1.7 convert_reduce_fusion.e_ref
  282.5 6.5 %place.1 = (f32[4,8,16,1280]{3,2,1,0:T(8,128)}, f32[3,8,16,1280]{3,2,1,0:T(8,128)}, f32[8,16,1280]{2,1,0:T(8,128)}, f32[8,16,1280]{2,1,0:T(8,128)}, f32[8,16,1280]{2,1,0:T(8,128)}, /*index=5*/f32[2,8,16,1280]{3,2,1,0:T(8,128)}) custom-call(s32[8]{0:T(128)} %convert_reduce_fusion.e_ref, bf16[2,8,96,1280]{3,2,1,0:T(8,128)(2,1)} %get-tuple-element.57.g_ref), custom_call_target="tpu_custom_call" | custom-call | tf_op jit(solution)/shard_map/place/pallas_call | solution.py:860
  289.0 0.0 copy-start.1
  289.0 0.0 copy-done.2
  289.0 1.5 copy.26
  290.4 0.7 copy-done.1
  (6 shorter events, 0.0 us)
Async XLA Ops:
  0.6 11.9 %copy-start = (bf16[4,8,1280,16]{2,3,1,0:T(8,128)(2,1)S(1)}, bf16[4,8,1280,16]{2,3,1,0:T(8,128)(2,1)}, u32[]{:S(2)}) copy-start(bf16[4,8,1280,16]{2,3,1,0:T(8,128)(2,1)} %param.26) | copy-start | bytes 3932164
  280.8 8.1 %copy-start.2 = (f32[512,1280]{1,0:T(8,128)S(1)}, f32[512,1280]{1,0:T(8,128)}, u32[]{:S(2)}) copy-start(f32[512,1280]{1,0:T(8,128)} %get-tuple-element.79) | copy-start | bytes 7864324
  289.0 2.2 copy-start.1

commit v3 on v2

--- a/solution.py
+++ b/solution.py
@@ -85,19 +85,6 @@
     mixt_ref[:, cols] = ot.astype(BF16)
     mix_ref[cols, :] = ot.T.astype(BF16)
 
-def seg_masks(len_ref, par_ref, segs, nblk):
-    start, km, qm = 0, [0] * nblk, [0] * nblk
-    for u in range(segs):
-        end = start + len_ref[u]
-        up = par_ref[u]
-        anc = jnp.int32(1 << u) | (jnp.int32(1) << up) | (jnp.int32(1) << par_ref[up])
-        for b in range(nblk):
-            inside = (start < (b + 1) * BLK) & (end > b * BLK)
-            km[b] = km[b] | jnp.where(inside, jnp.int32(1 << u), 0)
-            qm[b] = qm[b] | jnp.where(inside, anc, 0)
-        start = end
-    return km, qm
-
 def spread_heads(hcols, pad):
     c = lax.broadcasted_iota(jnp.int32, (hcols, pad), 0)
     l = lax.broadcasted_iota(jnp.int32, (hcols, pad), 1)
@@ -139,40 +126,6 @@
         dv_ref[h, rows, :] += dvs[h]
         dk_ref[h, rows, :] += dks[h]
         dqt_ref[h, :, cols] += dqs[h]
-
-def bwd_kernel(len_ref, par_ref, dm_ref, mixt_ref, q_ref, qt_ref, k_ref, kt_ref, v_ref, scale_ref,
-               dqo_ref, dko_ref, dvo_ref, do_ref, dot_ref, dqt_ref, dk_ref, dv_ref, list_ref):
-    nblk = dm_ref.shape[0] // BLK
-    heads = q_ref.shape[0]
-    km, qm = seg_masks(len_ref, par_ref, len_ref.shape[0], nblk)
-    n = jnp.int32(0)
-    for j in range(nblk):
-        for i in range(j + 1, nblk):
-            list_ref[n] = jnp.int32(i * nblk + j)
-            n = n + jnp.where((qm[i] & km[j]) != 0, 1, 0)
-    dqt_ref[...] = jnp.zeros_like(dqt_ref)
-    dk_ref[...] = jnp.zeros_like(dk_ref)
-    dv_ref[...] = jnp.zeros_like(dv_ref)
-    lax.fori_loop(0, nblk, lambda b, c: (bwd_prep(b, dm_ref, mixt_ref, do_ref, dot_ref), c)[1], 0)
-    args = (q_ref, qt_ref, k_ref, kt_ref, v_ref, do_ref, dot_ref, dqt_ref, dk_ref, dv_ref)
-    lax.fori_loop(0, nblk, lambda b, c: (bwd_pair(b, b, True, *args), c)[1], 0)
-    def one(t, c):
-        w = list_ref[t]
-        bwd_pair(w // nblk, w % nblk, False, *args)
-        return c
-    lax.fori_loop(0, n, one, 0)
-    lane = lax.broadcasted_iota(jnp.int32, (BLK, 128), 1)
-    def finish(b, c):
-        rows = pl.ds(pl.multiple_of(b * BLK, BLK), BLK)
-        for h in range(heads):
-            hl = slice(h * 128, (h + 1) * 128)
-            dq = jnp.concatenate([dqt_ref[h, :, rows], jnp.zeros((48, BLK), F32)], axis=0).T
-            dqo_ref[rows, hl] = (dq * scale_ref[:, hl]).astype(BF16)
-            dko_ref[rows, hl] = jnp.where(lane < HD, dk_ref[h, rows, :], 0.0).astype(BF16)
-            dvo_ref[rows, hl] = jnp.where(lane < HD, dv_ref[h, rows, :], 0.0).astype(BF16)
-        return c
-    lax.fori_loop(0, nblk, finish, 0)
-
 
 MESH = pl.DeviceIdType.MESH
 
@@ -515,25 +468,6 @@
         copy.wait()
 
 
-def swap_kernel(ndp, x_ref, o_ref, send, recv, ls):
-    me = Place(ndp)
-    greet(me, tensor=(me.t1, me.t2, me.t3))
-    size = o_ref.shape[1]
-
-    def copy(n, t):
-        return remote(x_ref.at[pl.ds(pl.multiple_of(t * size, size), size)], o_ref.at[me.t], send.at[n], recv.at[me.t], me.d, t)
-
-    own = pltpu.make_async_copy(x_ref.at[pl.ds(pl.multiple_of(me.t * size, size), size)], o_ref.at[me.t], ls.at[0])
-    for n, t in enumerate((me.t3, me.t2, me.t1)):
-        copy(n, t).start()
-    own.start()
-    for t in (me.t1, me.t2, me.t3):
-        remote(o_ref.at[t], o_ref.at[t], send.at[0], recv.at[t], me.d, t).wait_recv()
-    for n, t in enumerate((me.t3, me.t2, me.t1)):
-        copy(n, t).wait_send()
-    own.wait()
-
-
 def sigmoid(v):
     return 1.0 / (1.0 + jnp.exp(-v))
 
@@ -624,123 +558,260 @@
         dmix_ref[t] = act_ref[:, t * part:(t + 1) * part]
 
 
-def finish_kernel(ndp, chunks, dq_ref, dk_ref, dv_ref, wp_ref, bp_ref, at_ref, xn_ref, rank_ref, x_ref, dmid_ref, gain_ref, gmid_ref,
-                  ig_ref, gall_ref,
-                  dn_ref, r1_ref, s2_ref, r2_ref, ga_ref, gb_ref, gp_ref, gr_ref, g2_ref, gown_ref,
-                  s1s, s1r, s2s, s2r, g1s, g1r, gs, gr, fs, fr, ls):
+class GradSum:
+    def __init__(self, me, gp, gr, g2, own, out, s, r, ls_, lr, fs, fr, keep):
+        self.me, self.gp, self.gr, self.g2, self.own, self.out, self.s, self.r, self.fs, self.fr = me, gp, gr, g2, own, out, s, r, fs, fr
+        self.line = PairLine(me, own, out.at[me.c], ls_, lr)
+        self.keep = pltpu.make_async_copy(own, out.at[me.c, me.d], keep)
+
+    def one(self):
+        return remote(self.gp.at[1 - self.me.c], self.gr.at[0], self.s.at[0], self.r.at[0], self.me.d, self.me.t1)
+
+    def two(self):
+        return remote(self.g2, self.gr.at[1], self.s.at[1], self.r.at[1], self.me.d, self.me.t2)
+
+    def second(self):
+        self.one().wait_recv()
+        self.g2[...] = (self.gp[self.me.c].astype(F32) + self.gr[0].astype(F32)).astype(BF16)
+        self.two().start()
+
+    def relay(self, o, own=False):
+        src = self.own if own else self.out.at[self.me.c, o]
+        return remote(src, self.out.at[self.me.c, o], self.fs.at[o], self.fr.at[o], self.me.d, self.me.t1)
+
+    def gather(self):
+        self.two().wait_recv()
+        self.own[...] = (self.g2[...].astype(F32) + self.gr[1].astype(F32)).astype(BF16)
+        self.line.start()
+        self.relay(self.me.d, True).start()
+        self.keep.start()
+
+    def hop(self, k):
+        self.line.hop(k, lambda o: self.relay(o).start())
+
+    def arrivals(self):
+        self.line.pair_arrivals(lambda o: self.relay(o).start())
+
+    def settle(self, ndp):
+        def one(o, c):
+            self.relay(o, True).wait_send()
+            remote(self.own, self.out.at[1 - self.me.c, o], self.fs.at[o], self.fr.at[o], self.me.d, self.me.t1).wait_recv()
+            return c
+        lax.fori_loop(0, ndp, one, 0)
+        self.line.sent()
+        self.keep.wait()
+        self.one().wait_send()
+        self.two().wait_send()
+
+
+def back_kernel(ndp, dmix_ref, mixt_h, q_h, qt_h, k_h, kt_h, v_h, wp_h, xn_h, rank_h, x_h, dmid_h, scale_ref, bp_ref, at_ref, gain_ref, gmid_ref,
+                ig_h, gm_h, ga_h,
+                mixt_ref, q_ref, qt_ref, k_ref, kt_ref, v_ref, wp_ref, xn_ref, rank_ref, x_ref, dmid_ref, dm_ref, do_ref, dot_ref,
+                dqt_ref, dk_ref, dv_ref, dn_ref, r1_ref, s2_ref, r2_ref, ro_ref, ga_ref, gb_ref, put_ref,
+                gpm, grm, g2m, gom, gpa, gra, g2a, goa, lsem, dsem, drecv, es, er, s2s, r2r, ros, ror, igs,
+                ms, mr, mls, mlr, mfs, mfr, mk, as_, ar, als, alr, afs, afr, ak):
     me = Place(ndp)
     tok = x_ref.shape[0]
-    greet(me, tensor=(me.t1, me.t2), pair=True, line=True)
-    ga_ref[...] = jnp.zeros_like(ga_ref)
-    gb_ref[...] = jnp.zeros_like(gb_ref)
-
-    def shard(t, slot):
-        def half(b, c):
-            rows = pl.ds(pl.multiple_of(t * tok + b * BLK, BLK), BLK)
-            ds = [ref[rows, :] for ref in (dq_ref, dk_ref, dv_ref)]
-            dz = sum(dot_nt(ds[s], bp_ref[s]) for s in range(3)).astype(BF16)
-            dn = sum(dot_nt(ds[s], wp_ref[s]) for s in range(3)) + dot(dz, at_ref[...])
-            dn_ref[slot, pl.ds(pl.multiple_of(b * BLK, BLK), BLK), :] = dn.astype(BF16)
-            ga_ref[...] += dot_tn(dz, xn_ref[rows, :])
-            for s in range(3):
-                gb_ref[s] += dot_tn(rank_ref[rows, :], ds[s])
+    nblk = dm_ref.shape[0] // BLK
+    per, half, hb = tok // BLK, nblk // 2, BLK // 2
+    heads = q_ref.shape[0]
+    loads = [pltpu.make_async_copy(src, dst, lsem.at[n]) for n, (src, dst) in enumerate((
+        (mixt_h, mixt_ref), (q_h, q_ref), (qt_h, qt_ref), (k_h, k_ref), (kt_h, kt_ref), (v_h, v_ref),
+        (wp_h, wp_ref), (xn_h, xn_ref), (rank_h, rank_ref), (x_h, x_ref), (dmid_h, dmid_ref)))]
+    n48 = gpm.shape[1]
+    for c in range(2):
+        gpm[c] = gmid_ref[c * n48:(c + 1) * n48].astype(BF16)
+    greet(me, tensor=(me.t1, me.t2, me.t3), pair=True, line=True)
+
+    def token_rows(t):
+        return pl.ds(pl.multiple_of(t * tok, tok), tok)
+
+    def swap(n, t):
+        return remote(dmix_ref.at[t], dm_ref.at[token_rows(me.t)], dsem.at[n], drecv.at[me.t], me.d, t)
+
+    own = pltpu.make_async_copy(dmix_ref.at[me.t], dm_ref.at[token_rows(me.t)], dsem.at[3])
+    for n, t in enumerate((me.t3, me.t2, me.t1)):
+        swap(n, t).start()
+    own.start()
+    gm = GradSum(me, gpm, grm, g2m, gom, gm_h, ms, mr, mls, mlr, mfs, mfr, mk.at[0])
+    ga = GradSum(me, gpa, gra, g2a, goa, ga_h, as_, ar, als, alr, afs, afr, ak.at[0])
+    gm.one().start()
+    for copy in loads:
+        copy.start()
+    for ref in (dqt_ref, dk_ref, dv_ref, ga_ref, gb_ref):
+        ref[...] = jnp.zeros_like(ref)
+    hd = gb_ref.shape[2]
+    l = lax.broadcasted_iota(jnp.int32, put_ref.shape, 0)
+    col = lax.broadcasted_iota(jnp.int32, put_ref.shape, 1)
+    put = ((l & 127) < HD) & (me.t * (heads * HD) + (l >> 7) * HD + (l & 127) == col)
+    put_ref[...] = jnp.where(put, 1.0, 0.0).astype(BF16)
+    for copy in loads[:6]:
+        copy.wait()
+
+    def prep(t):
+        lax.fori_loop(t * per, (t + 1) * per, lambda b, c: (bwd_prep(b, dm_ref, mixt_ref, do_ref, dot_ref), c)[1], 0)
+
+    def arrived(t):
+        remote(dmix_ref.at[t], dm_ref.at[token_rows(t)], dsem.at[0], drecv.at[t], me.d, t).wait_recv()
+
+    own.wait()
+    prep(me.t)
+    arrived(me.t1)
+    prep(me.t1)
+    gm.second()
+    arrived(me.t2)
+    prep(me.t2)
+    arrived(me.t3)
+    prep(me.t3)
+    for copy in loads[6:]:
+        copy.wait()
+    args = (q_ref, qt_ref, k_ref, kt_ref, v_ref, do_ref, dot_ref, dqt_ref, dk_ref, dv_ref)
+    lane = lax.broadcasted_iota(jnp.int32, (BLK, 128), 1)
+
+    def block(a):
+        return (1 - me.y) * (nblk - 1 - a) + me.y * a
+
+    def exchange(a):
+        rows = pl.ds(pl.multiple_of((1 - me.c) * hb, hb), hb)
+        return remote(dn_ref.at[a, rows], r1_ref.at[a], es.at[a], er.at[a], me.d, me.t1)
+
+    def own_block(a):
+        return remote(dn_ref.at[a], ro_ref.at[block(a) % per], ros.at[a % per], ror.at[block(a) % per], me.d, me.t1)
+
+    def mine_rows():
+        return pl.ds(pl.multiple_of(me.c * hb, hb), hb)
+
+    def deliver(a):
+        b = block(a)
+        return remote(s2_ref.at[a], r2_ref.at[b % per, mine_rows()], s2s.at[a], r2r.at[b % per, me.c], me.d, b // per)
+
+    def is_mine(a):
+        return block(a) // per == me.t
+
+    def pass_on(a):
+        exchange(a).wait_recv()
+        s2_ref[a] = (dn_ref[a, mine_rows(), :].astype(F32) + r1_ref[a].astype(F32)).astype(BF16)
+        deliver(a).start()
+
+    def final(a):
+        rows = pl.ds(pl.multiple_of(block(a) * BLK, BLK), BLK)
+        dq, dk, dv = [], [], []
+        for h in range(heads):
+            g = jnp.concatenate([dqt_ref[h, :, rows], jnp.zeros((48, BLK), F32)], axis=0).T
+            dq.append((g * scale_ref[:, h * 128:(h + 1) * 128]).astype(BF16))
+            dk.append(jnp.where(lane < HD, dk_ref[h, rows, :], 0.0).astype(BF16))
+            dv.append(jnp.where(lane < HD, dv_ref[h, rows, :], 0.0).astype(BF16))
+        ds = [jnp.concatenate(g, axis=1) for g in (dq, dk, dv)]
+        dz = sum(dot_nt(ds[s], bp_ref[s]) for s in range(3)).astype(BF16)
+        dn = sum(dot_nt(ds[s], wp_ref[s]) for s in range(3)) + dot(dz, at_ref[...])
+        dn_ref[a] = dn.astype(BF16)
+        ga_ref[...] += dot_tn(dz, xn_ref[rows, :])
+        for s in range(3):
+            gb_ref[s] += dot_tn(rank_ref[rows, :], ds[s])
+
+    def upto(a):
+        return 1 + jnp.minimum(a * (me.line - 1) // (nblk - 2), me.line - 1)
+
+    def pairs(a):
+        b = block(a)
+        bwd_pair(b, b, True, *args)
+
+        def other(n, c):
+            bwd_pair(b + me.y * (1 + n), b - (1 - me.y) * (1 + n), False, *args)
             return c
-        lax.fori_loop(0, tok // BLK, half, 0)
-
-    def one(slot):
-        return remote(dn_ref.at[slot], r1_ref.at[slot], s1s.at[slot], s1r.at[slot], me.d, me.t1)
-
-    shard(me.t3, 0)
-    one(0).start()
-    shard(me.t2, 2)
-    one(0).wait_recv()
-    s2_ref[...] = (dn_ref[2].astype(F32) + r1_ref[0].astype(F32)).astype(BF16)
-    size = tok // chunks
-
-    def two(c):
-        rows = pl.ds(c * size, size)
-        return remote(s2_ref.at[rows], r2_ref.at[rows], s2s.at[c], s2r.at[c], me.d, me.t2)
-
-    two(0).start()
-    shard(me.t1, 1)
-    one(1).start()
-    shard(me.t, 3)
-    hd = gb_ref.shape[2]
-    heads_cols = (hd // 128) * HD
-    l = lax.broadcasted_iota(jnp.int32, (hd, at_ref.shape[1]), 0)
-    col = lax.broadcasted_iota(jnp.int32, (hd, at_ref.shape[1]), 1)
-    put = ((l & 127) < HD) & (me.t * heads_cols + (l >> 7) * HD + (l & 127) == col)
-    put = jnp.where(put, 1.0, 0.0).astype(BF16)
-    n16 = gb_ref.shape[1] // 3
-    n48 = 3 * n16
-    gp_ref[0, :n48] = ga_ref[...].astype(BF16)
-    for s in range(3):
-        gp_ref[0, n48 + s * n16:n48 + (s + 1) * n16] = dot((0.5 * gb_ref[s, s * n16:(s + 1) * n16]).astype(BF16), put).astype(BF16)
-    gp_ref[1] = gmid_ref[...].astype(BF16)
-
-    g1 = remote(gp_ref.at[1 - me.c], gr_ref.at[0], g1s.at[0], g1r.at[0], me.d, me.t1)
-    g1.start()
-    g1.wait_recv()
-    g2_ref[...] = (gp_ref[me.c].astype(F32) + gr_ref[0].astype(F32)).astype(BF16)
-    g2 = remote(g2_ref, gr_ref.at[1], g1s.at[1], g1r.at[1], me.d, me.t2)
-    g2.start()
-    for c in range(1, chunks):
-        two(c).start()
-    g2.wait_recv()
-    gown_ref[...] = (g2_ref[...].astype(F32) + gr_ref[1].astype(F32)).astype(BF16)
-    g = PairLine(me, gown_ref, gall_ref.at[me.c], gs, gr)
-    g.start()
-
-    def relay(o, own=False):
-        return remote(gown_ref if own else gall_ref.at[me.c, o], gall_ref.at[me.c, o], fs.at[o], fr.at[o], me.d, me.t1)
-
-    relay(me.d, True).start()
-    keep = pltpu.make_async_copy(gown_ref, gall_ref.at[me.c, me.d], ls.at[0])
-    keep.start()
-    lax.fori_loop(1, me.line, lambda k, c: (g.hop(k, lambda o: relay(o).start()), c)[1], 0)
-    g.pair_arrivals(lambda o: relay(o).start())
-    one(1).wait_recv()
-    for c in range(chunks):
-        two(c).wait_recv()
-        rows = pl.ds(c * size, size)
-        dn = dn_ref[3, rows, :].astype(F32) + r1_ref[1, rows, :].astype(F32) + r2_ref[rows, :].astype(F32)
+        lax.fori_loop(0, nblk - 1 - a, other, 0)
+
+    def far_step(a, c):
+        pairs(a)
+        @pl.when(a > 0)
+        def _():
+            pass_on(a - 1)
+        final(a)
+        exchange(a).start()
+        @pl.when(a == 0)
+        def _():
+            gm.gather()
+        lax.fori_loop(upto(a), upto(a + 1), lambda k, n: (gm.hop(k), n)[1], 0)
+        return c
+    lax.fori_loop(0, half, far_step, 0)
+
+    def near_step(a, c):
+        pairs(a)
+        @pl.when(a == half)
+        def _():
+            pass_on(a - 1)
+        final(a)
+        @pl.when(jnp.logical_not(is_mine(a)))
+        def _():
+            own_block(a).start()
+        lax.fori_loop(upto(a), upto(a + 1), lambda k, n: (gm.hop(k), n)[1], 0)
+        return c
+    lax.fori_loop(half, nblk, near_step, 0)
+    n16 = n48 // 3
+    gpa[0] = ga_ref[...].astype(BF16)
+    gb = jnp.concatenate([gb_ref[s, s * n16:(s + 1) * n16] for s in range(3)], axis=0)
+    gpa[1] = dot((0.5 * gb).astype(BF16), put_ref[...]).astype(BF16)
+    ga.one().start()
+    gm.arrivals()
+    ga.second()
+
+    def combine(i, c):
+        b = me.t * per + i
+        a = block(b)
+        rows = pl.ds(pl.multiple_of(i * BLK, BLK), BLK)
+        remote(dn_ref.at[a], ro_ref.at[i], ros.at[0], ror.at[i], me.d, me.t1).wait_recv()
+        for h in range(2):
+            remote(s2_ref.at[0], r2_ref.at[i, pl.ds(h * hb, hb)], s2s.at[0], r2r.at[i, h], me.d, me.t2).wait_recv()
+        dn = dn_ref[a].astype(F32) + ro_ref[i].astype(F32) + r2_ref[i].astype(F32)
         x = x_ref[rows, :].astype(F32)
         r = lax.rsqrt(jnp.mean(x * x, axis=-1, keepdims=True) + EPS)
         gd = gain_ref[0:1, :] * dn
-        ig_ref[rows, :] = dmid_ref[rows, :] + r * gd - x * (r * r * r * jnp.mean(x * gd, axis=-1, keepdims=True))
-    def settle(o, c):
-        remote(gown_ref, gall_ref.at[1 - me.c, o], fs.at[o], fr.at[o], me.d, me.t1).wait_recv()
-        remote(gown_ref, gall_ref.at[1 - me.c, o], fs.at[o], fr.at[o], me.d, me.t1).wait_send()
+        dmid_ref[rows, :] = dmid_ref[rows, :] + r * gd - x * (r * r * r * jnp.mean(x * gd, axis=-1, keepdims=True))
         return c
-    lax.fori_loop(0, ndp, settle, 0)
-    g.sent()
-    keep.wait()
-    for slot in range(2):
-        one(slot).wait_send()
-    for c in range(chunks):
-        two(c).wait_send()
-    g1.wait_send()
-    g2.wait_send()
-
-
-def place_kernel(e_ref, g_ref, ain_ref, bqkv_ref, bup_ref, aout_ref, adown_ref, bres_ref):
-    ndp = g_ref.shape[1]
-    for ref in (ain_ref, bqkv_ref, bup_ref, aout_ref, adown_ref, bres_ref):
-        ref[...] = jnp.zeros_like(ref)
-
-    def add(d, c):
-        e = e_ref[d]
-        for n in range(3):
-            ain_ref[n, e] += g_ref[0, d, n * 16:(n + 1) * 16, :].astype(F32)
-            bqkv_ref[n, e] += g_ref[0, d, (3 + n) * 16:(4 + n) * 16, :].astype(F32)
-        ain_ref[3, e] += g_ref[1, d, 0:16, :].astype(F32)
-        bup_ref[e] += g_ref[1, d, 16:32, :].astype(F32)
-        aout_ref[e] += g_ref[1, d, 32:48, :].astype(F32)
-        adown_ref[e] += g_ref[1, d, 48:64, :].astype(F32)
-        bres_ref[0, e] += g_ref[1, d, 64:80, :].astype(F32)
-        bres_ref[1, e] += g_ref[1, d, 80:96, :].astype(F32)
+    ga.gather()
+    lax.fori_loop(0, per, combine, 0)
+    put_ig = pltpu.make_async_copy(dmid_ref, ig_h, igs.at[0])
+    put_ig.start()
+    lax.fori_loop(1, me.line, lambda k, c: (ga.hop(k), c)[1], 0)
+    ga.arrivals()
+    ga.settle(ndp)
+    gm.settle(ndp)
+
+    def sent(a, c):
+        exchange(a).wait_send()
+        deliver(a).wait_send()
         return c
-    lax.fori_loop(0, ndp, add, 0)
+    lax.fori_loop(0, half, sent, 0)
+
+    def own_sent(a, c):
+        @pl.when(jnp.logical_not(is_mine(a)))
+        def _():
+            own_block(a).wait_send()
+        return c
+    lax.fori_loop(half, nblk, own_sent, 0)
+    for n, t in enumerate((me.t3, me.t2, me.t1)):
+        swap(n, t).wait_send()
+    put_ig.wait()
+
+
+def place_kernel(e_ref, gm_ref, ga_ref, ain_h, bqkv_h, bup_h, aout_h, adown_h, bres_h, out_ref, sem):
+    ndp = gm_ref.shape[1]
+    slots = ([(ga_ref, 0, n, ain_h.at[n]) for n in range(3)] + [(ga_ref, 1, n, bqkv_h.at[n]) for n in range(3)]
+             + [(gm_ref, 0, 0, ain_h.at[3]), (gm_ref, 0, 1, bup_h), (gm_ref, 0, 2, aout_h),
+                (gm_ref, 1, 0, adown_h), (gm_ref, 1, 1, bres_h.at[0]), (gm_ref, 1, 2, bres_h.at[1])])
+    copies = []
+    for n, (src, c, k, dst) in enumerate(slots):
+        out_ref[n] = jnp.zeros(out_ref.shape[1:], F32)
+
+        def add(d, carry):
+            e = e_ref[d, 0, 0].astype(jnp.int32)
+            out_ref[n, e] += src[c, d, k * 16:(k + 1) * 16, :].astype(F32)
+            return carry
+        lax.fori_loop(0, ndp, add, 0)
+        copies.append(pltpu.make_async_copy(out_ref.at[n], dst, sem.at[n]))
+        copies[-1].start()
+    for copy in copies:
+        copy.wait()
 
 
 VMEM = pltpu.VMEM
@@ -819,12 +890,6 @@
     )(inputs, norm_gain_rows, choice, at_qkv, b_attn, scale, seg, mq, attention_weights.reshape(wr, hcols), output_weight,
       feedforward_weights.reshape(2 * wrows, hcols))
 
-    def swap(x, cid):
-        return pl.pallas_call(
-            functools.partial(swap_kernel, ndp), out_shape=shape(nt, tok, hcols), in_specs=[IN_VMEM], out_specs=IN_ANY,
-            scratch_shapes=[DMA((3,)), DMA((nt,)), DMA((1,))], compiler_params=params(cid), name="swap",
-        )(x)
-
     output, d_mid, d_mix, g_mid = pl.pallas_call(
         mid_kernel,
         out_shape=[shape(tok, width), shape(tok, width, dtype=F32), shape(nt, tok, hcols), shape(6, rank, width, dtype=F32)],
@@ -834,35 +899,35 @@
         + [VMEM((ndp, nt, wrows, hcols), BF16)] * 3 + [DMA((3,))],
         compiler_params=params(), name="middle",
     )(inputs, cotangent, mixed, norm_gain_rows, at_mid, b_mid, wall)
-    d_mixed = swap(d_mix.reshape(nt * tok, hcols), 3).reshape(tree, hcols)
-
-    dq, dk, dv = pl.pallas_call(
-        bwd_kernel, out_shape=[shape(tree, pad)] * 3, in_specs=[IN_SMEM] * 2 + [IN_VMEM] * 8, out_specs=[IN_VMEM] * 3,
-        scratch_shapes=[VMEM((heads, tree, 128), BF16), VMEM((heads, 128, tree), BF16), VMEM((heads, HD, tree), F32),
-                        VMEM((heads, tree, 128), F32), VMEM((heads, tree, 128), F32), pltpu.SMEM((nblk * nblk,), jnp.int32)],
-        compiler_params=params(limit=62 << 20), name="attend_back",
-    )(lens, parents, d_mixed, mixt, q, qt, k, kt, v, scale)
-
     gr = 6 * rank
-    input_grad, gathered = pl.pallas_call(
-        functools.partial(finish_kernel, ndp, chunks),
-        out_shape=[shape(tok, width, dtype=F32), shape(2, ndp, gr, width)],
-        in_specs=[IN_VMEM] * 12, out_specs=[IN_VMEM, IN_ANY],
-        scratch_shapes=[VMEM((4, tok, width), BF16), VMEM((2, tok, width), BF16), VMEM((tok, width), BF16), VMEM((tok, width), BF16),
-                        VMEM((3 * rank, width), F32), VMEM((3, 3 * rank, pad), F32), VMEM((2, gr, width), BF16), VMEM((2, gr, width), BF16),
-                        VMEM((gr, width), BF16), VMEM((gr, width), BF16),
-                        DMA((2,)), DMA((2,)), DMA((chunks,)), DMA((chunks,)), DMA((2,)), DMA((2,)), DMA((3, ndp)), DMA((ndp,)),
-                        DMA((ndp,)), DMA((ndp,)), DMA((1,))],
-        compiler_params=params(4, 62 << 20), name="finish",
-    )(dq, dk, dv, wp, bp, at_qkv, xn, ranks, inputs, d_mid, norm_gain_rows, g_mid.reshape(gr, width))
+    half_rows = gr // 2
+    half, hb, per = nblk // 2, BLK // 2, tok // BLK
+    grad_bufs = [VMEM((2, half_rows, width), BF16), VMEM((2, half_rows, width), BF16), VMEM((half_rows, width), BF16), VMEM((half_rows, width), BF16)]
+    grad_sems = [DMA((2,)), DMA((2,)), DMA((3, ndp)), DMA((ndp,)), DMA((ndp,)), DMA((ndp,)), DMA((1,))]
+    input_grad, grads_mid, grads_attn = pl.pallas_call(
+        functools.partial(back_kernel, ndp),
+        out_shape=[shape(tok, width, dtype=F32), shape(2, ndp, half_rows, width), shape(2, ndp, half_rows, width)],
+        in_specs=[IN_ANY] * 12 + [IN_VMEM] * 5, out_specs=[IN_ANY] * 3,
+        scratch_shapes=[VMEM((hcols, tree), BF16), VMEM(tall, BF16), VMEM((heads, 128, tree), BF16), VMEM(tall, BF16), VMEM((heads, HD, tree), BF16),
+                        VMEM(tall, BF16), VMEM((3, width, pad), BF16), VMEM((tree, width), BF16), VMEM((tree, 3 * rank), BF16),
+                        VMEM((tok, width), BF16), VMEM((tok, width), F32), VMEM((tree, hcols), BF16), VMEM(tall, BF16), VMEM((heads, 128, tree), BF16),
+                        VMEM((heads, HD, tree), F32), VMEM(tall, F32), VMEM(tall, F32), VMEM((nblk, BLK, width), BF16), VMEM((half, hb, width), BF16),
+                        VMEM((half, hb, width), BF16), VMEM((per, BLK, width), BF16), VMEM((per, BLK, width), BF16),
+                        VMEM((3 * rank, width), F32), VMEM((3, 3 * rank, pad), F32), VMEM((pad, width), BF16)]
+        + grad_bufs + grad_bufs + [DMA((11,)), DMA((4,)), DMA((nt,)), DMA((half,)), DMA((half,)), DMA((half,)), DMA((per, 2)), DMA((per,)), DMA((per,)), DMA((1,))]
+        + grad_sems + grad_sems,
+        compiler_params=params(4, 62 << 20), name="back",
+    )(d_mix, mixt, q, qt, k, kt, v, wp, xn, ranks, inputs, d_mid, scale, bp, at_qkv, norm_gain_rows, g_mid.reshape(gr, width))
 
     count = adapter_first_input.shape[1]
+    table = shape(count, rank, width, dtype=F32)
     ga_in, gb_qkv, gb_up, ga_out, ga_down, gb_res = pl.pallas_call(
         place_kernel,
-        out_shape=[shape(4, count, rank, width, dtype=F32), shape(3, count, rank, width, dtype=F32), shape(count, rank, width, dtype=F32),
-                   shape(count, rank, width, dtype=F32), shape(count, rank, width, dtype=F32), shape(2, count, rank, width, dtype=F32)],
-        in_specs=[IN_SMEM, IN_VMEM], out_specs=[IN_VMEM] * 6, compiler_params=params(), name="place",
-    )(choices[:, 0, 0].astype(jnp.int32), gathered)
+        out_shape=[shape(4, count, rank, width, dtype=F32), shape(3, count, rank, width, dtype=F32), table, table, table,
+                   shape(2, count, rank, width, dtype=F32)],
+        in_specs=[IN_SMEM] + [IN_VMEM] * 2, out_specs=[IN_ANY] * 6,
+        scratch_shapes=[VMEM((12, count, rank, width), F32), DMA((12,))], compiler_params=params(), name="place",
+    )(choices, grads_mid, grads_attn)
     return (output, input_grad, jnp.swapaxes(ga_in, 2, 3), gb_qkv, gb_up, jnp.swapaxes(ga_out, 1, 2), jnp.swapaxes(ga_down, 1, 2), gb_res)
 
 

time: 292 us -> 260 us (0.89)
  Pallas kernels: 273 us -> 244 us
    pallas_call x3 -> x1, Pallas kernels: 120 us -> 91.6 us  [local(): pl.pallas_call(functools.partial(back_kernel, ndp), out_shape=[shape(tok,...]
where the time goes in v3:
time: 260 us
  Pallas kernels  244 us (94%)
  local copies, waits for them, and re-layouts  8.1 us (3%)
  other arithmetic  5.88 us (2%)
    pallas_call x1, Pallas kernels, local(): pl.pallas_call(functools.partial(forward_kernel, ndp, chunks), out_shape=...  115 us
    pallas_call x1, Pallas kernels, local(): pl.pallas_call(functools.partial(back_kernel, ndp), out_shape=[shape(tok,...  91.6 us
    pallas_call x1, Pallas kernels, local(): pl.pallas_call(mid_kernel, out_shape=[shape(tok, width), shape(tok, width...  32.1 us
    pallas_call x1, Pallas kernels, local(): pl.pallas_call(place_kernel, out_shape=[shape(4, count, rank, width, dtyp...  5.7 us

profile of v3, /device:TPU:0, one launch (start us, length us, event | category | flops | bytes accessed | tf_op | source)
XLA Modules:
  0.0 259.6 jit_solution(8462305783068549004)
XLA Ops:
  0.6 0.0 copy-start
  1.4 0.8 reduce-window.7
  2.2 0.7 bitcast_subtract_fusion
  2.9 0.9 select_reduce_fusion
  3.8 0.7 broadcast_multiply_fusion
  4.5 0.1 pad.22.clone
  4.6 0.1 pad.21.clone
  4.6 0.1 select_reduce_fusion.2
  4.7 0.6 pad.11
  5.3 0.7 add_convert_fusion.seg_ref
  6.0 0.7 select_convert_fusion
  6.7 0.6 broadcast_in_dim.55.choice_ref
  7.3 0.7 pad.12.mq_ref
  8.0 1.5 dynamic-slice_bitcast_fusion.5.b_ref
  9.5 0.8 constant_dynamic-slice_fusion
  10.3 0.8 dynamic-slice_bitcast_fusion.2
  11.1 0.7 pad_maximum_fusion.1.b_ref
  11.7 0.8 dynamic-slice_bitcast_fusion.3
  12.5 0.0 copy-done
  12.6 0.7 slice.29
  13.3 0.7 pad_maximum_fusion.at_ref
  13.9 114.6 %forward.1 = (bf16[8,4,480,320]{3,2,1,0:T(8,128)(2,1)}, f32[8,8,128]{2,1,0:T(8,128)}, bf16[4,512,320]{2,1,0:T(8,128)(2,1)}, bf16[2048,1280]{1,0:T(8,128)(2,1)}, ...) custom-call(bf16[512,1280]{1,0:T(8,128)(2,1)} %x_h.1, ...), custom_call_target="tpu_custom_call" | custom-call | tf_op jit(solution)/shard_map/forward/pallas_call | solution.py:876
  128.6 32.1 %middle.1 = (bf16[512,1280]{1,0:T(8,128)(2,1)}, f32[512,1280]{1,0:T(8,128)}, bf16[4,512,320]{2,1,0:T(8,128)(2,1)}, f32[6,16,1280]{2,1,0:T(8,128)}) custom-call(bf16[512,1280]{1,0:T(8,128)(2,1)} %x_h.1, bf16[512,1280]{1,0:T(8,128)(2,1)} %g_ref.1, bf16[4,512,320]{2,1,0:T(8,128)(2,1)} %get-tuple-element.34.mix4_ref, f32[2,1280]{1,0:T(2,128)} %gain_ref.5, ...), custom_call_target="tpu_custom_call" | custom-call | tf_op jit(solution)/shard_map/middle/pallas_call | solution.py:893
  160.7 91.6 %back.1 = (f32[512,1280]{1,0:T(8,128)}, bf16[2,8,48,1280]{3,2,1,0:T(8,128)(2,1)}, bf16[2,8,48,1280]{3,2,1,0:T(8,128)(2,1)}) custom-call(bf16[4,512,320]{2,1,0:T(8,128)(2,1)} %get-tuple-element.37.dmix_ref, bf16[320,2048]{1,0:T(8,128)(2,1)} %get-tuple-element.38.mixt_h, bf16[4,2048,128]{2,1,0:T(8,128)(2,1)} %get-tuple-element.39.q_h, ...), custom_call_target="tpu_custom_call" | custom-call | tf_op jit(solution)/shard_map/back/pallas_call | solution.py:907
  252.4 0.0 copy-start.1
  252.4 5.7 %place.1 = (f32[4,8,16,1280]{3,2,1,0:T(8,128)}, f32[3,8,16,1280]{3,2,1,0:T(8,128)}, f32[8,16,1280]{2,1,0:T(8,128)}, f32[8,16,1280]{2,1,0:T(8,128)}, f32[8,16,1280]{2,1,0:T(8,128)}, /*index=5*/f32[2,8,16,1280]{3,2,1,0:T(8,128)}) custom-call(f32[8,8,128]{2,1,0:T(8,128)} %get-tuple-element.51.e_ref, bf16[2,8,48,1280]{3,2,1,0:T(8,128)(2,1)} %get-tuple-element.52.gm_ref, ...), custom_call_target="tpu_custom_call" | custom-call | tf_op jit(solution)/shard_map/place/pallas_call | solution.py:924
  258.1 0.0 copy-done.1
  258.1 1.5 copy.26
  (6 shorter events, 0.0 us)
Async XLA Ops:
  0.6 11.9 %copy-start = (bf16[4,8,1280,16]{2,3,1,0:T(8,128)(2,1)S(1)}, bf16[4,8,1280,16]{2,3,1,0:T(8,128)(2,1)}, u32[]{:S(2)}) copy-start(bf16[4,8,1280,16]{2,3,1,0:T(8,128)(2,1)} %param.26) | copy-start | bytes 3932164
  252.4 5.7 %copy-start.1 = (f32[512,1280]{1,0:T(8,128)S(1)}, f32[512,1280]{1,0:T(8,128)}, u32[]{:S(2)}) copy-start(f32[512,1280]{1,0:T(8,128)} %get-tuple-element.75) | copy-start | bytes 7864324

commit v4 on v3

--- a/solution.py
+++ b/solution.py
@@ -20,27 +20,28 @@
 def dot_tn(a, b):
     return lax.dot_general(a, b, (((0,), (0,)), ((), ())), preferred_element_type=F32)
 
-def project(b, x_ref, wp_ref, a_ref, bp_ref, scale_ref, seg_ref, mq_ref, q_ref, qt_ref, k_ref, kt_ref, v_ref, vt_ref, rank_ref):
+def project(b, s, x_ref, wp_ref, a_ref, bp_ref, scale_ref, seg_ref, mq_ref, n_ref, t_ref, rank_ref):
     rows = pl.ds(pl.multiple_of(b * BLK, BLK), BLK)
     xb = x_ref[rows, :]
-    rank = dot_nt(xb, a_ref[...]).astype(BF16)
-    rank_ref[rows, :] = rank
+    if s == 0:
+        rank_ref[rows, :] = dot_nt(xb, a_ref[...]).astype(BF16)
     lane = lax.broadcasted_iota(jnp.int32, (BLK, 128), 1)
-    tok = (lax.broadcasted_iota(jnp.int32, (BLK, 128), 0) + b * BLK).astype(F32)
-    hot = jnp.where((tok >= seg_ref[0:1, :]) & (tok < seg_ref[1:2, :]), 1.0, 0.0)
-    qfeat = dot(hot.astype(BF16), mq_ref[...])
-    kfeat = jnp.where((lane >= HD + 13) & (lane < HD + 16), 1.0, hot)
-    vfeat = jnp.where(lane < HD + 2, 1.0, 0.0)
-    heads = q_ref.shape[0]
-    for s, (n_ref, t_ref, feat) in enumerate(((q_ref, qt_ref, qfeat), (k_ref, kt_ref, kfeat), (v_ref, vt_ref, vfeat))):
-        y = dot(xb, wp_ref[s]) + dot(rank, bp_ref[s])
+    if s == 2:
+        feat = jnp.where(lane < HD + 2, 1.0, 0.0)
+    else:
+        tok = (lax.broadcasted_iota(jnp.int32, (BLK, 128), 0) + b * BLK).astype(F32)
+        feat = jnp.where((tok >= seg_ref[0:1, :]) & (tok < seg_ref[1:2, :]), 1.0, 0.0)
         if s == 0:
-            y = y * scale_ref[...]
-        for h in range(heads):
-            yh = jnp.where(lane < HD, y[:, h * 128:(h + 1) * 128], feat)
-            n_ref[h, rows, :] = yh.astype(BF16)
-            yt = yh.T
-            t_ref[h, :, rows] = yt[:t_ref.shape[1]].astype(BF16)
+            feat = dot(feat.astype(BF16), mq_ref[...])
+        else:
+            feat = jnp.where((lane >= HD + 13) & (lane < HD + 16), 1.0, feat)
+    y = dot(xb, wp_ref[s]) + dot(rank_ref[rows, :], bp_ref[s])
+    if s == 0:
+        y = y * scale_ref[...]
+    for h in range(n_ref.shape[0]):
+        yh = jnp.where(lane < HD, y[:, h * 128:(h + 1) * 128], feat)
+        n_ref[h, rows, :] = yh.astype(BF16)
+        t_ref[h, :, rows] = yh.T[:t_ref.shape[1]].astype(BF16)
 
 def attend_block(i, qt_ref, k_ref, vt_ref, m_ref, acc_ref, mixt_ref, mix_ref, count=None, jlist=None):
     heads = qt_ref.shape[0]
@@ -90,6 +91,32 @@
     l = lax.broadcasted_iota(jnp.int32, (hcols, pad), 1)
     return jnp.where(((l & 127) < HD) & ((l >> 7) * HD + (l & 127) == c), 1.0, 0.0).astype(BF16)
 
+def head_columns(me, pad, width):
+    l = lax.broadcasted_iota(jnp.int32, (pad, width), 0)
+    col = lax.broadcasted_iota(jnp.int32, (pad, width), 1)
+    put = ((l & 127) < HD) & (me.t * (pad // 128 * HD) + (l >> 7) * HD + (l & 127) == col)
+    return jnp.where(put, 1.0, 0.0).astype(BF16)
+
+def tree_masks(len_ref, par_ref, seg_ref, mq_ref):
+    segs = len_ref.shape[1]
+    lane = lax.broadcasted_iota(jnp.int32, (1, 128), 1) - HD
+    row = lax.broadcasted_iota(jnp.int32, (128, 1), 0) - HD
+    lo = hi = jnp.zeros((1, 128), jnp.int32)
+    up = grand = jnp.full((128, 1), -1, jnp.int32)
+    start = 0
+    for u in range(segs):
+        end = start + len_ref[0, u]
+        parent = par_ref[0, u]
+        lo = jnp.where(lane == u, start, lo)
+        hi = jnp.where(lane == u, end, hi)
+        up = jnp.where(row == u, parent, up)
+        grand = jnp.where(row == u, par_ref[0, parent], grand)
+        start = end
+    seg_ref[0:1, :] = lo.astype(F32)
+    seg_ref[1:2, :] = hi.astype(F32)
+    reach = (lane == row) | (lane == up) | (lane == grand)
+    inside = (row >= 0) & (row < segs) & (lane >= 0) & (lane < segs)
+    mq_ref[...] = jnp.where(inside & jnp.logical_not(reach), -BIG, 0.0).astype(BF16)
 
 def bwd_prep(b, dm_ref, mixt_ref, do_ref, dot_ref):
     rows = pl.ds(pl.multiple_of(b * BLK, BLK), BLK)
@@ -170,11 +197,15 @@
 
 
 class PairLine:
-    def __init__(self, me, own, buf, send, recv):
-        self.me, self.own, self.buf, self.send, self.recv = me, own, buf, send, recv
+    def __init__(self, me, own, buf, send, recv, part=None):
+        self.me, self.own, self.buf, self.send, self.recv, self.part = me, own, buf, send, recv, part
+
+    def slot(self, o):
+        return self.buf.at[o] if self.part is None else self.buf.at[o, self.part]
 
     def copy(self, o, src, d, kind):
-        return remote(src, self.buf.at[o], self.send.at[kind, o], self.recv.at[o], d, self.me.t)
+        send, recv = (self.send.at[kind, o], self.recv.at[o]) if self.part is None else (self.send.at[kind, o, self.part], self.recv.at[o, self.part])
+        return remote(src, self.slot(o), send, recv, d, self.me.t)
 
     def start(self):
         me = self.me
@@ -191,28 +222,28 @@
         @pl.when(me.p - k >= 0)
         def _():
             o = me.d - 2 * k
-            self.copy(o, self.buf.at[o], me.dx, 2).wait_recv()
+            self.copy(o, self.slot(o), me.dx, 2).wait_recv()
             @pl.when(me.has_right)
             def _():
-                self.copy(o, self.buf.at[o], me.d + 2, 1).start()
-            self.copy(o, self.buf.at[o], me.dx, 2).start()
+                self.copy(o, self.slot(o), me.d + 2, 1).start()
+            self.copy(o, self.slot(o), me.dx, 2).start()
             if then is not None:
                 then(o)
         @pl.when(me.p + k < me.line)
         def _():
             o = me.d + 2 * k
-            self.copy(o, self.buf.at[o], me.dx, 2).wait_recv()
+            self.copy(o, self.slot(o), me.dx, 2).wait_recv()
             @pl.when(me.has_left)
             def _():
-                self.copy(o, self.buf.at[o], me.d - 2, 0).start()
-            self.copy(o, self.buf.at[o], me.dx, 2).start()
+                self.copy(o, self.slot(o), me.d - 2, 0).start()
+            self.copy(o, self.slot(o), me.dx, 2).start()
             if then is not None:
                 then(o)
 
     def pair_arrivals(self, then=None):
         def one(q, c):
             o = 2 * q + 1 - self.me.par
-            self.copy(o, self.buf.at[o], self.me.dx, 2).wait_recv()
+            self.copy(o, self.slot(o), self.me.dx, 2).wait_recv()
             if then is not None:
                 then(o)
             return c
@@ -222,13 +253,13 @@
         me = self.me
         def one(q, c):
             o = 2 * q + me.par
-            self.copy(o, self.buf.at[o], me.dx, 2).wait_send()
+            self.copy(o, self.slot(o), me.dx, 2).wait_send()
             @pl.when((q >= me.p) & me.has_left)
             def _():
-                self.copy(o, self.buf.at[o], me.dx, 0).wait_send()
+                self.copy(o, self.slot(o), me.dx, 0).wait_send()
             @pl.when((q <= me.p) & me.has_right)
             def _():
-                self.copy(o, self.buf.at[o], me.dx, 1).wait_send()
+                self.copy(o, self.slot(o), me.dx, 1).wait_send()
             return c
         lax.fori_loop(0, me.line, one, 0)
 
@@ -236,7 +267,7 @@
 class FullGather:
     def __init__(self, me, own, buf, send, first, recv):
         self.me, self.own, self.buf, self.send, self.first, self.recv = me, own, buf, send, first, recv
-        cut = own.shape[0] // 32 * 16
+        cut = own.shape[0] // 48 * 16
         self.parts = (pl.ds(0, cut), pl.ds(cut, own.shape[0] - cut))
 
     def copy(self, h, o, t, d2, t2, kind, own=False):
@@ -264,7 +295,7 @@
         me = self.me
         self.copy(0, me.d, me.t, me.dx, me.t, 4, True).start()
         self.copy(1, me.d, me.t, me.d, me.t2, 4, True).start()
-        for h in range(2):
+        for h in (1, 0):
             self.spread(h, me.d, me.t, me.has_left, me.has_right, True)
 
     def arrived(self, h, o, t):
@@ -294,14 +325,20 @@
                 self.arrived(h, o, t)
                 self.spread(h, o, t, me.has_left, False)
 
-    def lasts(self):
-        me = self.me
-        def one(q, c):
+    def lasts(self, k):
+        me = self.me
+
+        def place(q):
             for h, o, t in ((0, 2 * q, me.t2), (0, 2 * q + 1, me.t2), (1, 2 * q + 1 - me.par, me.t), (1, 2 * q + 1 - me.par, me.t2)):
                 self.arrived(h, o, t)
                 self.copy(h, o, t, me.d, me.t1, 3).start()
-            return c
-        lax.fori_loop(0, me.line, one, 0)
+
+        @pl.when(me.p - k >= 0)
+        def _():
+            place(me.p - k)
+        @pl.when((me.p + k < me.line) & (k > 0))
+        def _():
+            place(me.p + k)
 
     def finish(self):
         me = self.me
@@ -331,8 +368,9 @@
 EPS = 1e-6
 
 
-def forward_kernel(ndp, chunks, x_ref, gain_ref, choice_ref, at_ref, b_ref, scale_ref, seg_ref, mq_ref, a_ref, wo_ref, wf_ref,
-                   wout_ref, cho_ref, mixed_ref, xno_ref, qo_ref, qto_ref, ko_ref, kto_ref, vo_ref, ranko_ref, mixto_ref, wpo_ref, bpo_ref,
+def forward_kernel(ndp, chunks, choice_in, len_ref, par_ref, x_ref, gain_ref, qs_ref, ain_h, btab_h, a_ref, wo_ref, wf_ref,
+                   wout_ref, cho_ref, mixed_ref, xno_ref, qo_ref, qto_ref, ko_ref, kto_ref, vo_ref, ranko_ref, mixto_ref, wpo_ref, bpo_ref, ato_ref, scaleo_ref,
+                   ain_ref, btab_ref, choice_ref, at_ref, scale_ref, seg_ref, mq_ref, put_ref,
                    aown_ref, wown_ref, xn_ref, wa_ref, wp_ref, bp_ref, q_ref, qt_ref, k_ref, kt_ref, v_ref, vt_ref, rank_ref, mixt_ref,
                    mix_ref, m_ref, acc_ref, ls, os, xs, xr, a_s, a_r, c_s, c_r, w_s, w_f, w_r, ms, mr):
     me = Place(ndp)
@@ -340,8 +378,11 @@
     rows_o = wo_ref.shape[0]
     loads = [pltpu.make_async_copy(a_ref, aown_ref, ls.at[0]), pltpu.make_async_copy(wo_ref, wown_ref.at[pl.ds(0, rows_o)], ls.at[1]),
              pltpu.make_async_copy(wf_ref, wown_ref.at[pl.ds(rows_o, wf_ref.shape[0])], ls.at[2])]
-    for copy in loads:
+    tables = [pltpu.make_async_copy(ain_h.at[pl.ds(0, 3)], ain_ref, ls.at[3]), pltpu.make_async_copy(btab_h, btab_ref, ls.at[4])]
+    for copy in loads + tables:
         copy.start()
+    e = choice_in[0]
+    choice_ref[...] = jnp.zeros_like(choice_ref) + e.astype(F32)
     x = x_ref[...].astype(F32)
     mine = pl.ds(pl.multiple_of(me.t * tok, tok), tok)
     xn_ref[mine, :] = (x * lax.rsqrt(jnp.mean(x * x, axis=-1, keepdims=True) + EPS) * gain_ref[0:1, :]).astype(BF16)
@@ -358,23 +399,43 @@
         xcopy(me.t, c, me.t1, 1).start()
     for copy in loads:
         copy.wait()
-    a = PairLine(me, aown_ref, wa_ref, a_s, a_r)
+    parts = [PairLine(me, aown_ref.at[n], wa_ref, a_s, a_r, n) for n in range(3)]
     ch = PairLine(me, choice_ref, cho_ref, c_s, c_r)
     w = FullGather(me, wown_ref, wout_ref, w_s, w_f, w_r)
-    a.start()
-    ch.start()
+    parts[0].start()
+    parts[1].start()
     keep = [pltpu.make_async_copy(wown_ref, wout_ref.at[me.d, me.t], ls.at[0]), pltpu.make_async_copy(choice_ref, cho_ref.at[me.d], ls.at[1])]
     for copy in keep:
         copy.start()
     wa_ref[me.d] = aown_ref[...]
-    early = max(1, me.line - 2)
-
-    def hop(k, carry):
-        a.hop(k)
-        ch.hop(k)
+    tree_masks(len_ref, par_ref, seg_ref, mq_ref)
+    scale_ref[...] = jnp.zeros_like(scale_ref)
+    for h in range(q_ref.shape[0]):
+        scale_ref[:, h * 128:h * 128 + HD] = qs_ref[...] * (1.0 / math.sqrt(HD))
+    put_ref[...] = head_columns(me, *put_ref.shape)
+    for copy in tables:
+        copy.wait()
+    parts[0].hop(1)
+    parts[2].start()
+    ch.start()
+
+    def diagonal(n, carry):
+        for part in range(3):
+            k = n - part
+            @pl.when((k >= 1) & (k < me.line))
+            def _():
+                parts[part].hop(k)
         return carry
-    lax.fori_loop(1, early + 1, hop, 0)
+    lax.fori_loop(2, me.line + 2, diagonal, 0)
     w.start()
+    n16 = ain_ref.shape[2]
+    for s in range(3):
+        at_ref[s * n16:(s + 1) * n16] = ain_ref[s, e]
+    picked = jnp.concatenate([btab_ref[s, e] for s in range(3)], axis=0)
+    spread = (0.5 * dot_nt(picked, put_ref[...])).astype(BF16)
+    bp_ref[...] = jnp.zeros_like(bp_ref)
+    for s in range(3):
+        bp_ref[s, s * n16:(s + 1) * n16] = spread[s * n16:(s + 1) * n16]
 
     def forward(c):
         xcopy(me.t2, c, me.t1, 2).wait_recv()
@@ -382,43 +443,42 @@
 
     for c in range(chunks // 2):
         forward(c)
-    lax.fori_loop(early + 1, me.line, hop, 0)
-    for c in range(chunks // 2, chunks):
-        forward(c)
-    a.pair_arrivals()
-    ch.pair_arrivals()
-
-    sel = spread_heads(wa_ref.shape[2], wp_ref.shape[2])
-    bp_ref[...] = jnp.zeros_like(bp_ref)
-    wrows = wa_ref.shape[1] // 3
+    nblk = xn_ref.shape[0] // BLK
+    near = nblk // 2
+    wrows = wa_ref.shape[2]
     group = 16 // math.gcd(wrows, 16)
-    for s in range(3):
-        n = b_ref.shape[1]
-        bp_ref[s, s * n:(s + 1) * n] = (0.5 * dot(b_ref[s], sel)).astype(BF16)
-        for o in range(0, ndp, group):
-            wp_ref[s, o * wrows:(o + group) * wrows] = jnp.concatenate(
-                [dot(wa_ref[o + j, s * wrows:(s + 1) * wrows], sel) for j in range(group)], axis=0).astype(BF16)
+    sel = spread_heads(wa_ref.shape[3], wp_ref.shape[2])
+
+    def project_blocks(first, s):
+        n_ref, t_ref = ((q_ref, qt_ref), (k_ref, kt_ref), (v_ref, vt_ref))[s]
+        lax.fori_loop(0, near, lambda n, c: (project(first + n, s, xn_ref, wp_ref, at_ref, bp_ref, scale_ref, seg_ref, mq_ref, n_ref, t_ref, rank_ref), c)[1], 0)
+
     for c in range(chunks):
         xcopy(me.t1, c, me.t1, 2).wait_recv()
+    for s in range(3):
+        parts[s].pair_arrivals()
+        for o in range(0, ndp, group):
+            wp_ref[s, o * wrows:(o + group) * wrows] = jnp.concatenate([dot(wa_ref[o + j, s], sel) for j in range(group)], axis=0).astype(BF16)
+        project_blocks(me.y * near, s)
+        if s < 2:
+            forward(chunks // 2 + s)
+    for c in range(chunks):
         xcopy(me.t3, c, me.t1, 2).wait_recv()
     w.firsts()
-    nblk = xn_ref.shape[0] // BLK
-    span = 2 * nblk - 3
-
-    def upto(step):
-        return 1 + jnp.minimum(step * (me.line - 1) // span, me.line - 1)
-
-    def relay(step):
-        lax.fori_loop(upto(step), upto(step + 1), lambda k, c: (w.hop(k), c)[1], 0)
-
-    def project_step(b, c):
-        project(b, xn_ref, wp_ref, at_ref, bp_ref, scale_ref, seg_ref, mq_ref, q_ref, qt_ref, k_ref, kt_ref, v_ref, vt_ref, rank_ref)
-        relay(b)
-        return c
-    lax.fori_loop(0, nblk, project_step, 0)
+    for s in range(3):
+        project_blocks((1 - me.y) * near, s)
+
+    def hops(i):
+        done = 1 + jnp.maximum((me.line - 2) * (i + 1) * (i + 2) + 2 * nblk, 0) // ((nblk - 1) * nblk)
+        return jnp.minimum(done, me.line - 1)
+
+    def relay(i):
+        lax.fori_loop(hops(i - 1), hops(i), lambda k, c: (w.hop(k + 1), ch.hop(k + 1), c)[2], 0)
+    w.hop(1)
+    ch.hop(1)
     outs = [pltpu.make_async_copy(src, dst, os.at[n]) for n, (src, dst) in enumerate((
         (xn_ref, xno_ref), (q_ref, qo_ref), (k_ref, ko_ref), (kt_ref, kto_ref), (v_ref, vo_ref), (rank_ref, ranko_ref),
-        (wp_ref, wpo_ref), (bp_ref, bpo_ref)))]
+        (wp_ref, wpo_ref), (bp_ref, bpo_ref), (at_ref, ato_ref), (scale_ref, scaleo_ref)))]
     for copy in outs:
         copy.start()
     per = tok // BLK
@@ -436,19 +496,22 @@
         @pl.when(t != me.t)
         def _():
             remote(src, dst, ms.at[i], mr.at[me.t, i % per], me.d, t).start()
-        relay(nblk + i)
+        relay(i)
+        lax.fori_loop(jnp.where(i == 0, 0, hops(i - 2)), hops(i - 1), lambda k, n: (w.lasts(k), n)[1], 0)
         return c
     lax.fori_loop(0, nblk, attend_step, 0)
     late = [pltpu.make_async_copy(qt_ref, qto_ref, os.at[len(outs)]), pltpu.make_async_copy(mixt_ref, mixto_ref, os.at[len(outs) + 1])]
     for copy in late:
         copy.start()
-    w.lasts()
+    lax.fori_loop(hops(nblk - 2), me.line, lambda k, c: (w.lasts(k), c)[1], 0)
+    ch.pair_arrivals()
     for t in (me.t1, me.t2, me.t3):
         for h in range(per):
             dst = mixed_ref.at[t, pl.ds(h * BLK, BLK)]
             remote(dst, dst, ms.at[0], mr.at[t, h], me.d, t).wait_recv()
     w.finish()
-    a.sent()
+    for part in parts:
+        part.sent()
     ch.sent()
     for c in range(chunks):
         for kind in range(3):
@@ -472,16 +535,22 @@
     return 1.0 / (1.0 + jnp.exp(-v))
 
 
-def mid_kernel(x_ref, g_ref, mix4_ref, gain_ref, at_ref, b_ref, wall_ref, out_ref, dmid_ref, dmix_ref, grads_ref,
-               mix_ref, mid_ref, hid_ref, up_ref, act_ref, f_ref, low_ref, w_ref, wb0_ref, wb1_ref, wb2_ref, ls):
+def mid_kernel(e_ref, x_ref, g_ref, mix4_ref, gain_ref, wall_ref, aout_h, ain_h, adown_h, bup_h, bres_h, out_ref, dmid_ref, dmix_ref, grads_ref,
+               at_ref, b_ref, ts, mix_ref, mid_ref, hid_ref, up_ref, act_ref, f_ref, low_ref, w_ref, wb0_ref, wb1_ref, wb2_ref, ls):
     width = x_ref.shape[1]
     step = 256
     part = mix4_ref.shape[2]
     blocks = (wb0_ref, wb1_ref, wb2_ref)
     ndp, nt, wrows = wb0_ref.shape[:3]
     loads = [pltpu.make_async_copy(wall_ref.at[:, :, pl.ds(n * wrows, wrows)], blocks[n], ls.at[n]) for n in range(3)]
-    for copy in loads:
+    e = e_ref[0]
+    tables = [pltpu.make_async_copy(src, dst, ts.at[n]) for n, (src, dst) in enumerate((
+        (aout_h.at[e], at_ref.at[0]), (ain_h.at[3, e], at_ref.at[1]), (adown_h.at[e], at_ref.at[2]),
+        (bres_h.at[0, e], b_ref.at[0]), (bup_h.at[e], b_ref.at[1]), (bres_h.at[1, e], b_ref.at[2])))]
+    for copy in tables + loads:
         copy.start()
+    for copy in tables:
+        copy.wait()
 
     def assemble(n):
         loads[n].wait()
@@ -640,11 +709,7 @@
         copy.start()
     for ref in (dqt_ref, dk_ref, dv_ref, ga_ref, gb_ref):
         ref[...] = jnp.zeros_like(ref)
-    hd = gb_ref.shape[2]
-    l = lax.broadcasted_iota(jnp.int32, put_ref.shape, 0)
-    col = lax.broadcasted_iota(jnp.int32, put_ref.shape, 1)
-    put = ((l & 127) < HD) & (me.t * (heads * HD) + (l >> 7) * HD + (l & 127) == col)
-    put_ref[...] = jnp.where(put, 1.0, 0.0).astype(BF16)
+    put_ref[...] = head_columns(me, *put_ref.shape)
     for copy in loads[:6]:
         copy.wait()
 
@@ -794,12 +859,13 @@
     put_ig.wait()
 
 
-def place_kernel(e_ref, gm_ref, ga_ref, ain_h, bqkv_h, bup_h, aout_h, adown_h, bres_h, out_ref, sem):
+def place_kernel(e_ref, gm_ref, ga_ref, ig_in, ain_h, bqkv_h, bup_h, aout_h, adown_h, bres_h, ig_out, out_ref, sem):
     ndp = gm_ref.shape[1]
     slots = ([(ga_ref, 0, n, ain_h.at[n]) for n in range(3)] + [(ga_ref, 1, n, bqkv_h.at[n]) for n in range(3)]
              + [(gm_ref, 0, 0, ain_h.at[3]), (gm_ref, 0, 1, bup_h), (gm_ref, 0, 2, aout_h),
                 (gm_ref, 1, 0, adown_h), (gm_ref, 1, 1, bres_h.at[0]), (gm_ref, 1, 2, bres_h.at[1])])
-    copies = []
+    copies = [pltpu.make_async_copy(ig_in, ig_out, sem.at[len(slots)])]
+    copies[0].start()
     for n, (src, c, k, dst) in enumerate(slots):
         out_ref[n] = jnp.zeros(out_ref.shape[1:], F32)
 
@@ -837,68 +903,49 @@
     adapter_first_output, adapter_first_down, adapter_second_residual,
 ):
     ndp, nt = lax.axis_size("dp"), lax.axis_size("tensor")
-    tpos = lax.axis_index("tensor")
     tok, width = inputs.shape
     tree = tok * nt
     wrows, hcols = output_weight.shape
     heads = hcols // HD
     pad = heads * 128
-    segs = segment_lengths.shape[1]
     rank = adapter_first_input.shape[3]
     nblk = tree // BLK
-    e = adapter_choice_per_tree[0]
-    lens, parents = segment_lengths[0], segment_parents[0]
-
-    def pick(table, axis):
-        return lax.dynamic_index_in_dim(table, e, axis, keepdims=False)
-
-    a_in = pick(jnp.swapaxes(adapter_first_input, 2, 3), 1)
-    b_attn = lax.dynamic_slice_in_dim(pick(adapter_second_attention, 1), tpos * hcols, hcols, 2)
-    b_res = pick(adapter_second_residual, 1)
-    at_qkv = a_in[:3].reshape(3 * rank, width)
-    at_mid = jnp.stack([pick(jnp.swapaxes(adapter_first_output, 1, 2), 0), a_in[3], pick(jnp.swapaxes(adapter_first_down, 1, 2), 0)])
-    b_mid = jnp.stack([b_res[0], pick(adapter_second_up, 0), b_res[1]])
-    ends = jnp.cumsum(lens)
-    lane = jnp.arange(128, dtype=jnp.int32) - HD
-    spot = (lane[None, :] == jnp.arange(segs, dtype=jnp.int32)[:, None])
-    seg = jnp.stack([jnp.sum(jnp.where(spot, (ends - lens)[:, None], 0), 0), jnp.sum(jnp.where(spot, ends[:, None], 0), 0)]
-                    + [jnp.zeros((128,), jnp.int32)] * 6).astype(F32)
-    idx = jnp.arange(segs, dtype=jnp.int32)
-    grand = jnp.sum(jnp.where(parents[:, None] == idx[None, :], parents[None, :], 0), axis=1)
-    reach = (idx[:, None] == idx[None, :]) | (parents[:, None] == idx[None, :]) | (grand[:, None] == idx[None, :])
-    mq = jnp.pad(jnp.where(reach, 0.0, -BIG).astype(BF16), ((HD, 128 - HD - segs), (HD, 128 - HD - segs)))
-    scale = jnp.pad(jnp.broadcast_to(query_dimension_scale[None, :] / math.sqrt(HD), (heads, HD)), ((0, 0), (0, 128 - HD))).reshape(1, pad)
+    a_in, a_out, a_down = (jnp.swapaxes(table, -1, -2) for table in (adapter_first_input, adapter_first_output, adapter_first_down))
 
     chunks = 4
-    choice = jnp.full((8, 128), e, F32)
+    count = a_in.shape[1]
     wr = wrows * 3
     tall = (heads, tree, 128)
-    wall, choices, mixed, xn, q, qt, k, kt, v, ranks, mixt, wp, bp = pl.pallas_call(
+    wall, choices, mixed, xn, q, qt, k, kt, v, ranks, mixt, wp, bp, at_qkv, scale = pl.pallas_call(
         functools.partial(forward_kernel, ndp, chunks),
         out_shape=[shape(ndp, nt, wr, hcols), shape(ndp, 8, 128, dtype=F32), shape(nt, tok, hcols), shape(tree, width),
                    shape(*tall), shape(heads, 128, tree), shape(*tall), shape(heads, HD, tree), shape(*tall),
-                   shape(tree, 3 * rank), shape(hcols, tree), shape(3, width, pad), shape(3, 3 * rank, pad)],
-        in_specs=[IN_VMEM] * 8 + [IN_ANY] * 3, out_specs=[IN_ANY] * 13,
-        scratch_shapes=[VMEM((wr, hcols), BF16), VMEM((wr, hcols), BF16), VMEM((tree, width), BF16), VMEM((ndp, wr, hcols), BF16),
+                   shape(tree, 3 * rank), shape(hcols, tree), shape(3, width, pad), shape(3, 3 * rank, pad), shape(3 * rank, width),
+                   shape(1, pad, dtype=F32)],
+        in_specs=[IN_SMEM] * 3 + [IN_VMEM] * 3 + [IN_ANY] * 5, out_specs=[IN_ANY] * 15,
+        scratch_shapes=[VMEM((3, count, rank, width), BF16), VMEM((3, count, rank, width), BF16), VMEM((8, 128), F32), VMEM((3 * rank, width), BF16),
+                        VMEM((1, pad), F32), VMEM((8, 128), F32), VMEM((128, 128), BF16), VMEM((pad, width), BF16),
+                        VMEM((3, wrows, hcols), BF16), VMEM((wr, hcols), BF16), VMEM((tree, width), BF16), VMEM((ndp, 3, wrows, hcols), BF16),
                         VMEM((3, width, pad), BF16), VMEM((3, 3 * rank, pad), BF16), VMEM(tall, BF16), VMEM((heads, 128, tree), BF16),
                         VMEM(tall, BF16), VMEM((heads, HD, tree), BF16), VMEM(tall, BF16), VMEM((heads, HD + 16, tree), BF16),
                         VMEM((tree, 3 * rank), BF16), VMEM((hcols, tree), BF16), VMEM((tree, hcols), BF16),
-                        VMEM((heads, 1, BLK), F32), VMEM((heads, HD + 16, BLK), F32), DMA((3,)), DMA((10,)),
-                        DMA((3, chunks)), DMA((nt, chunks)), DMA((3, ndp)), DMA((ndp,)), DMA((3, ndp)), DMA((ndp,)),
+                        VMEM((heads, 1, BLK), F32), VMEM((heads, HD + 16, BLK), F32), DMA((5,)), DMA((12,)),
+                        DMA((3, chunks)), DMA((nt, chunks)), DMA((3, ndp, 3)), DMA((ndp, 3)), DMA((3, ndp)), DMA((ndp,)),
                         DMA((2, ndp, nt, 4)), DMA((2,)), DMA((2, ndp, nt)), DMA((nblk,)), DMA((nt, tok // BLK))],
         compiler_params=params(1), name="forward",
-    )(inputs, norm_gain_rows, choice, at_qkv, b_attn, scale, seg, mq, attention_weights.reshape(wr, hcols), output_weight,
+    )(adapter_choice_per_tree, segment_lengths, segment_parents, inputs, norm_gain_rows, query_dimension_scale[None, :], a_in,
+      adapter_second_attention, attention_weights, output_weight,
       feedforward_weights.reshape(2 * wrows, hcols))
 
     output, d_mid, d_mix, g_mid = pl.pallas_call(
         mid_kernel,
         out_shape=[shape(tok, width), shape(tok, width, dtype=F32), shape(nt, tok, hcols), shape(6, rank, width, dtype=F32)],
-        in_specs=[IN_VMEM] * 6 + [IN_ANY], out_specs=[IN_VMEM] * 4,
-        scratch_shapes=[VMEM((tok, width), BF16), VMEM((tok, width), F32), VMEM((tok, width), BF16), VMEM((tok, width), F32),
+        in_specs=[IN_SMEM] + [IN_VMEM] * 4 + [IN_ANY] * 6, out_specs=[IN_VMEM] * 4,
+        scratch_shapes=[VMEM((3, rank, width), BF16), VMEM((3, rank, width), BF16), DMA((6,)), VMEM((tok, width), BF16), VMEM((tok, width), F32), VMEM((tok, width), BF16), VMEM((tok, width), F32),
                         VMEM((tok, width), BF16), VMEM((tok, width), F32), VMEM((tok, width), BF16), VMEM((3, width, width), BF16)]
         + [VMEM((ndp, nt, wrows, hcols), BF16)] * 3 + [DMA((3,))],
         compiler_params=params(), name="middle",
-    )(inputs, cotangent, mixed, norm_gain_rows, at_mid, b_mid, wall)
+    )(adapter_choice_per_tree, inputs, cotangent, mixed, norm_gain_rows, wall, a_out, a_in, a_down, adapter_second_up, adapter_second_residual)
     gr = 6 * rank
     half_rows = gr // 2
     half, hb, per = nblk // 2, BLK // 2, tok // BLK
@@ -919,15 +966,14 @@
         compiler_params=params(4, 62 << 20), name="back",
     )(d_mix, mixt, q, qt, k, kt, v, wp, xn, ranks, inputs, d_mid, scale, bp, at_qkv, norm_gain_rows, g_mid.reshape(gr, width))
 
-    count = adapter_first_input.shape[1]
     table = shape(count, rank, width, dtype=F32)
-    ga_in, gb_qkv, gb_up, ga_out, ga_down, gb_res = pl.pallas_call(
+    ga_in, gb_qkv, gb_up, ga_out, ga_down, gb_res, input_grad = pl.pallas_call(
         place_kernel,
         out_shape=[shape(4, count, rank, width, dtype=F32), shape(3, count, rank, width, dtype=F32), table, table, table,
-                   shape(2, count, rank, width, dtype=F32)],
-        in_specs=[IN_SMEM] + [IN_VMEM] * 2, out_specs=[IN_ANY] * 6,
-        scratch_shapes=[VMEM((12, count, rank, width), F32), DMA((12,))], compiler_params=params(), name="place",
-    )(choices, grads_mid, grads_attn)
+                   shape(2, count, rank, width, dtype=F32), shape(tok, width, dtype=F32)],
+        in_specs=[IN_SMEM] + [IN_VMEM] * 2 + [IN_ANY], out_specs=[IN_ANY] * 7,
+        scratch_shapes=[VMEM((12, count, rank, width), F32), DMA((13,))], compiler_params=params(), name="place",
+    )(choices, grads_mid, grads_attn, input_grad)
     return (output, input_grad, jnp.swapaxes(ga_in, 2, 3), gb_qkv, gb_up, jnp.swapaxes(ga_out, 1, 2), jnp.swapaxes(ga_down, 1, 2), gb_res)
 
 

time: 260 us -> 312 us (1.20)
  Pallas kernels: 244 us -> 310 us
  local copies, waits for them, and re-layouts: 8.1 us -> 0 us
  other arithmetic: 5.88 us -> 0 us
    pallas_call x1, Pallas kernels: 5.7 us -> 82.8 us  [local(): pl.pallas_call(place_kernel, out_shape=[shape(4, count, rank, width, dtyp...]
    pallas_call x1, Pallas kernels: 115 us -> 100 us  [local(): pl.pallas_call(functools.partial(forward_kernel, ndp, chunks), out_shape=...]
where the time goes in v4:
time: 312 us
  Pallas kernels  310 us (99%)
    pallas_call x1, Pallas kernels, local(): pl.pallas_call(functools.partial(forward_kernel, ndp, chunks), out_shape=...  100 us
    pallas_call x1, Pallas kernels, local(): pl.pallas_call(functools.partial(back_kernel, ndp), out_shape=[shape(tok,...  93.7 us
    pallas_call x1, Pallas kernels, local(): pl.pallas_call(place_kernel, out_shape=[shape(4, count, rank, width, dtyp...  82.8 us
    pallas_call x1, Pallas kernels, local(): pl.pallas_call(mid_kernel, out_shape=[shape(tok, width), shape(tok, width...  34 us

profile of v4, /device:TPU:0, one launch (start us, length us, event | category | flops | bytes accessed | tf_op | source)
XLA Modules:
  0.0 312.0 jit_solution(5053520933672259599)
XLA Ops:
  1.3 100.0 %forward.1 = (bf16[8,4,480,320]{3,2,1,0:T(8,128)(2,1)}, f32[8,8,128]{2,1,0:T(8,128)}, bf16[4,512,320]{2,1,0:T(8,128)(2,1)}, bf16[2048,1280]{1,0:T(8,128)(2,1)}, ...) custom-call(s32[1]{0:T(128)S(6)} %copy.24.choice_in.e_ref, ...), custom_call_target="tpu_custom_call" | custom-call | tf_op jit(solution)/shard_map/forward/pallas_call | solution.py:919
  101.3 34.0 %middle.1 = (bf16[512,1280]{1,0:T(8,128)(2,1)}, f32[512,1280]{1,0:T(8,128)}, bf16[4,512,320]{2,1,0:T(8,128)(2,1)}, f32[6,16,1280]{2,1,0:T(8,128)}) custom-call(s32[1]{0:T(128)S(6)} %copy.24.choice_in.e_ref, bf16[512,1280]{1,0:T(8,128)(2,1)} %x_h.1, bf16[512,1280]{1,0:T(8,128)(2,1)} %g_ref.1, bf16[4,512,320]{2,1,0:T(8,128)(2,1)} %get-tuple-element.37.mix4_ref, ...), custom_call_target="tpu_custom_call" | custom-call | tf_op jit(solution)/shard_map/middle/pallas_call | solution.py:940
  135.3 93.7 %back.1 = (f32[512,1280]{1,0:T(8,128)}, bf16[2,8,48,1280]{3,2,1,0:T(8,128)(2,1)}, bf16[2,8,48,1280]{3,2,1,0:T(8,128)(2,1)}) custom-call(bf16[4,512,320]{2,1,0:T(8,128)(2,1)} %get-tuple-element.41.dmix_ref, bf16[320,2048]{1,0:T(8,128)(2,1)} %get-tuple-element.42.mixt_h, bf16[4,2048,128]{2,1,0:T(8,128)(2,1)} %get-tuple-element.43.q_h, ...), custom_call_target="tpu_custom_call" | custom-call | tf_op jit(solution)/shard_map/back/pallas_call | solution.py:954
  229.0 82.8 %place.1 = (f32[4,8,16,1280]{3,2,1,0:T(8,128)}, f32[3,8,16,1280]{3,2,1,0:T(8,128)}, f32[8,16,1280]{2,1,0:T(8,128)}, f32[8,16,1280]{2,1,0:T(8,128)}, f32[8,16,128...) custom-call(f32[8,8,128]{2,1,0:T(8,128)} %get-tuple-element.40.e_ref, ...), custom_call_target="tpu_custom_call" | custom-call | tf_op jit(solution)/shard_map/place/pallas_call | solution.py:970

commit v5 on v4

--- a/solution.py
+++ b/solution.py
@@ -86,10 +86,34 @@
     mixt_ref[:, cols] = ot.astype(BF16)
     mix_ref[cols, :] = ot.T.astype(BF16)
 
-def spread_heads(hcols, pad):
-    c = lax.broadcasted_iota(jnp.int32, (hcols, pad), 0)
-    l = lax.broadcasted_iota(jnp.int32, (hcols, pad), 1)
-    return jnp.where(((l & 127) < HD) & ((l >> 7) * HD + (l & 127) == c), 1.0, 0.0).astype(BF16)
+def row_parts(rows):
+    return 2 if rows % 32 == 0 else 1
+
+def third_lanes(j, part, c):
+    return (j >> 6) == (part + c) % 2, (j & 63) + 256 * (1 - c)
+
+def pack_block(block, c, store):
+    rows, cols = block.shape
+    parts = row_parts(rows)
+    size = rows // parts
+    src = lax.broadcasted_iota(jnp.int32, (cols, 256), 0)
+    dst = lax.broadcasted_iota(jnp.int32, (cols, 256), 1)
+    full = dot(block, jnp.where(src == dst + 64 * c, 1.0, 0.0).astype(BF16)).astype(BF16)
+    rest = jnp.zeros((size, 128), F32)
+    for r in range(parts):
+        store(r, full[r * size:(r + 1) * size, :128])
+        store(parts + r, full[r * size:(r + 1) * size, 128:])
+        held, col = third_lanes(dst[:, :128], r, c)
+        rest = rest + dot(block[r * size:(r + 1) * size], jnp.where(held & (src[:, :128] == col), 1.0, 0.0).astype(BF16))
+    store(2 * parts, rest.astype(BF16))
+
+def spread_heads(c, parts, pad):
+    def matrix(k, held, col):
+        l = lax.broadcasted_iota(jnp.int32, (k, pad), 1)
+        return jnp.where(held & ((l & 127) < HD) & ((l >> 7) * HD + (l & 127) == col), 1.0, 0.0).astype(BF16)
+    lane = lax.broadcasted_iota(jnp.int32, (256, 1), 0)
+    rest = lax.broadcasted_iota(jnp.int32, (128, 1), 0)
+    return matrix(256, lane >= 0, lane + 64 * c), [matrix(128, *third_lanes(rest, r, c)) for r in range(parts)]
 
 def head_columns(me, pad, width):
     l = lax.broadcasted_iota(jnp.int32, (pad, width), 0)
@@ -267,7 +291,7 @@
 class FullGather:
     def __init__(self, me, own, buf, send, first, recv):
         self.me, self.own, self.buf, self.send, self.first, self.recv = me, own, buf, send, first, recv
-        cut = own.shape[0] // 48 * 16
+        cut = own.shape[0] // 3
         self.parts = (pl.ds(0, cut), pl.ds(cut, own.shape[0] - cut))
 
     def copy(self, h, o, t, d2, t2, kind, own=False):
@@ -371,13 +395,12 @@
 def forward_kernel(ndp, chunks, choice_in, len_ref, par_ref, x_ref, gain_ref, qs_ref, ain_h, btab_h, a_ref, wo_ref, wf_ref,
                    wout_ref, cho_ref, mixed_ref, xno_ref, qo_ref, qto_ref, ko_ref, kto_ref, vo_ref, ranko_ref, mixto_ref, wpo_ref, bpo_ref, ato_ref, scaleo_ref,
                    ain_ref, btab_ref, choice_ref, at_ref, scale_ref, seg_ref, mq_ref, put_ref,
-                   aown_ref, wown_ref, xn_ref, wa_ref, wp_ref, bp_ref, q_ref, qt_ref, k_ref, kt_ref, v_ref, vt_ref, rank_ref, mixt_ref,
+                   araw_ref, wraw_ref, aown_ref, wown_ref, xn_ref, wa_ref, wp_ref, bp_ref, q_ref, qt_ref, k_ref, kt_ref, v_ref, vt_ref, rank_ref, mixt_ref,
                    mix_ref, m_ref, acc_ref, ls, os, xs, xr, a_s, a_r, c_s, c_r, w_s, w_f, w_r, ms, mr):
     me = Place(ndp)
     tok, width = x_ref.shape
-    rows_o = wo_ref.shape[0]
-    loads = [pltpu.make_async_copy(a_ref, aown_ref, ls.at[0]), pltpu.make_async_copy(wo_ref, wown_ref.at[pl.ds(0, rows_o)], ls.at[1]),
-             pltpu.make_async_copy(wf_ref, wown_ref.at[pl.ds(rows_o, wf_ref.shape[0])], ls.at[2])]
+    loads = [pltpu.make_async_copy(a_ref, araw_ref, ls.at[0]), pltpu.make_async_copy(wo_ref, wraw_ref.at[0], ls.at[1]),
+             pltpu.make_async_copy(wf_ref, wraw_ref.at[pl.ds(1, 2)], ls.at[2])]
     tables = [pltpu.make_async_copy(ain_h.at[pl.ds(0, 3)], ain_ref, ls.at[3]), pltpu.make_async_copy(btab_h, btab_ref, ls.at[4])]
     for copy in loads + tables:
         copy.start()
@@ -399,11 +422,21 @@
         xcopy(me.t, c, me.t1, 1).start()
     for copy in loads:
         copy.wait()
+    pieces = aown_ref.shape[1]
+
+    def pack(raw_ref, own_ref, n, index):
+        def store(k, v):
+            own_ref[index(n, k)] = v
+        pack_block(raw_ref[n], me.c, store)
+    for n in range(3):
+        pack(araw_ref, aown_ref, n, lambda n, k: (n, k))
     parts = [PairLine(me, aown_ref.at[n], wa_ref, a_s, a_r, n) for n in range(3)]
     ch = PairLine(me, choice_ref, cho_ref, c_s, c_r)
     w = FullGather(me, wown_ref, wout_ref, w_s, w_f, w_r)
     parts[0].start()
     parts[1].start()
+    for n in range(3):
+        pack(wraw_ref, wown_ref, n, lambda n, k: n * pieces + k)
     keep = [pltpu.make_async_copy(wown_ref, wout_ref.at[me.d, me.t], ls.at[0]), pltpu.make_async_copy(choice_ref, cho_ref.at[me.d], ls.at[1])]
     for copy in keep:
         copy.start()
@@ -445,9 +478,24 @@
         forward(c)
     nblk = xn_ref.shape[0] // BLK
     near = nblk // 2
-    wrows = wa_ref.shape[2]
-    group = 16 // math.gcd(wrows, 16)
-    sel = spread_heads(wa_ref.shape[3], wp_ref.shape[2])
+    half_rows = wa_ref.shape[3]
+    sides = pieces // 2
+    wrows = half_rows * sides
+    sel, sel_rest = spread_heads(me.c, sides, wp_ref.shape[2])
+
+    def spread_weights(s):
+        if sides == 1:
+            group = 16 // math.gcd(wrows, 16)
+            for o in range(0, ndp, group):
+                wp_ref[s, o * wrows:(o + group) * wrows] = jnp.concatenate([
+                    dot(jnp.concatenate([wa_ref[o + j, s, 0], wa_ref[o + j, s, 1]], axis=1), sel) + dot(wa_ref[o + j, s, 2], sel_rest[0])
+                    for j in range(group)], axis=0).astype(BF16)
+            return
+        flat = [wa_ref[:, s, k].reshape(ndp * half_rows, 128) for k in range(pieces)]
+        for r in range(sides):
+            y = (dot(jnp.concatenate([flat[r], flat[sides + r]], axis=1), sel) + dot(flat[2 * sides], sel_rest[r])).astype(BF16)
+            for o in range(ndp):
+                wp_ref[s, o * wrows + r * half_rows:o * wrows + (r + 1) * half_rows] = y[o * half_rows:(o + 1) * half_rows]
 
     def project_blocks(first, s):
         n_ref, t_ref = ((q_ref, qt_ref), (k_ref, kt_ref), (v_ref, vt_ref))[s]
@@ -457,8 +505,7 @@
         xcopy(me.t1, c, me.t1, 2).wait_recv()
     for s in range(3):
         parts[s].pair_arrivals()
-        for o in range(0, ndp, group):
-            wp_ref[s, o * wrows:(o + group) * wrows] = jnp.concatenate([dot(wa_ref[o + j, s], sel) for j in range(group)], axis=0).astype(BF16)
+        spread_weights(s)
         project_blocks(me.y * near, s)
         if s < 2:
             forward(chunks // 2 + s)
@@ -541,8 +588,9 @@
     step = 256
     part = mix4_ref.shape[2]
     blocks = (wb0_ref, wb1_ref, wb2_ref)
-    ndp, nt, wrows = wb0_ref.shape[:3]
-    loads = [pltpu.make_async_copy(wall_ref.at[:, :, pl.ds(n * wrows, wrows)], blocks[n], ls.at[n]) for n in range(3)]
+    ndp, nt, pieces, size = wb0_ref.shape[:4]
+    sides = pieces // 2
+    loads = [pltpu.make_async_copy(wall_ref.at[:, :, pl.ds(n * pieces, pieces)], blocks[n], ls.at[n]) for n in range(3)]
     e = e_ref[0]
     tables = [pltpu.make_async_copy(src, dst, ts.at[n]) for n, (src, dst) in enumerate((
         (aout_h.at[e], at_ref.at[0]), (ain_h.at[3, e], at_ref.at[1]), (adown_h.at[e], at_ref.at[2]),
@@ -554,9 +602,22 @@
 
     def assemble(n):
         loads[n].wait()
+        low_lane = lax.broadcasted_iota(jnp.int32, (size, 128), 1) < 64
+
+        def block(o, y, even, odd):
+            for r in range(sides):
+                rows = pl.ds((o * sides + r) * size, size)
+                base = 2 * part * y
+                w_ref[n, rows, base:base + 128] = even[r]
+                w_ref[n, rows, base + 128:base + 256] = even[sides + r]
+                first, second = (even, odd) if r == 0 else (odd, even)
+                both = jnp.where(low_lane, first[2 * sides].astype(F32), second[2 * sides].astype(F32))
+                w_ref[n, rows, base + 256:base + 384] = (both if r == 0 else pltpu.roll(both, 64, 1)).astype(BF16)
+                w_ref[n, rows, base + 384:base + 512] = odd[r]
+                w_ref[n, rows, base + 512:base + 640] = odd[sides + r]
         for o in range(ndp):
-            for t in range(nt):
-                w_ref[n, o * wrows:(o + 1) * wrows, t * part:(t + 1) * part] = blocks[n][o, t]
+            for y in range(nt // 2):
+                block(o, y, blocks[n].at[o, 2 * y], blocks[n].at[o, 2 * y + 1])
 
     for t in range(mix4_ref.shape[0]):
         mix_ref[:, t * part:(t + 1) * part] = mix4_ref[t]
@@ -859,13 +920,12 @@
     put_ig.wait()
 
 
-def place_kernel(e_ref, gm_ref, ga_ref, ig_in, ain_h, bqkv_h, bup_h, aout_h, adown_h, bres_h, ig_out, out_ref, sem):
+def place_kernel(e_ref, gm_ref, ga_ref, ain_h, bqkv_h, bup_h, aout_h, adown_h, bres_h, out_ref, sem):
     ndp = gm_ref.shape[1]
     slots = ([(ga_ref, 0, n, ain_h.at[n]) for n in range(3)] + [(ga_ref, 1, n, bqkv_h.at[n]) for n in range(3)]
              + [(gm_ref, 0, 0, ain_h.at[3]), (gm_ref, 0, 1, bup_h), (gm_ref, 0, 2, aout_h),
                 (gm_ref, 1, 0, adown_h), (gm_ref, 1, 1, bres_h.at[0]), (gm_ref, 1, 2, bres_h.at[1])])
-    copies = [pltpu.make_async_copy(ig_in, ig_out, sem.at[len(slots)])]
-    copies[0].start()
+    copies = []
     for n, (src, c, k, dst) in enumerate(slots):
         out_ref[n] = jnp.zeros(out_ref.shape[1:], F32)
 
@@ -914,18 +974,21 @@
 
     chunks = 4
     count = a_in.shape[1]
-    wr = wrows * 3
+    sides = row_parts(wrows)
+    packed = (2 * sides + 1, wrows // sides, 128)
+    flat = (3 * packed[0],) + packed[1:]
     tall = (heads, tree, 128)
     wall, choices, mixed, xn, q, qt, k, kt, v, ranks, mixt, wp, bp, at_qkv, scale = pl.pallas_call(
         functools.partial(forward_kernel, ndp, chunks),
-        out_shape=[shape(ndp, nt, wr, hcols), shape(ndp, 8, 128, dtype=F32), shape(nt, tok, hcols), shape(tree, width),
+        out_shape=[shape(ndp, nt, *flat), shape(ndp, 8, 128, dtype=F32), shape(nt, tok, hcols), shape(tree, width),
                    shape(*tall), shape(heads, 128, tree), shape(*tall), shape(heads, HD, tree), shape(*tall),
                    shape(tree, 3 * rank), shape(hcols, tree), shape(3, width, pad), shape(3, 3 * rank, pad), shape(3 * rank, width),
                    shape(1, pad, dtype=F32)],
         in_specs=[IN_SMEM] * 3 + [IN_VMEM] * 3 + [IN_ANY] * 5, out_specs=[IN_ANY] * 15,
         scratch_shapes=[VMEM((3, count, rank, width), BF16), VMEM((3, count, rank, width), BF16), VMEM((8, 128), F32), VMEM((3 * rank, width), BF16),
                         VMEM((1, pad), F32), VMEM((8, 128), F32), VMEM((128, 128), BF16), VMEM((pad, width), BF16),
-                        VMEM((3, wrows, hcols), BF16), VMEM((wr, hcols), BF16), VMEM((tree, width), BF16), VMEM((ndp, 3, wrows, hcols), BF16),
+                        VMEM((3, wrows, hcols), BF16), VMEM((3, wrows, hcols), BF16), VMEM((3, *packed), BF16), VMEM(flat, BF16), VMEM((tree, width), BF16),
+                        VMEM((ndp, 3, *packed), BF16),
                         VMEM((3, width, pad), BF16), VMEM((3, 3 * rank, pad), BF16), VMEM(tall, BF16), VMEM((heads, 128, tree), BF16),
                         VMEM(tall, BF16), VMEM((heads, HD, tree), BF16), VMEM(tall, BF16), VMEM((heads, HD + 16, tree), BF16),
                         VMEM((tree, 3 * rank), BF16), VMEM((hcols, tree), BF16), VMEM((tree, hcols), BF16),
@@ -935,7 +998,7 @@
         compiler_params=params(1), name="forward",
     )(adapter_choice_per_tree, segment_lengths, segment_parents, inputs, norm_gain_rows, query_dimension_scale[None, :], a_in,
       adapter_second_attention, attention_weights, output_weight,
-      feedforward_weights.reshape(2 * wrows, hcols))
+      feedforward_weights)
 
     output, d_mid, d_mix, g_mid = pl.pallas_call(
         mid_kernel,
@@ -943,7 +1006,7 @@
         in_specs=[IN_SMEM] + [IN_VMEM] * 4 + [IN_ANY] * 6, out_specs=[IN_VMEM] * 4,
         scratch_shapes=[VMEM((3, rank, width), BF16), VMEM((3, rank, width), BF16), DMA((6,)), VMEM((tok, width), BF16), VMEM((tok, width), F32), VMEM((tok, width), BF16), VMEM((tok, width), F32),
                         VMEM((tok, width), BF16), VMEM((tok, width), F32), VMEM((tok, width), BF16), VMEM((3, width, width), BF16)]
-        + [VMEM((ndp, nt, wrows, hcols), BF16)] * 3 + [DMA((3,))],
+        + [VMEM((ndp, nt, *packed), BF16)] * 3 + [DMA((3,))],
         compiler_params=params(), name="middle",
     )(adapter_choice_per_tree, inputs, cotangent, mixed, norm_gain_rows, wall, a_out, a_in, a_down, adapter_second_up, adapter_second_residual)
     gr = 6 * rank
@@ -967,13 +1030,13 @@
     )(d_mix, mixt, q, qt, k, kt, v, wp, xn, ranks, inputs, d_mid, scale, bp, at_qkv, norm_gain_rows, g_mid.reshape(gr, width))
 
     table = shape(count, rank, width, dtype=F32)
-    ga_in, gb_qkv, gb_up, ga_out, ga_down, gb_res, input_grad = pl.pallas_call(
+    ga_in, gb_qkv, gb_up, ga_out, ga_down, gb_res = pl.pallas_call(
         place_kernel,
         out_shape=[shape(4, count, rank, width, dtype=F32), shape(3, count, rank, width, dtype=F32), table, table, table,
-                   shape(2, count, rank, width, dtype=F32), shape(tok, width, dtype=F32)],
-        in_specs=[IN_SMEM] + [IN_VMEM] * 2 + [IN_ANY], out_specs=[IN_ANY] * 7,
-        scratch_shapes=[VMEM((12, count, rank, width), F32), DMA((13,))], compiler_params=params(), name="place",
-    )(choices, grads_mid, grads_attn, input_grad)
+                   shape(2, count, rank, width, dtype=F32)],
+        in_specs=[IN_SMEM] + [IN_VMEM] * 2, out_specs=[IN_ANY] * 6,
+        scratch_shapes=[VMEM((12, count, rank, width), F32), DMA((12,))], compiler_params=params(), name="place",
+    )(choices, grads_mid, grads_attn)
     return (output, input_grad, jnp.swapaxes(ga_in, 2, 3), gb_qkv, gb_up, jnp.swapaxes(ga_out, 1, 2), jnp.swapaxes(ga_down, 1, 2), gb_res)
 
 

time: 312 us -> 229 us (0.73)
  Pallas kernels: 310 us -> 226 us
    pallas_call x1, Pallas kernels: 82.8 us -> 5.7 us  [local(): pl.pallas_call(place_kernel, out_shape=[shape(4, count, rank, width, dtyp...]
    pallas_call x1, Pallas kernels: 100 us -> 92.1 us  [local(): pl.pallas_call(functools.partial(forward_kernel, ndp, chunks), out_shape=...]
where the time goes in v5:
time: 229 us
  Pallas kernels  226 us (99%)
    pallas_call x1, Pallas kernels, local(): pl.pallas_call(functools.partial(back_kernel, ndp), out_shape=[shape(tok,...  95 us
    pallas_call x1, Pallas kernels, local(): pl.pallas_call(functools.partial(forward_kernel, ndp, chunks), out_shape=...  92.1 us
    pallas_call x1, Pallas kernels, local(): pl.pallas_call(mid_kernel, out_shape=[shape(tok, width), shape(tok, width...  33.1 us
    pallas_call x1, Pallas kernels, local(): pl.pallas_call(place_kernel, out_shape=[shape(4, count, rank, width, dtyp...  5.7 us

profile of v5, /device:TPU:0, one launch (start us, length us, event | category | flops | bytes accessed | tf_op | source)
XLA Modules:
  0.0 228.8 jit_solution(16222908781012013497)
XLA Ops:
  1.3 92.1 %forward.1 = (bf16[8,4,15,80,128]{4,3,2,1,0:T(8,128)(2,1)}, f32[8,8,128]{2,1,0:T(8,128)}, bf16[4,512,320]{2,1,0:T(8,128)(2,1)}, bf16[2048,1280]{1,0:T(8,128)(2,1...) custom-call(s32[1]{0:T(128)S(6)} %copy.25.choice_in.e_ref, ...), custom_call_target="tpu_custom_call" | custom-call | tf_op jit(solution)/shard_map/forward/pallas_call | solution.py:981
  93.4 33.1 %middle.1 = (bf16[512,1280]{1,0:T(8,128)(2,1)}, f32[512,1280]{1,0:T(8,128)}, bf16[4,512,320]{2,1,0:T(8,128)(2,1)}, f32[6,16,1280]{2,1,0:T(8,128)}) custom-call(s32[1]{0:T(128)S(6)} %copy.25.choice_in.e_ref, bf16[512,1280]{1,0:T(8,128)(2,1)} %x_h.1, bf16[512,1280]{1,0:T(8,128)(2,1)} %g_ref.1, bf16[4,512,320]{2,1,0:T(8,128)(2,1)} %get-tuple-element.36.mix4_ref, ...), custom_call_target="tpu_custom_call" | custom-call | tf_op jit(solution)/shard_map/middle/pallas_call | solution.py:1003
  126.6 95.0 %back.1 = (f32[512,1280]{1,0:T(8,128)}, bf16[2,8,48,1280]{3,2,1,0:T(8,128)(2,1)}, bf16[2,8,48,1280]{3,2,1,0:T(8,128)(2,1)}) custom-call(bf16[4,512,320]{2,1,0:T(8,128)(2,1)} %get-tuple-element.39.dmix_ref, bf16[320,2048]{1,0:T(8,128)(2,1)} %get-tuple-element.40.mixt_h, bf16[4,2048,128]{2,1,0:T(8,128)(2,1)} %get-tuple-element.41.q_h, ...), custom_call_target="tpu_custom_call" | custom-call | tf_op jit(solution)/shard_map/back/pallas_call | solution.py:1017
  221.6 0.0 copy-start
  221.6 5.7 %place.1 = (f32[4,8,16,1280]{3,2,1,0:T(8,128)}, f32[3,8,16,1280]{3,2,1,0:T(8,128)}, f32[8,16,1280]{2,1,0:T(8,128)}, f32[8,16,1280]{2,1,0:T(8,128)}, f32[8,16,1280]{2,1,0:T(8,128)}, /*index=5*/f32[2,8,16,1280]{3,2,1,0:T(8,128)}) custom-call(f32[8,8,128]{2,1,0:T(8,128)} %get-tuple-element.55.e_ref, bf16[2,8,48,1280]{3,2,1,0:T(8,128)(2,1)} %get-tuple-element.56.gm_ref, ...), custom_call_target="tpu_custom_call" | custom-call | tf_op jit(solution)/shard_map/place/pallas_call | solution.py:1033
  227.3 0.0 copy-done
  227.3 1.5 copy.26
Async XLA Ops:
  221.6 5.7 %copy-start = (f32[512,1280]{1,0:T(8,128)S(1)}, f32[512,1280]{1,0:T(8,128)}, u32[]{:S(2)}) copy-start(f32[512,1280]{1,0:T(8,128)} %get-tuple-element.73) | copy-start | bytes 7864324

commit v6 on v5

--- a/solution.py
+++ b/solution.py
@@ -43,7 +43,7 @@
         n_ref[h, rows, :] = yh.astype(BF16)
         t_ref[h, :, rows] = yh.T[:t_ref.shape[1]].astype(BF16)
 
-def attend_block(i, qt_ref, k_ref, vt_ref, m_ref, acc_ref, mixt_ref, mix_ref, count=None, jlist=None):
+def attend_block(i, c, qt_ref, k_ref, vt_ref, m_ref, acc_ref, mixt_ref, mix_ref):
     heads = qt_ref.shape[0]
     cols = pl.ds(pl.multiple_of(i * BLK, BLK), BLK)
     m_ref[...] = jnp.full_like(m_ref, -3e38)
@@ -63,10 +63,7 @@
         for h in hs:
             acc_ref[h] = accs[h]
             m_ref[h] = news[h]
-    if jlist is None:
-        lax.fori_loop(0, i, lambda j, c: (step(j, False), c)[1], 0)
-    else:
-        lax.fori_loop(0, count, lambda n, c: (step(jlist(n), False), c)[1], 0)
+    lax.fori_loop(0, i, lambda j, n: (step(j, False), n)[1], 0)
     step(i, True)
     outs = []
     for h in range(heads):
@@ -84,7 +81,14 @@
         outs.append(o)
     ot = jnp.concatenate(outs, axis=0)
     mixt_ref[:, cols] = ot.astype(BF16)
-    mix_ref[cols, :] = ot.T.astype(BF16)
+    half = BLK // 2
+    full = jnp.where(c == 0, ot[:256], ot[64:]).T.astype(BF16)
+    rest = jnp.where(c == 0, ot[256:], ot[:64])
+    first, second = rest[:, :half], rest[:, half:]
+    for r in range(2):
+        for k in range(2):
+            mix_ref[i, 2 * k + r] = full[r * half:(r + 1) * half, k * 128:(k + 1) * 128]
+    mix_ref[i, 4] = jnp.concatenate([jnp.where(c == 0, first, second), jnp.where(c == 0, second, first)], axis=0).T.astype(BF16)
 
 def row_parts(rows):
     return 2 if rows % 32 == 0 else 1
@@ -142,10 +146,15 @@
     inside = (row >= 0) & (row < segs) & (lane >= 0) & (lane < segs)
     mq_ref[...] = jnp.where(inside & jnp.logical_not(reach), -BIG, 0.0).astype(BF16)
 
-def bwd_prep(b, dm_ref, mixt_ref, do_ref, dot_ref):
+def bwd_prep(b, c, dm_ref, mixt_ref, do_ref, dot_ref):
     rows = pl.ds(pl.multiple_of(b * BLK, BLK), BLK)
     heads = do_ref.shape[0]
-    dt = dm_ref[rows, :].astype(F32).T
+    t, i = b // dm_ref.shape[1], b % dm_ref.shape[1]
+    full = [jnp.concatenate([dm_ref[t, i, 2 * k + r].astype(F32).T for r in range(2)], axis=1) for k in range(2)]
+    rest = dm_ref[t, i, 4].astype(F32).T
+    low, high = rest[:64], rest[64:]
+    rest = jnp.concatenate([jnp.where(c == 0, low, high), jnp.where(c == 0, high, low)], axis=1)
+    dt = jnp.where(c == 0, jnp.concatenate(full + [rest], axis=0), jnp.concatenate([rest] + full, axis=0))
     prod = dt * mixt_ref[:, rows].astype(F32)
     r = lax.broadcasted_iota(jnp.int32, (16, BLK), 0)
     for h in range(heads):
@@ -531,11 +540,10 @@
     per = tok // BLK
 
     def piece(i):
-        rows = pl.ds(pl.multiple_of(i * BLK, BLK), BLK)
-        return mix_ref.at[rows], mixed_ref.at[me.t, pl.ds(pl.multiple_of((i % per) * BLK, BLK), BLK)], i // per
+        return mix_ref.at[i], mixed_ref.at[me.t, i % per], i // per
 
     def attend_step(i, c):
-        attend_block(i, qt_ref, k_ref, vt_ref, m_ref, acc_ref, mixt_ref, mix_ref)
+        attend_block(i, me.c, qt_ref, k_ref, vt_ref, m_ref, acc_ref, mixt_ref, mix_ref)
         src, dst, t = piece(i)
         @pl.when(t == me.t)
         def _():
@@ -554,7 +562,7 @@
     ch.pair_arrivals()
     for t in (me.t1, me.t2, me.t3):
         for h in range(per):
-            dst = mixed_ref.at[t, pl.ds(h * BLK, BLK)]
+            dst = mixed_ref.at[t, h]
             remote(dst, dst, ms.at[0], mr.at[t, h], me.d, t).wait_recv()
     w.finish()
     for part in parts:
@@ -586,7 +594,7 @@
                at_ref, b_ref, ts, mix_ref, mid_ref, hid_ref, up_ref, act_ref, f_ref, low_ref, w_ref, wb0_ref, wb1_ref, wb2_ref, ls):
     width = x_ref.shape[1]
     step = 256
-    part = mix4_ref.shape[2]
+    part = width // mix4_ref.shape[0]
     blocks = (wb0_ref, wb1_ref, wb2_ref)
     ndp, nt, pieces, size = wb0_ref.shape[:4]
     sides = pieces // 2
@@ -600,27 +608,31 @@
     for copy in tables:
         copy.wait()
 
+    def join(dst_ref, first_part, y, even, odd):
+        pieces, size = even.shape[:2]
+        sides = pieces // 2
+        low_lane = lax.broadcasted_iota(jnp.int32, (size, 128), 1) < 64
+        base = 2 * part * y
+        for r in range(sides):
+            rows = pl.ds((first_part + r) * size, size)
+            dst_ref[rows, base:base + 128] = even[r]
+            dst_ref[rows, base + 128:base + 256] = even[sides + r]
+            first, second = (even, odd) if r == 0 else (odd, even)
+            both = jnp.where(low_lane, first[2 * sides].astype(F32), second[2 * sides].astype(F32))
+            dst_ref[rows, base + 256:base + 384] = (both if r == 0 else pltpu.roll(both, 64, 1)).astype(BF16)
+            dst_ref[rows, base + 384:base + 512] = odd[r]
+            dst_ref[rows, base + 512:base + 640] = odd[sides + r]
+
     def assemble(n):
         loads[n].wait()
-        low_lane = lax.broadcasted_iota(jnp.int32, (size, 128), 1) < 64
-
-        def block(o, y, even, odd):
-            for r in range(sides):
-                rows = pl.ds((o * sides + r) * size, size)
-                base = 2 * part * y
-                w_ref[n, rows, base:base + 128] = even[r]
-                w_ref[n, rows, base + 128:base + 256] = even[sides + r]
-                first, second = (even, odd) if r == 0 else (odd, even)
-                both = jnp.where(low_lane, first[2 * sides].astype(F32), second[2 * sides].astype(F32))
-                w_ref[n, rows, base + 256:base + 384] = (both if r == 0 else pltpu.roll(both, 64, 1)).astype(BF16)
-                w_ref[n, rows, base + 384:base + 512] = odd[r]
-                w_ref[n, rows, base + 512:base + 640] = odd[sides + r]
+        dst = w_ref.at[n]
         for o in range(ndp):
             for y in range(nt // 2):
-                block(o, y, blocks[n].at[o, 2 * y], blocks[n].at[o, 2 * y + 1])
-
-    for t in range(mix4_ref.shape[0]):
-        mix_ref[:, t * part:(t + 1) * part] = mix4_ref[t]
+                join(dst, o * sides, y, blocks[n].at[o, 2 * y], blocks[n].at[o, 2 * y + 1])
+
+    for y in range(nt // 2):
+        for i in range(mix4_ref.shape[1]):
+            join(mix_ref, 2 * i, y, mix4_ref.at[2 * y, i], mix4_ref.at[2 * y + 1, i])
 
     def cols(n):
         return pl.ds(pl.multiple_of(n * step, step), step)
@@ -684,8 +696,21 @@
     def mixed_back(n):
         act_ref[:, n] = (dot(low_ref[...], w_ref[0, :, n]) + dot(dz_out, at_ref[0, :, n])).astype(BF16)
     each(mixed_back)
-    for t in range(dmix_ref.shape[0]):
-        dmix_ref[t] = act_ref[:, t * part:(t + 1) * part]
+    half = dmix_ref.shape[3]
+    low_lane = lax.broadcasted_iota(jnp.int32, (half, 128), 1) < 64
+    for y in range(nt // 2):
+        base = 2 * part * y
+        for i in range(dmix_ref.shape[1]):
+            halves = [pl.ds((2 * i + r) * half, half) for r in range(2)]
+            for r in range(2):
+                dmix_ref[2 * y, i, r] = act_ref[halves[r], base:base + 128]
+                dmix_ref[2 * y, i, 2 + r] = act_ref[halves[r], base + 128:base + 256]
+                dmix_ref[2 * y + 1, i, r] = act_ref[halves[r], base + 384:base + 512]
+                dmix_ref[2 * y + 1, i, 2 + r] = act_ref[halves[r], base + 512:base + 640]
+            top = act_ref[halves[0], base + 256:base + 384].astype(F32)
+            turned = pltpu.roll(act_ref[halves[1], base + 256:base + 384].astype(F32), 64, 1)
+            dmix_ref[2 * y, i, 4] = jnp.where(low_lane, top, turned).astype(BF16)
+            dmix_ref[2 * y + 1, i, 4] = jnp.where(low_lane, turned, top).astype(BF16)
 
 
 class GradSum:
@@ -742,8 +767,9 @@
                 ms, mr, mls, mlr, mfs, mfr, mk, as_, ar, als, alr, afs, afr, ak):
     me = Place(ndp)
     tok = x_ref.shape[0]
-    nblk = dm_ref.shape[0] // BLK
-    per, half, hb = tok // BLK, nblk // 2, BLK // 2
+    per, hb = tok // BLK, BLK // 2
+    nblk = per * dm_ref.shape[0]
+    half = nblk // 2
     heads = q_ref.shape[0]
     loads = [pltpu.make_async_copy(src, dst, lsem.at[n]) for n, (src, dst) in enumerate((
         (mixt_h, mixt_ref), (q_h, q_ref), (qt_h, qt_ref), (k_h, k_ref), (kt_h, kt_ref), (v_h, v_ref),
@@ -753,13 +779,10 @@
         gpm[c] = gmid_ref[c * n48:(c + 1) * n48].astype(BF16)
     greet(me, tensor=(me.t1, me.t2, me.t3), pair=True, line=True)
 
-    def token_rows(t):
-        return pl.ds(pl.multiple_of(t * tok, tok), tok)
-
     def swap(n, t):
-        return remote(dmix_ref.at[t], dm_ref.at[token_rows(me.t)], dsem.at[n], drecv.at[me.t], me.d, t)
-
-    own = pltpu.make_async_copy(dmix_ref.at[me.t], dm_ref.at[token_rows(me.t)], dsem.at[3])
+        return remote(dmix_ref.at[t], dm_ref.at[me.t], dsem.at[n], drecv.at[me.t], me.d, t)
+
+    own = pltpu.make_async_copy(dmix_ref.at[me.t], dm_ref.at[me.t], dsem.at[3])
     for n, t in enumerate((me.t3, me.t2, me.t1)):
         swap(n, t).start()
     own.start()
@@ -775,27 +798,38 @@
         copy.wait()
 
     def prep(t):
-        lax.fori_loop(t * per, (t + 1) * per, lambda b, c: (bwd_prep(b, dm_ref, mixt_ref, do_ref, dot_ref), c)[1], 0)
+        lax.fori_loop(t * per, (t + 1) * per, lambda b, c: (bwd_prep(b, me.c, dm_ref, mixt_ref, do_ref, dot_ref), c)[1], 0)
+
+    args = (q_ref, qt_ref, k_ref, kt_ref, v_ref, do_ref, dot_ref, dqt_ref, dk_ref, dv_ref)
+
+    def block(a):
+        return (1 - me.y) * (nblk - 1 - a) + me.y * a
+
+    def pairs(a):
+        b = block(a)
+        bwd_pair(b, b, True, *args)
+
+        def other(n, c):
+            bwd_pair(b + me.y * (1 + n), b - (1 - me.y) * (1 + n), False, *args)
+            return c
+        lax.fori_loop(0, nblk - 1 - a, other, 0)
 
     def arrived(t):
-        remote(dmix_ref.at[t], dm_ref.at[token_rows(t)], dsem.at[0], drecv.at[t], me.d, t).wait_recv()
+        remote(dmix_ref.at[t], dm_ref.at[t], dsem.at[0], drecv.at[t], me.d, t).wait_recv()
 
     own.wait()
     prep(me.t)
     arrived(me.t1)
     prep(me.t1)
     gm.second()
+    lax.fori_loop(half, nblk, lambda a, c: (pairs(a), c)[1], 0)
     arrived(me.t2)
     prep(me.t2)
     arrived(me.t3)
     prep(me.t3)
     for copy in loads[6:]:
         copy.wait()
-    args = (q_ref, qt_ref, k_ref, kt_ref, v_ref, do_ref, dot_ref, dqt_ref, dk_ref, dv_ref)
     lane = lax.broadcasted_iota(jnp.int32, (BLK, 128), 1)
-
-    def block(a):
-        return (1 - me.y) * (nblk - 1 - a) + me.y * a
 
     def exchange(a):
         rows = pl.ds(pl.multiple_of((1 - me.c) * hb, hb), hb)
@@ -838,15 +872,6 @@
     def upto(a):
         return 1 + jnp.minimum(a * (me.line - 1) // (nblk - 2), me.line - 1)
 
-    def pairs(a):
-        b = block(a)
-        bwd_pair(b, b, True, *args)
-
-        def other(n, c):
-            bwd_pair(b + me.y * (1 + n), b - (1 - me.y) * (1 + n), False, *args)
-            return c
-        lax.fori_loop(0, nblk - 1 - a, other, 0)
-
     def far_step(a, c):
         pairs(a)
         @pl.when(a > 0)
@@ -862,11 +887,10 @@
     lax.fori_loop(0, half, far_step, 0)
 
     def near_step(a, c):
-        pairs(a)
+        final(a)
         @pl.when(a == half)
         def _():
             pass_on(a - 1)
-        final(a)
         @pl.when(jnp.logical_not(is_mine(a)))
         def _():
             own_block(a).start()
@@ -973,6 +997,8 @@
     a_in, a_out, a_down = (jnp.swapaxes(table, -1, -2) for table in (adapter_first_input, adapter_first_output, adapter_first_down))
 
     chunks = 4
+    halves = (5, BLK // 2, 128)
+    swapped = (nt, tok // BLK) + halves
     count = a_in.shape[1]
     sides = row_parts(wrows)
     packed = (2 * sides + 1, wrows // sides, 128)
@@ -980,7 +1006,7 @@
     tall = (heads, tree, 128)
     wall, choices, mixed, xn, q, qt, k, kt, v, ranks, mixt, wp, bp, at_qkv, scale = pl.pallas_call(
         functools.partial(forward_kernel, ndp, chunks),
-        out_shape=[shape(ndp, nt, *flat), shape(ndp, 8, 128, dtype=F32), shape(nt, tok, hcols), shape(tree, width),
+        out_shape=[shape(ndp, nt, *flat), shape(ndp, 8, 128, dtype=F32), shape(*swapped), shape(tree, width),
                    shape(*tall), shape(heads, 128, tree), shape(*tall), shape(heads, HD, tree), shape(*tall),
                    shape(tree, 3 * rank), shape(hcols, tree), shape(3, width, pad), shape(3, 3 * rank, pad), shape(3 * rank, width),
                    shape(1, pad, dtype=F32)],
@@ -991,7 +1017,7 @@
                         VMEM((ndp, 3, *packed), BF16),
                         VMEM((3, width, pad), BF16), VMEM((3, 3 * rank, pad), BF16), VMEM(tall, BF16), VMEM((heads, 128, tree), BF16),
                         VMEM(tall, BF16), VMEM((heads, HD, tree), BF16), VMEM(tall, BF16), VMEM((heads, HD + 16, tree), BF16),
-                        VMEM((tree, 3 * rank), BF16), VMEM((hcols, tree), BF16), VMEM((tree, hcols), BF16),
+                        VMEM((tree, 3 * rank), BF16), VMEM((hcols, tree), BF16), VMEM((nblk, *halves), BF16),
                         VMEM((heads, 1, BLK), F32), VMEM((heads, HD + 16, BLK), F32), DMA((5,)), DMA((12,)),
                         DMA((3, chunks)), DMA((nt, chunks)), DMA((3, ndp, 3)), DMA((ndp, 3)), DMA((3, ndp)), DMA((ndp,)),
                         DMA((2, ndp, nt, 4)), DMA((2,)), DMA((2, ndp, nt)), DMA((nblk,)), DMA((nt, tok // BLK))],
@@ -1002,7 +1028,7 @@
 
     output, d_mid, d_mix, g_mid = pl.pallas_call(
         mid_kernel,
-        out_shape=[shape(tok, width), shape(tok, width, dtype=F32), shape(nt, tok, hcols), shape(6, rank, width, dtype=F32)],
+        out_shape=[shape(tok, width), shape(tok, width, dtype=F32), shape(*swapped), shape(6, rank, width, dtype=F32)],
         in_specs=[IN_SMEM] + [IN_VMEM] * 4 + [IN_ANY] * 6, out_specs=[IN_VMEM] * 4,
         scratch_shapes=[VMEM((3, rank, width), BF16), VMEM((3, rank, width), BF16), DMA((6,)), VMEM((tok, width), BF16), VMEM((tok, width), F32), VMEM((tok, width), BF16), VMEM((tok, width), F32),
                         VMEM((tok, width), BF16), VMEM((tok, width), F32), VMEM((tok, width), BF16), VMEM((3, width, width), BF16)]
@@ -1020,7 +1046,7 @@
         in_specs=[IN_ANY] * 12 + [IN_VMEM] * 5, out_specs=[IN_ANY] * 3,
         scratch_shapes=[VMEM((hcols, tree), BF16), VMEM(tall, BF16), VMEM((heads, 128, tree), BF16), VMEM(tall, BF16), VMEM((heads, HD, tree), BF16),
                         VMEM(tall, BF16), VMEM((3, width, pad), BF16), VMEM((tree, width), BF16), VMEM((tree, 3 * rank), BF16),
-                        VMEM((tok, width), BF16), VMEM((tok, width), F32), VMEM((tree, hcols), BF16), VMEM(tall, BF16), VMEM((heads, 128, tree), BF16),
+                        VMEM((tok, width), BF16), VMEM((tok, width), F32), VMEM(swapped, BF16), VMEM(tall, BF16), VMEM((heads, 128, tree), BF16),
                         VMEM((heads, HD, tree), F32), VMEM(tall, F32), VMEM(tall, F32), VMEM((nblk, BLK, width), BF16), VMEM((half, hb, width), BF16),
                         VMEM((half, hb, width), BF16), VMEM((per, BLK, width), BF16), VMEM((per, BLK, width), BF16),
                         VMEM((3 * rank, width), F32), VMEM((3, 3 * rank, pad), F32), VMEM((pad, width), BF16)]

time: 229 us -> 220 us (0.961)
  Pallas kernels: 226 us -> 217 us
    pallas_call x1, Pallas kernels: 95 us -> 87.1 us  [local(): pl.pallas_call(functools.partial(back_kernel, ndp), out_shape=[shape(tok,...]
where the time goes in v6:
time: 220 us
  Pallas kernels  217 us (99%)
    pallas_call x1, Pallas kernels, local(): pl.pallas_call(functools.partial(forward_kernel, ndp, chunks), out_shape=...  91.8 us
    pallas_call x1, Pallas kernels, local(): pl.pallas_call(functools.partial(back_kernel, ndp), out_shape=[shape(tok,...  87.1 us
    pallas_call x1, Pallas kernels, local(): pl.pallas_call(mid_kernel, out_shape=[shape(tok, width), shape(tok, width...  32.3 us
    pallas_call x1, Pallas kernels, local(): pl.pallas_call(place_kernel, out_shape=[shape(4, count, rank, width, dtyp...  5.7 us

profile of v6, /device:TPU:0, one launch (start us, length us, event | category | flops | bytes accessed | tf_op | source)
XLA Modules:
  0.0 219.7 jit_solution(13385394329220643598)
XLA Ops:
  1.3 91.8 %forward.1 = (bf16[8,4,15,80,128]{4,3,2,1,0:T(8,128)(2,1)}, f32[8,8,128]{2,1,0:T(8,128)}, bf16[4,2,5,128,128]{4,3,2,1,0:T(8,128)(2,1)}, bf16[2048,1280]{1,0:T(8,...) custom-call(s32[1]{0:T(128)S(6)} %copy.25.choice_in.e_ref, ...), custom_call_target="tpu_custom_call" | custom-call | tf_op jit(solution)/shard_map/forward/pallas_call | solution.py:1007
  93.1 32.3 %middle.1 = (bf16[512,1280]{1,0:T(8,128)(2,1)}, f32[512,1280]{1,0:T(8,128)}, bf16[4,2,5,128,128]{4,3,2,1,0:T(8,128)(2,1)}, f32[6,16,1280]{2,1,0:T(8,128)}) custom-call(s32[1]{0:T(128)S(6)} %copy.25.choice_in.e_ref, bf16[512,1280]{1,0:T(8,128)(2,1)} %x_h.1, bf16[512,1280]{1,0:T(8,128)(2,1)} %g_ref.1, bf16[4,2,5,128,128]{4,3,2,1,0:T(8,128)(2,1)} %get-tuple-element.36.mix4_ref, ...), custom_call_target="tpu_custom_call" | custom-call | tf_op jit(solution)/shard_map/middle/pallas_call | solution.py:1029
  125.4 87.1 %back.1 = (f32[512,1280]{1,0:T(8,128)}, bf16[2,8,48,1280]{3,2,1,0:T(8,128)(2,1)}, bf16[2,8,48,1280]{3,2,1,0:T(8,128)(2,1)}) custom-call(bf16[4,2,5,128,128]{4,3,2,1,0:T(8,128)(2,1)} %get-tuple-element.39.dmix_ref, bf16[320,2048]{1,0:T(8,128)(2,1)} %get-tuple-element.40.mixt_h, bf16[4,2048,128]{2,1,0:T(8,128)(2,1)} %get-tuple-element.41.q_h, ...), custom_call_target="tpu_custom_call" | custom-call | tf_op jit(solution)/shard_map/back/pallas_call | solution.py:1043
  212.5 0.0 copy-start
  212.5 5.7 %place.1 = (f32[4,8,16,1280]{3,2,1,0:T(8,128)}, f32[3,8,16,1280]{3,2,1,0:T(8,128)}, f32[8,16,1280]{2,1,0:T(8,128)}, f32[8,16,1280]{2,1,0:T(8,128)}, f32[8,16,1280]{2,1,0:T(8,128)}, /*index=5*/f32[2,8,16,1280]{3,2,1,0:T(8,128)}) custom-call(f32[8,8,128]{2,1,0:T(8,128)} %get-tuple-element.55.e_ref, bf16[2,8,48,1280]{3,2,1,0:T(8,128)(2,1)} %get-tuple-element.56.gm_ref, ...), custom_call_target="tpu_custom_call" | custom-call | tf_op jit(solution)/shard_map/place/pallas_call | solution.py:1059
  218.2 0.0 copy-done
  218.2 1.5 copy.26
Async XLA Ops:
  212.5 5.7 %copy-start = (f32[512,1280]{1,0:T(8,128)S(1)}, f32[512,1280]{1,0:T(8,128)}, u32[]{:S(2)}) copy-start(f32[512,1280]{1,0:T(8,128)} %get-tuple-element.73) | copy-start | bytes 7864324

commit v7 on v6

--- a/solution.py
+++ b/solution.py
@@ -716,7 +716,7 @@
 class GradSum:
     def __init__(self, me, gp, gr, g2, own, out, s, r, ls_, lr, fs, fr, keep):
         self.me, self.gp, self.gr, self.g2, self.own, self.out, self.s, self.r, self.fs, self.fr = me, gp, gr, g2, own, out, s, r, fs, fr
-        self.line = PairLine(me, own, out.at[me.c], ls_, lr)
+        self.lines = [PairLine(me, own.at[n], out.at[me.c], ls_, lr, n) for n in range(3)]
         self.keep = pltpu.make_async_copy(own, out.at[me.c, me.d], keep)
 
     def one(self):
@@ -730,30 +730,39 @@
         self.g2[...] = (self.gp[self.me.c].astype(F32) + self.gr[0].astype(F32)).astype(BF16)
         self.two().start()
 
-    def relay(self, o, own=False):
-        src = self.own if own else self.out.at[self.me.c, o]
-        return remote(src, self.out.at[self.me.c, o], self.fs.at[o], self.fr.at[o], self.me.d, self.me.t1)
+    def relay(self, o, n, own=False):
+        src = self.own.at[n] if own else self.out.at[self.me.c, o, n]
+        return remote(src, self.out.at[self.me.c, o, n], self.fs.at[o, n], self.fr.at[o, n], self.me.d, self.me.t1)
 
     def gather(self):
         self.two().wait_recv()
-        self.own[...] = (self.g2[...].astype(F32) + self.gr[1].astype(F32)).astype(BF16)
-        self.line.start()
-        self.relay(self.me.d, True).start()
+        total = (self.g2[...].astype(F32) + self.gr[1].astype(F32)).astype(BF16)
+        size = self.own.shape[1]
+        for n in range(3):
+            self.own[n] = total[n * size:(n + 1) * size]
+        for n in range(3):
+            self.lines[n].start()
+        for n in range(3):
+            self.relay(self.me.d, n, True).start()
         self.keep.start()
 
     def hop(self, k):
-        self.line.hop(k, lambda o: self.relay(o).start())
+        for n in range(3):
+            self.lines[n].hop(k, lambda o: self.relay(o, n).start())
 
     def arrivals(self):
-        self.line.pair_arrivals(lambda o: self.relay(o).start())
+        for n in range(3):
+            self.lines[n].pair_arrivals(lambda o: self.relay(o, n).start())
 
     def settle(self, ndp):
         def one(o, c):
-            self.relay(o, True).wait_send()
-            remote(self.own, self.out.at[1 - self.me.c, o], self.fs.at[o], self.fr.at[o], self.me.d, self.me.t1).wait_recv()
+            for n in range(3):
+                self.relay(o, n, True).wait_send()
+                remote(self.own.at[n], self.out.at[1 - self.me.c, o, n], self.fs.at[o, n], self.fr.at[o, n], self.me.d, self.me.t1).wait_recv()
             return c
         lax.fori_loop(0, ndp, one, 0)
-        self.line.sent()
+        for line in self.lines:
+            line.sent()
         self.keep.wait()
         self.one().wait_send()
         self.two().wait_send()
@@ -805,14 +814,13 @@
     def block(a):
         return (1 - me.y) * (nblk - 1 - a) + me.y * a
 
-    def pairs(a):
+    def others(a, first, last):
         b = block(a)
-        bwd_pair(b, b, True, *args)
 
         def other(n, c):
             bwd_pair(b + me.y * (1 + n), b - (1 - me.y) * (1 + n), False, *args)
             return c
-        lax.fori_loop(0, nblk - 1 - a, other, 0)
+        lax.fori_loop(first, last, other, 0)
 
     def arrived(t):
         remote(dmix_ref.at[t], dm_ref.at[t], dsem.at[0], drecv.at[t], me.d, t).wait_recv()
@@ -822,7 +830,7 @@
     arrived(me.t1)
     prep(me.t1)
     gm.second()
-    lax.fori_loop(half, nblk, lambda a, c: (pairs(a), c)[1], 0)
+    lax.fori_loop(half, nblk, lambda a, c: (bwd_pair(block(a), block(a), True, *args), others(a, 0, nblk - 1 - a), c)[2], 0)
     arrived(me.t2)
     prep(me.t2)
     arrived(me.t3)
@@ -853,7 +861,7 @@
         s2_ref[a] = (dn_ref[a, mine_rows(), :].astype(F32) + r1_ref[a].astype(F32)).astype(BF16)
         deliver(a).start()
 
-    def final(a):
+    def gradients(a):
         rows = pl.ds(pl.multiple_of(block(a) * BLK, BLK), BLK)
         dq, dk, dv = [], [], []
         for h in range(heads):
@@ -862,23 +870,31 @@
             dk.append(jnp.where(lane < HD, dk_ref[h, rows, :], 0.0).astype(BF16))
             dv.append(jnp.where(lane < HD, dv_ref[h, rows, :], 0.0).astype(BF16))
         ds = [jnp.concatenate(g, axis=1) for g in (dq, dk, dv)]
-        dz = sum(dot_nt(ds[s], bp_ref[s]) for s in range(3)).astype(BF16)
-        dn = sum(dot_nt(ds[s], wp_ref[s]) for s in range(3)) + dot(dz, at_ref[...])
-        dn_ref[a] = dn.astype(BF16)
+        return rows, ds, sum(dot_nt(ds[s], bp_ref[s]) for s in range(3)).astype(BF16)
+
+    def adapters(rows, ds, dz):
         ga_ref[...] += dot_tn(dz, xn_ref[rows, :])
         for s in range(3):
             gb_ref[s] += dot_tn(rank_ref[rows, :], ds[s])
 
+    def normed_gradient(a, ds, dz):
+        dn = sum(dot_nt(ds[s], wp_ref[s]) for s in range(3)) + dot(dz, at_ref[...])
+        dn_ref[a] = dn.astype(BF16)
+
     def upto(a):
         return 1 + jnp.minimum(a * (me.line - 1) // (nblk - 2), me.line - 1)
 
     def far_step(a, c):
-        pairs(a)
+        bwd_pair(block(a), block(a), True, *args)
+        others(a, 0, 2)
         @pl.when(a > 0)
         def _():
             pass_on(a - 1)
-        final(a)
+        others(a, 2, nblk - 1 - a)
+        rows, ds, dz = gradients(a)
+        normed_gradient(a, ds, dz)
         exchange(a).start()
+        adapters(rows, ds, dz)
         @pl.when(a == 0)
         def _():
             gm.gather()
@@ -886,24 +902,31 @@
         return c
     lax.fori_loop(0, half, far_step, 0)
 
-    def near_step(a, c):
-        final(a)
-        @pl.when(a == half)
-        def _():
-            pass_on(a - 1)
-        @pl.when(jnp.logical_not(is_mine(a)))
-        def _():
-            own_block(a).start()
-        lax.fori_loop(upto(a), upto(a + 1), lambda k, n: (gm.hop(k), n)[1], 0)
+    def near_adapters(a, c):
+        adapters(*gradients(a))
         return c
-    lax.fori_loop(half, nblk, near_step, 0)
+    lax.fori_loop(half, nblk, near_adapters, 0)
     n16 = n48 // 3
     gpa[0] = ga_ref[...].astype(BF16)
     gb = jnp.concatenate([gb_ref[s, s * n16:(s + 1) * n16] for s in range(3)], axis=0)
     gpa[1] = dot((0.5 * gb).astype(BF16), put_ref[...]).astype(BF16)
     ga.one().start()
+
+    def near_step(a, c):
+        _, ds, dz = gradients(a)
+        normed_gradient(a, ds, dz)
+        @pl.when(jnp.logical_not(is_mine(a)))
+        def _():
+            own_block(a).start()
+        @pl.when(a == half)
+        def _():
+            ga.second()
+            pass_on(a - 1)
+        lax.fori_loop(upto(a), upto(a + 1), lambda k, n: (gm.hop(k), n)[1], 0)
+        return c
+    lax.fori_loop(half, nblk, near_step, 0)
     gm.arrivals()
-    ga.second()
+    ga.gather()
 
     def combine(i, c):
         b = me.t * per + i
@@ -918,11 +941,10 @@
         gd = gain_ref[0:1, :] * dn
         dmid_ref[rows, :] = dmid_ref[rows, :] + r * gd - x * (r * r * r * jnp.mean(x * gd, axis=-1, keepdims=True))
         return c
-    ga.gather()
+    lax.fori_loop(1, me.line, lambda k, c: (ga.hop(k), c)[1], 0)
     lax.fori_loop(0, per, combine, 0)
     put_ig = pltpu.make_async_copy(dmid_ref, ig_h, igs.at[0])
     put_ig.start()
-    lax.fori_loop(1, me.line, lambda k, c: (ga.hop(k), c)[1], 0)
     ga.arrivals()
     ga.settle(ndp)
     gm.settle(ndp)
@@ -955,7 +977,7 @@
 
         def add(d, carry):
             e = e_ref[d, 0, 0].astype(jnp.int32)
-            out_ref[n, e] += src[c, d, k * 16:(k + 1) * 16, :].astype(F32)
+            out_ref[n, e] += src[c, d, k].astype(F32)
             return carry
         lax.fori_loop(0, ndp, add, 0)
         copies.append(pltpu.make_async_copy(out_ref.at[n], dst, sem.at[n]))
@@ -1038,11 +1060,11 @@
     gr = 6 * rank
     half_rows = gr // 2
     half, hb, per = nblk // 2, BLK // 2, tok // BLK
-    grad_bufs = [VMEM((2, half_rows, width), BF16), VMEM((2, half_rows, width), BF16), VMEM((half_rows, width), BF16), VMEM((half_rows, width), BF16)]
-    grad_sems = [DMA((2,)), DMA((2,)), DMA((3, ndp)), DMA((ndp,)), DMA((ndp,)), DMA((ndp,)), DMA((1,))]
+    grad_bufs = [VMEM((2, half_rows, width), BF16), VMEM((2, half_rows, width), BF16), VMEM((half_rows, width), BF16), VMEM((3, rank, width), BF16)]
+    grad_sems = [DMA((2,)), DMA((2,)), DMA((3, ndp, 3)), DMA((ndp, 3)), DMA((ndp, 3)), DMA((ndp, 3)), DMA((1,))]
     input_grad, grads_mid, grads_attn = pl.pallas_call(
         functools.partial(back_kernel, ndp),
-        out_shape=[shape(tok, width, dtype=F32), shape(2, ndp, half_rows, width), shape(2, ndp, half_rows, width)],
+        out_shape=[shape(tok, width, dtype=F32), shape(2, ndp, 3, rank, width), shape(2, ndp, 3, rank, width)],
         in_specs=[IN_ANY] * 12 + [IN_VMEM] * 5, out_specs=[IN_ANY] * 3,
         scratch_shapes=[VMEM((hcols, tree), BF16), VMEM(tall, BF16), VMEM((heads, 128, tree), BF16), VMEM(tall, BF16), VMEM((heads, HD, tree), BF16),
                         VMEM(tall, BF16), VMEM((3, width, pad), BF16), VMEM((tree, width), BF16), VMEM((tree, 3 * rank), BF16),

time: 220 us -> 216 us (0.982)
  Pallas kernels: 217 us -> 213 us
    pallas_call x1, Pallas kernels: 87.1 us -> 83.5 us  [local(): pl.pallas_call(functools.partial(back_kernel, ndp), out_shape=[shape(tok,...]
where the time goes in v7:
time: 216 us
  Pallas kernels  213 us (99%)
    pallas_call x1, Pallas kernels, local(): pl.pallas_call(functools.partial(forward_kernel, ndp, chunks), out_shape=...  91.8 us
    pallas_call x1, Pallas kernels, local(): pl.pallas_call(functools.partial(back_kernel, ndp), out_shape=[shape(tok,...  83.5 us
    pallas_call x1, Pallas kernels, local(): pl.pallas_call(mid_kernel, out_shape=[shape(tok, width), shape(tok, width...  32.2 us
    pallas_call x1, Pallas kernels, local(): pl.pallas_call(place_kernel, out_shape=[shape(4, count, rank, width, dtyp...  5.7 us

profile of v7, /device:TPU:0, one launch (start us, length us, event | category | flops | bytes accessed | tf_op | source)
XLA Modules:
  0.0 216.1 jit_solution(17974028632399359774)
XLA Ops:
  1.3 91.8 %forward.1 = (bf16[8,4,15,80,128]{4,3,2,1,0:T(8,128)(2,1)}, f32[8,8,128]{2,1,0:T(8,128)}, bf16[4,2,5,128,128]{4,3,2,1,0:T(8,128)(2,1)}, bf16[2048,1280]{1,0:T(8,...) custom-call(s32[1]{0:T(128)S(6)} %copy.25.choice_in.e_ref, ...), custom_call_target="tpu_custom_call" | custom-call | tf_op jit(solution)/shard_map/forward/pallas_call | solution.py:1029
  93.1 32.2 %middle.1 = (bf16[512,1280]{1,0:T(8,128)(2,1)}, f32[512,1280]{1,0:T(8,128)}, bf16[4,2,5,128,128]{4,3,2,1,0:T(8,128)(2,1)}, f32[6,16,1280]{2,1,0:T(8,128)}) custom-call(s32[1]{0:T(128)S(6)} %copy.25.choice_in.e_ref, bf16[512,1280]{1,0:T(8,128)(2,1)} %x_h.1, bf16[512,1280]{1,0:T(8,128)(2,1)} %g_ref.1, bf16[4,2,5,128,128]{4,3,2,1,0:T(8,128)(2,1)} %get-tuple-element.36.mix4_ref, ...), custom_call_target="tpu_custom_call" | custom-call | tf_op jit(solution)/shard_map/middle/pallas_call | solution.py:1051
  125.4 83.5 %back.1 = (f32[512,1280]{1,0:T(8,128)}, bf16[2,8,3,16,1280]{4,3,2,1,0:T(8,128)(2,1)}, bf16[2,8,3,16,1280]{4,3,2,1,0:T(8,128)(2,1)}) custom-call(bf16[4,2,5,128,128]{4,3,2,1,0:T(8,128)(2,1)} %get-tuple-element.39.dmix_ref, bf16[320,2048]{1,0:T(8,128)(2,1)} %get-tuple-element.40.mixt_h, bf16[4,2048,128]{2,1,0:T(8,128)(2,1)} %get-tuple-element.41.q_h, ...), custom_call_target="tpu_custom_call" | custom-call | tf_op jit(solution)/shard_map/back/pallas_call | solution.py:1065
  208.9 0.0 copy-start
  208.9 5.7 %place.1 = (f32[4,8,16,1280]{3,2,1,0:T(8,128)}, f32[3,8,16,1280]{3,2,1,0:T(8,128)}, f32[8,16,1280]{2,1,0:T(8,128)}, f32[8,16,1280]{2,1,0:T(8,128)}, f32[8,16,1280]{2,1,0:T(8,128)}, /*index=5*/f32[2,8,16,1280]{3,2,1,0:T(8,128)}) custom-call(f32[8,8,128]{2,1,0:T(8,128)} %get-tuple-element.55.e_ref, bf16[2,8,3,16,1280]{4,3,2,1,0:T(8,128)(2,1)} %get-tuple-element.56.gm_ref, ...), custom_call_target="tpu_custom_call" | custom-call | tf_op jit(solution)/shard_map/place/pallas_call | solution.py:1081
  214.6 0.0 copy-done
  214.6 1.5 copy.26
Async XLA Ops:
  208.9 5.7 %copy-start = (f32[512,1280]{1,0:T(8,128)S(1)}, f32[512,1280]{1,0:T(8,128)}, u32[]{:S(2)}) copy-start(f32[512,1280]{1,0:T(8,128)} %get-tuple-element.73) | copy-start | bytes 7864324

commit v8 on v7

--- a/solution.py
+++ b/solution.py
@@ -966,11 +966,13 @@
     put_ig.wait()
 
 
-def place_kernel(e_ref, gm_ref, ga_ref, ain_h, bqkv_h, bup_h, aout_h, adown_h, bres_h, out_ref, sem):
+def place_kernel(e_ref, gm_ref, ga_ref, ig_in, ain_h, bqkv_h, bup_h, aout_h, adown_h, bres_h, ig_out, out_ref, ig_ref, sem):
     ndp = gm_ref.shape[1]
     slots = ([(ga_ref, 0, n, ain_h.at[n]) for n in range(3)] + [(ga_ref, 1, n, bqkv_h.at[n]) for n in range(3)]
              + [(gm_ref, 0, 0, ain_h.at[3]), (gm_ref, 0, 1, bup_h), (gm_ref, 0, 2, aout_h),
                 (gm_ref, 1, 0, adown_h), (gm_ref, 1, 1, bres_h.at[0]), (gm_ref, 1, 2, bres_h.at[1])])
+    fetch = pltpu.make_async_copy(ig_in, ig_ref, sem.at[len(slots)])
+    fetch.start()
     copies = []
     for n, (src, c, k, dst) in enumerate(slots):
         out_ref[n] = jnp.zeros(out_ref.shape[1:], F32)
@@ -982,7 +984,11 @@
         lax.fori_loop(0, ndp, add, 0)
         copies.append(pltpu.make_async_copy(out_ref.at[n], dst, sem.at[n]))
         copies[-1].start()
-    for copy in copies:
+        if n == 3:
+            fetch.wait()
+            keep = pltpu.make_async_copy(ig_ref, ig_out, sem.at[len(slots) + 1])
+            keep.start()
+    for copy in copies + [keep]:
         copy.wait()
 
 
@@ -1078,13 +1084,13 @@
     )(d_mix, mixt, q, qt, k, kt, v, wp, xn, ranks, inputs, d_mid, scale, bp, at_qkv, norm_gain_rows, g_mid.reshape(gr, width))
 
     table = shape(count, rank, width, dtype=F32)
-    ga_in, gb_qkv, gb_up, ga_out, ga_down, gb_res = pl.pallas_call(
+    ga_in, gb_qkv, gb_up, ga_out, ga_down, gb_res, input_grad = pl.pallas_call(
         place_kernel,
         out_shape=[shape(4, count, rank, width, dtype=F32), shape(3, count, rank, width, dtype=F32), table, table, table,
-                   shape(2, count, rank, width, dtype=F32)],
-        in_specs=[IN_SMEM] + [IN_VMEM] * 2, out_specs=[IN_ANY] * 6,
-        scratch_shapes=[VMEM((12, count, rank, width), F32), DMA((12,))], compiler_params=params(), name="place",
-    )(choices, grads_mid, grads_attn)
+                   shape(2, count, rank, width, dtype=F32), shape(tok, width, dtype=F32)],
+        in_specs=[IN_SMEM] + [IN_VMEM] * 2 + [IN_ANY], out_specs=[IN_ANY] * 7,
+        scratch_shapes=[VMEM((12, count, rank, width), F32), VMEM((tok, width), F32), DMA((14,))], compiler_params=params(), name="place",
+    )(choices, grads_mid, grads_attn, input_grad)
     return (output, input_grad, jnp.swapaxes(ga_in, 2, 3), gb_qkv, gb_up, jnp.swapaxes(ga_out, 1, 2), jnp.swapaxes(ga_down, 1, 2), gb_res)
 
 

time: 216 us -> 217 us (level)
  Pallas kernels: 213 us -> 216 us
    pallas_call x1, Pallas kernels: 5.7 us -> 8.09 us  [local(): pl.pallas_call(place_kernel, out_shape=[shape(4, count, rank, width, dtyp...]
where the time goes in v8:
time: 217 us
  Pallas kernels  216 us (100%)
    pallas_call x1, Pallas kernels, local(): pl.pallas_call(functools.partial(forward_kernel, ndp, chunks), out_shape=...  91.8 us
    pallas_call x1, Pallas kernels, local(): pl.pallas_call(functools.partial(back_kernel, ndp), out_shape=[shape(tok,...  83.5 us
    pallas_call x1, Pallas kernels, local(): pl.pallas_call(mid_kernel, out_shape=[shape(tok, width), shape(tok, width...  32.3 us
    pallas_call x1, Pallas kernels, local(): pl.pallas_call(place_kernel, out_shape=[shape(4, count, rank, width, dtyp...  8.09 us

profile of v8, /device:TPU:0, one launch (start us, length us, event | category | flops | bytes accessed | tf_op | source)
XLA Modules:
  0.0 217.2 jit_solution(2296429533884684372)
XLA Ops:
  1.3 91.8 %forward.1 = (bf16[8,4,15,80,128]{4,3,2,1,0:T(8,128)(2,1)}, f32[8,8,128]{2,1,0:T(8,128)}, bf16[4,2,5,128,128]{4,3,2,1,0:T(8,128)(2,1)}, bf16[2048,1280]{1,0:T(8,...) custom-call(s32[1]{0:T(128)S(6)} %copy.24.choice_in.e_ref, ...), custom_call_target="tpu_custom_call" | custom-call | tf_op jit(solution)/shard_map/forward/pallas_call | solution.py:1035
  93.1 32.3 %middle.1 = (bf16[512,1280]{1,0:T(8,128)(2,1)}, f32[512,1280]{1,0:T(8,128)}, bf16[4,2,5,128,128]{4,3,2,1,0:T(8,128)(2,1)}, f32[6,16,1280]{2,1,0:T(8,128)}) custom-call(s32[1]{0:T(128)S(6)} %copy.24.choice_in.e_ref, bf16[512,1280]{1,0:T(8,128)(2,1)} %x_h.1, bf16[512,1280]{1,0:T(8,128)(2,1)} %g_ref.1, bf16[4,2,5,128,128]{4,3,2,1,0:T(8,128)(2,1)} %get-tuple-element.37.mix4_ref, ...), custom_call_target="tpu_custom_call" | custom-call | tf_op jit(solution)/shard_map/middle/pallas_call | solution.py:1057
  125.4 83.5 %back.1 = (f32[512,1280]{1,0:T(8,128)}, bf16[2,8,3,16,1280]{4,3,2,1,0:T(8,128)(2,1)}, bf16[2,8,3,16,1280]{4,3,2,1,0:T(8,128)(2,1)}) custom-call(bf16[4,2,5,128,128]{4,3,2,1,0:T(8,128)(2,1)} %get-tuple-element.41.dmix_ref, bf16[320,2048]{1,0:T(8,128)(2,1)} %get-tuple-element.42.mixt_h, bf16[4,2048,128]{2,1,0:T(8,128)(2,1)} %get-tuple-element.43.q_h, ...), custom_call_target="tpu_custom_call" | custom-call | tf_op jit(solution)/shard_map/back/pallas_call | solution.py:1071
  209.0 8.1 %place.1 = (f32[4,8,16,1280]{3,2,1,0:T(8,128)}, f32[3,8,16,1280]{3,2,1,0:T(8,128)}, f32[8,16,1280]{2,1,0:T(8,128)}, f32[8,16,1280]{2,1,0:T(8,128)}, f32[8,16,128...) custom-call(f32[8,8,128]{2,1,0:T(8,128)} %get-tuple-element.40.e_ref, ...), custom_call_target="tpu_custom_call" | custom-call | tf_op jit(solution)/shard_map/place/pallas_call | solution.py:1087
